TPU v7x, 256 devices: a whole 4x4x8 slice. The times are simulated.
256 devices in a mesh: group: 4 (over y), rank: 64 (over z, x, core).
Axes of the slice: x: 4, y: 4, z: 8, core: 2. Of those that a mesh axis runs over, the one named last changes fastest.
Arguments:
- queries: bfloat16 [65536, 2048], P(('group', 'rank')), may hold values from -32 to 32
- key_rows: bfloat16 [65536, 2048], P(('group', 'rank')), may hold values from -6 to 6
- value_rows: bfloat16 [65536, 2048], P(('group', 'rank')), may hold values from -6 to 6
- tile_links: int32 [512, 8], P(('group', 'rank')), may hold values from 0 to 15, as said below
- link_counts: int32 [512], P(('group', 'rank')), may hold values from 1 to 8, 2048 in all
Outputs:
- attended: bfloat16 [65536, 2048], P(('group', 'rank'))
Inputs may be any that keep to these rules, and one draw needn't show every extreme that they name: `tile_links`: each row names 8 different candidates.
All inputs are finite; a program needn't handle non-finite values. No bound on the sum of `link_counts` on one device may be relied on, other than what follows from the above.
Results may differ from a plain program's by a relative error of at most 0.0045.
Values may be sent and summed in bfloat16 or wider, within the bound.
No kernel may reach another device: no remote copies, remote signals or barrier semaphores. Data moves between devices by JAX's collectives and lax.ppermute only.
A program may use at most 128 MiB of HBM per device.

v0:
```python
import jax
import jax.numpy as jnp
from jax import lax
from jax.sharding import PartitionSpec as P

H = 16
HD = 128
LMAX = 8


def passed_along(block, axis, distance):
    devices = range(lax.axis_size(axis))
    route = [((i - distance) % len(devices), i) for i in devices]
    return lax.ppermute(block, axis, route)


def side_by_side(arrays, axis, dim, along):
    both = jnp.concatenate(arrays, axis=along)
    result, at, done = (lax.all_gather(both, axis, axis=dim, tiled=True), 0, [])
    for a in arrays:
        done.append(lax.slice_in_dim(result, at, at + a.shape[along], axis=along))
        at += a.shape[along]
    return tuple(done)


def shards(queries, key_rows, value_rows, tile_links, link_counts):
    rows_dev, row_width = queries.shape
    tiles_dev = tile_links.shape[0]
    tile_rows = rows_dev // tiles_dev
    groups = lax.axis_size("group")
    chains = []
    for step_by in (1, -1):
        current = (key_rows, value_rows)
        reached = []
        for repeat_index in range(2):
            current = passed_along((current[0], current[1]), "rank", step_by)
            reached.append(current)
        chains.append(reached)
    near_tiles = [chains[0][1], chains[0][0], chains[1][0], chains[1][1]]
    gathered = side_by_side((key_rows, value_rows), "group", 0, 1)
    group_id = lax.axis_index("group")
    sources = [(key_rows, value_rows)] + list(near_tiles)
    for peer_step in range(1, groups):
        start = (group_id + peer_step) % groups * rows_dev
        sources.append(
            (
                lax.dynamic_slice_in_dim(gathered[0], start, rows_dev, 0),
                lax.dynamic_slice_in_dim(gathered[1], start, rows_dev, 0),
            )
        )
    cand_total = len(sources) * tiles_dev
    cand_ids = jnp.arange(cand_total, dtype=jnp.int32)
    listed = (tile_links[:, :, None] == cand_ids[None, None, :]) & (
        jnp.arange(LMAX, dtype=jnp.int32)[None, :, None] < link_counts[:, None, None]
    )
    own_slot = jnp.arange(tiles_dev, dtype=jnp.int32)[:, None] == cand_ids[None, :]
    multiplicity = jnp.sum(listed.astype(jnp.float32), axis=1) + own_slot.astype(jnp.float32)
    query_heads = queries.reshape(rows_dev, H, HD)
    blocks = []
    row_max = None
    for source_index, (source_keys, source_values) in enumerate(sources):
        scores = jnp.einsum(
            "qhd,khd->hqk",
            query_heads,
            source_keys.reshape(rows_dev, H, HD),
            preferred_element_type=jnp.float32,
        ) * HD ** (-0.5)
        scores = scores.reshape(H, tiles_dev, tile_rows, tiles_dev, tile_rows)
        counted = multiplicity[:, source_index * tiles_dev : (source_index + 1) * tiles_dev]
        scores = jnp.where(counted[None, :, None, :, None] > 0, scores, -jnp.inf)
        block_max = jnp.max(scores, axis=(3, 4), keepdims=True)
        row_max = block_max if row_max is None else jnp.maximum(row_max, block_max)
        blocks.append((scores, counted, source_values))
    row_total = jnp.zeros((H, tiles_dev, tile_rows), jnp.float32)
    mixed_rows = jnp.zeros((rows_dev, H, HD), jnp.float32)
    for scores, counted, source_values in blocks:
        weights = jnp.exp(scores - row_max)
        factor = counted[None, :, None, :, None]
        row_total = row_total + jnp.sum(weights * factor, axis=(3, 4))
        rounded = weights.astype(jnp.bfloat16) * factor.astype(jnp.bfloat16)
        mixed_rows = mixed_rows + jnp.einsum(
            "hqk,khd->qhd",
            rounded.reshape(H, rows_dev, rows_dev),
            source_values.reshape(rows_dev, H, HD),
            preferred_element_type=jnp.float32,
        )
    totals = jnp.transpose(row_total.reshape(H, rows_dev))
    return (mixed_rows / totals[:, :, None]).reshape(rows_dev, row_width).astype(jnp.bfloat16)


def solution(mesh):
    return jax.shard_map(
        shards,
        mesh=mesh,
        in_specs=(
            P(("group", "rank"), None),
            P(("group", "rank"), None),
            P(("group", "rank"), None),
            P(("group", "rank"), None),
            P(("group", "rank")),
        ),
        out_specs=P(("group", "rank"), None),
        check_vma=False,
    )
```

profile of v0, /device:TPU:1, one launch (start us, length us, event | category | flops | bytes accessed | tf_op | source)
XLA Modules:
  0.0 160.2 jit_solution(3764443688378237039)
XLA Ops:
  6.5 1.6 copy.112
  8.1 1.5 copy.132
  9.6 1.5 pad_maximum_fusion
  11.1 3.3 %collective-permute-start.2 = (bf16[256,2048]{0,1:T(8,128)(2,1)S(1)}, bf16[256,2048]{0,1:T(8,128)(2,1)}, u32[]{:S(2)}, u32[]{:S(2)}) collective-permute-start(bf16[256,2048]{0,1:T(8,128)(2,1)S(1)} %copy.112), channel_id=1, source_target_pairs={{1,0},{2,1},{3,2},{4,3},{5,4},{6,5},{7,6},{8,7},{9,8},{10,9},{11,1... | collective-permute-start | bytes 3145736 | tf_op jit(solution)/shard_map/ppermute | solution.py:14
  14.4 5.8 %collective-permute-start.6 = (bf16[256,2048]{1,0:T(8,128)(2,1)}, bf16[256,2048]{1,0:T(8,128)(2,1)}, u32[]{:S(2)}, u32[]{:S(2)}) collective-permute-start(bf16[256,2048]{1,0:T(8,128)(2,1)} %param.7), channel_id=1, source_target_pairs={{1,0},{2,1},{3,2},{4,3},{5,4},{6,5},{7,6},{8,7},{9,8},{10,9},{11,1... | collective-permute-start | bytes 3145736 | tf_op jit(solution)/shard_map/ppermute | solution.py:14
  20.5 0.1 broadcast_in_dim.117
  20.6 0.2 copy.108
  21.4 0.8 copy_bitcast_fusion.3
  22.5 0.8 copy_bitcast_fusion.5
  23.6 0.8 copy_bitcast_fusion
  24.5 3.4 %fusion = (f32[16,256]{1,0:T(8,128)}, f32[16,256,256]{1,2,0:T(8,128)}) fusion(pred[256,256]{0,1:T(8,128)(4,1)S(1)} %copy.108, bf16[256,2048]{1,0:T(8,128)(2,1)S(1)} %copy-done.10, bf16[256,2048]{1,0:T(8,128)(2,1)S(1)} %copy-done), kind=kOutput, calls=%fused_computation.24 | convolution fusion | flops 271577088 | bytes 6373376 | tf_op jit(solution)/shard_map/qhd,khd->hqk/dot_general | solution.py:62
  27.8 5.1 %collective-permute-start.3 = (bf16[256,2048]{0,1:T(8,128)(2,1)}, bf16[256,2048]{0,1:T(8,128)(2,1)}, u32[]{:S(2)}, u32[]{:S(2)}) collective-permute-start(bf16[256,2048]{0,1:T(8,128)(2,1)} %collective-permute-done.2), channel_id=1, source_target_pairs={{1,0},{2,1},{3,2},{4,3},{5,4},{6,5},{7,6},{8,7},{9,8},{10,9},{11,1... | collective-permute-start | bytes 3145736 | tf_op jit(solution)/shard_map/ppermute | solution.py:14
  32.9 4.6 %collective-permute-done.4 = bf16[256,2048]{1,0:T(8,128)(2,1)} collective-permute-done((bf16[256,2048]{1,0:T(8,128)(2,1)}, bf16[256,2048]{1,0:T(8,128)(2,1)}, u32[]{:S(2)}, u32[]{:S(2)}) %collective-permute-start.4) | collective-permute-done | bytes 1048608 | tf_op jit(solution)/shard_map/ppermute | solution.py:14
  37.5 2.5 %collective-permute-start.5 = (bf16[256,2048]{1,0:T(8,128)(2,1)}, bf16[256,2048]{1,0:T(8,128)(2,1)}, u32[]{:S(2)}, u32[]{:S(2)}) collective-permute-start(bf16[256,2048]{1,0:T(8,128)(2,1)} %collective-permute-done.4), channel_id=1, source_target_pairs={{63,0},{0,1},{1,2},{2,3},{3,4},{4,5},{5,6},{6,7},{7,8},{8,9},{9,10... | collective-permute-start | bytes 3145736 | tf_op jit(solution)/shard_map/ppermute | solution.py:14
  40.0 9.1 %collective-permute-start.7 = (bf16[256,2048]{1,0:T(8,128)(2,1)}, bf16[256,2048]{1,0:T(8,128)(2,1)}, u32[]{:S(2)}, u32[]{:S(2)}) collective-permute-start(bf16[256,2048]{1,0:T(8,128)(2,1)} %collective-permute-done.6), channel_id=1, source_target_pairs={{1,0},{2,1},{3,2},{4,3},{5,4},{6,5},{7,6},{8,7},{9,8},{10,9},{11,1... | collective-permute-start | bytes 3145736 | tf_op jit(solution)/shard_map/ppermute | solution.py:14
  49.2 0.1 broadcast_in_dim.139
  49.3 0.2 copy.138
  49.5 0.1 broadcast_in_dim.136
  49.7 0.8 copy.135
  50.7 0.8 copy.130
  51.6 0.1 broadcast_in_dim.121
  51.8 0.1 broadcast_in_dim.127
  52.0 0.1 broadcast_in_dim.124
  52.6 0.7 copy.306
  53.4 0.7 copy.304
  54.2 0.7 copy.305
  55.0 0.1 mul.264
  55.1 0.7 copy.307
  55.9 0.1 mul.284
  56.0 0.7 copy.302
  56.8 0.1 mul.288
  56.9 0.7 copy.301
  57.7 0.1 mul.292
  57.8 0.7 copy.300
  58.7 0.7 copy.303
  59.6 0.9 copy_bitcast_fusion.2
  60.5 2.3 %copy.149 = bf16[256,2048]{0,1:T(8,128)(2,1)} copy(bf16[256,2048]{1,0:T(8,128)(2,1)} %collective-permute-done.6) | data formatting | bytes 2097152 | tf_op jit(solution)/shard_map/ppermute | solution.py:14
  62.7 2.3 %copy.147 = bf16[256,2048]{0,1:T(8,128)(2,1)} copy(bf16[256,2048]{1,0:T(8,128)(2,1)} %collective-permute-done.4) | data formatting | bytes 2097152 | tf_op jit(solution)/shard_map/ppermute | solution.py:14
  65.0 4.0 %fusion.3 = (f32[16,256]{1,0:T(8,128)S(1)}, f32[16,256,256]{2,1,0:T(8,128)}) fusion(pred[256,256]{1,0:T(8,128)(4,1)S(1)} %bitcast.304, bf16[256,16,128]{0,2,1:T(8,128)(2,1)} %bitcast.2, bf16[256,2048]{1,0:T(8,128)(2,1)S(1)} %copy-done), kind=kOutput, calls=%fused_computation.27 | convolution fusion | flops 271577088 | bytes 6373376 | tf_op jit(solution)/shard_map/qhd,khd->hqk/dot_general | solution.py:62
  69.1 3.9 %fusion.2 = (f32[16,256]{1,0:T(8,128)S(1)}, f32[16,256,256]{2,1,0:T(8,128)}) fusion(pred[256,256]{1,0:T(8,128)(4,1)S(1)} %bitcast.307, bf16[256,16,128]{0,2,1:T(8,128)(2,1)} %bitcast.1, bf16[256,2048]{1,0:T(8,128)(2,1)S(1)} %copy-done), kind=kOutput, calls=%fused_computation.26 | convolution fusion | flops 271577088 | bytes 6373376 | tf_op jit(solution)/shard_map/qhd,khd->hqk/dot_general | solution.py:62
  73.0 2.3 %copy.145 = bf16[256,2048]{0,1:T(8,128)(2,1)} copy(bf16[256,2048]{1,0:T(8,128)(2,1)} %collective-permute-done.5) | data formatting | bytes 2097152 | tf_op jit(solution)/shard_map/ppermute | solution.py:14
  75.3 2.3 %copy.151 = bf16[256,2048]{0,1:T(8,128)(2,1)} copy(bf16[256,2048]{1,0:T(8,128)(2,1)} %collective-permute-done.7) | data formatting | bytes 2097152 | tf_op jit(solution)/shard_map/ppermute | solution.py:14
  77.5 3.9 %fusion.4 = (f32[16,256]{1,0:T(8,128)S(1)}, f32[16,256,256]{2,1,0:T(8,128)}) fusion(pred[256,256]{1,0:T(8,128)(4,1)S(1)} %bitcast.298, bf16[256,16,128]{0,2,1:T(8,128)(2,1)} %bitcast.3, bf16[256,2048]{1,0:T(8,128)(2,1)S(1)} %copy-done), kind=kOutput, calls=%fused_computation.28 | convolution fusion | flops 271577088 | bytes 6373376 | tf_op jit(solution)/shard_map/qhd,khd->hqk/dot_general | solution.py:62
  81.5 3.3 %fusion.1 = (f32[16,256]{1,0:T(8,128)}, f32[16,256,256]{2,1,0:T(8,128)}) fusion(pred[256,256]{1,0:T(8,128)(4,1)S(1)} %bitcast.301, bf16[256,16,128]{0,2,1:T(8,128)(2,1)S(1)} %bitcast.286, bf16[256,2048]{1,0:T(8,128)(2,1)S(1)} %copy-done), kind=kOutput, calls=%fused_computation.25 | convolution fusion | flops 271577088 | bytes 6373376 | tf_op jit(solution)/shard_map/qhd,khd->hqk/dot_general | solution.py:62
  84.8 19.1 %all-gather.2.cloned.1.call-done = bf16[1024,4096]{0,1:T(8,128)(2,1)} async-done(((bf16[256,4096]{0,1:T(8,128)(2,1)}), bf16[1024,4096]{0,1:T(8,128)(2,1)}) %all-gather.2.cloned.1.call-update) | async-done | bytes 8388624 | tf_op jit(solution)/shard_map/all_gather | solution.py:19
  103.9 3.9 %fusion.128 = (bf16[1024,2048]{0,1:T(8,128)(2,1)S(1)}, bf16[1024,2048]{0,1:T(8,128)(2,1)S(1)}) fusion(bf16[1024,4096]{0,1:T(8,128)(2,1)} %all-gather.2.cloned.1.call-done), kind=kLoop, calls=%fused_computation.198 | loop fusion | bytes 16777216 | tf_op jit(solution)/shard_map/slice | solution.py:21
  107.8 1.8 %constant_dynamic-slice_fusion.2 = (bf16[256,2048]{0,1:T(8,128)(2,1)S(1)}, bf16[256,2048]{0,1:T(8,128)(2,1)}, bf16[256,2048]{0,1:T(8,128)(2,1)S(1)}, bf16[256,20...) fusion(bf16[1024,2048]{0,1:T(8,128)(2,1)S(1)} %get-tuple-element.14, ...), kind=kLoop, calls=%fused_computation.160 | loop fusion | bytes 12582924 | tf_op jit(solution)/shard_map/dynamic_slice | solution.py:48
  109.6 0.9 fusion.15
  110.6 0.9 fusion.14
  111.6 0.9 fusion.13
  112.6 1.1 copy-done.5
  113.8 0.3 copy-done.13
  114.1 2.7 %fusion.26 = f32[16,256,128]{1,2,0:T(8,128)} fusion(bf16[256,16,128]{0,2,1:T(8,128)(2,1)S(1)} %bitcast.289, f32[16,256,256]{2,1,0:T(8,128)S(1)} %copy-done.5, f32[16,256]{1,0:T(8,128)S(1)} %maximum_maximum_fusion, pred[256,256]{1,0:T(8,128)(4,1)S(1)} %bitcast.302, bf16[256,256]{1,0:T(8,128)(2,1)S(1)} %bitcast.331), kind=kOutput, calls=%fused_computation.47 | convolution fusion | flops 273678336 | bytes 7553024 | tf_op jit(solution)/shard_map/hqk,khd->qhd/dot_general | solution.py:81
  116.8 2.7 %fusion.20 = f32[16,256,128]{1,2,0:T(8,128)} fusion(bf16[256,16,128]{0,2,1:T(8,128)(2,1)S(1)} %bitcast.288, f32[16,256,256]{2,1,0:T(8,128)S(1)} %copy-done.3, f32[16,256]{1,0:T(8,128)S(1)} %maximum_maximum_fusion, pred[256,256]{1,0:T(8,128)(4,1)S(1)} %bitcast.305, bf16[256,256]{1,0:T(8,128)(2,1)S(1)} %bitcast.332), kind=kOutput, calls=%fused_computation.43 | convolution fusion | flops 273678336 | bytes 7553024 | tf_op jit(solution)/shard_map/hqk,khd->qhd/dot_general | solution.py:81
  119.5 0.4 copy-done.11
  120.0 2.7 %fusion.23 = f32[16,256,128]{1,2,0:T(8,128)} fusion(bf16[256,16,128]{0,2,1:T(8,128)(2,1)S(1)} %bitcast.287, f32[16,256,256]{2,1,0:T(8,128)S(1)} %copy-done.4, f32[16,256]{1,0:T(8,128)S(1)} %maximum_maximum_fusion, pred[256,256]{1,0:T(8,128)(4,1)S(1)} %bitcast.308, bf16[256,256]{1,0:T(8,128)(2,1)S(1)} %bitcast.333), kind=kOutput, calls=%fused_computation.45 | convolution fusion | flops 273678336 | bytes 7553024 | tf_op jit(solution)/shard_map/hqk,khd->qhd/dot_general | solution.py:81
  122.7 2.7 %fusion.29 = f32[16,256,128]{1,2,0:T(8,128)} fusion(bf16[256,16,128]{0,2,1:T(8,128)(2,1)S(1)} %bitcast.280, f32[16,256,256]{1,2,0:T(8,128)S(1)} %copy-done.6, f32[16,256]{1,0:T(8,128)S(1)} %maximum_maximum_fusion, pred[256,256]{0,1:T(8,128)(4,1)S(1)} %copy-done.29, bf16[256,256]{0,1:T(8,128)(2,1)S(1)} %bitcast.334), kind=kOutput, calls=%fused_computation.49 | convolution fusion | flops 276824064 | bytes 7553024 | tf_op jit(solution)/shard_map/hqk,khd->qhd/dot_general | solution.py:81
  125.4 2.7 %fusion.38 = f32[16,128,256]{2,1,0:T(8,128)} fusion(bf16[256,16,128]{0,2,1:T(8,128)(2,1)S(1)} %bitcast.285, f32[16,256,256]{2,1,0:T(8,128)S(1)} %get-tuple-element.50, f32[16,256]{1,0:T(8,128)S(1)} %maximum_maximum_fusion, pred[256,256]{0,1:T(8,128)(4,1)S(1)} %copy-done.26, bf16[256,256]{0,1:T(8,128)(2,1)S(1)} %bitcast.335), kind=kOutput, calls=%fused_computation.55 | convolution fusion | flops 273678336 | bytes 7553024 | tf_op jit(solution)/shard_map/hqk,khd->qhd/dot_general | solution.py:81
  128.1 2.6 %fusion.35 = f32[16,128,256]{2,1,0:T(8,128)} fusion(bf16[256,16,128]{0,2,1:T(8,128)(2,1)S(1)} %bitcast.284, f32[16,256,256]{2,1,0:T(8,128)S(1)} %get-tuple-element.48, f32[16,256]{1,0:T(8,128)S(1)} %maximum_maximum_fusion, pred[256,256]{0,1:T(8,128)(4,1)S(1)} %copy-done.25, bf16[256,256]{0,1:T(8,128)(2,1)S(1)} %bitcast.336), kind=kOutput, calls=%fused_computation.53 | convolution fusion | flops 273678336 | bytes 7553024 | tf_op jit(solution)/shard_map/hqk,khd->qhd/dot_general | solution.py:81
  130.7 2.7 %fusion.32 = f32[16,128,256]{2,1,0:T(8,128)} fusion(bf16[256,16,128]{0,2,1:T(8,128)(2,1)S(1)} %bitcast.283, f32[16,256,256]{2,1,0:T(8,128)S(1)} %get-tuple-element.46, f32[16,256]{1,0:T(8,128)S(1)} %maximum_maximum_fusion, pred[256,256]{0,1:T(8,128)(4,1)S(1)} %copy-done.24, bf16[256,256]{0,1:T(8,128)(2,1)S(1)} %bitcast.337), kind=kOutput, calls=%fused_computation.51 | convolution fusion | flops 273678336 | bytes 7553024 | tf_op jit(solution)/shard_map/hqk,khd->qhd/dot_general | solution.py:81
  133.4 6.0 %multiply_reduce_fusion.7 = (f32[16,256]{1,0:T(8,128)S(1)}, f32[16,256]{1,0:T(8,128)S(1)}, f32[16,256]{1,0:T(8,128)}, f32[16,256]{1,0:T(8,128)}) fusion(f32[16,256,256]{1,2,0:T(8,128)S(1)} %copy-done.7, f32[256,256]{0,1:T(8,128)} %get-tuple-element.67, f32[16,256]{1,0:T(8,128)S(1)} %maximum_maximum_fusion, pred[256,256]{0,1:T(8,128)(4,1)} %copy-done.28, ...), kind=kLoop, calls=%fused_computation.10 | loop fusion | flops 20955136 | bytes 18169856 | tf_op jit(solution)/shard_map/reduce_sum | solution.py:79
  139.5 5.9 %multiply_reduce_fusion.6 = (f32[16,256]{1,0:T(8,128)S(1)}, f32[16,256]{1,0:T(8,128)S(1)}, f32[16,256]{1,0:T(8,128)S(1)}, f32[16,256]{1,0:T(8,128)S(1)}) fusion(f32[16,256,256]{2,1,0:T(8,128)S(1)} %copy-done.5, f32[16,256]{1,0:T(8,128)S(1)} %maximum_maximum_fusion, f32[256,256]{1,0:T(8,128)S(1)} %copy-done.17, pred[256,256]{1,0:T(8,128)(4,1)} %bitcast.303, ...), kind=kLoop, calls=%fused_computation.9 | loop fusion | flops 20955136 | bytes 18169856 | tf_op jit(solution)/shard_map/reduce_sum | solution.py:79
  145.5 6.4 %fusion.50 = bf16[256,16,128]{0,2,1:T(8,128)(2,1)S(1)} fusion(f32[16,128,256]{2,1,0:T(8,128)} %fusion.32, f32[16,128,256]{2,1,0:T(8,128)} %fusion.35, f32[16,128,256]{2,1,0:T(8,128)} %fusion.38, f32[16,256,128]{1,2,0:T(8,128)} %fusion.20, f32[16,256,128]{1,2,0:T(8,128)} %fusion.23, f32[16,256,128]{1,2,0:T(8,128)} %fusion.29, f32[16,256,128]{1,2,0:T(8,128)} %fusion.26, ...), kind=kOutput, calls=%fused_computation.68 | convolution fusion | flops 278396928 | bytes 21200896 | tf_op jit(solution)/shard_map/hqk,khd->qhd/dot_general | solution.py:81
  152.0 1.4 copy.162
  (133 shorter events, 3.6 us)
Async XLA Ops:
  6.5 17.9 %copy-start = (bf16[256,2048]{1,0:T(8,128)(2,1)S(1)}, bf16[256,2048]{1,0:T(8,128)(2,1)}, u32[]{:S(2)}) copy-start(bf16[256,2048]{1,0:T(8,128)(2,1)} %param.5) | copy-start | bytes 3145732
  6.5 97.3 %all-gather.2.cloned.1.call-start = ((), (), s32[]{:S(2)}) async-start(), calls=%async_computation | async-start | bytes 10485760 | tf_op jit(solution)/shard_map/all_gather | solution.py:19
  8.1 12.1 %copy-start.42 = (s32[2]{0:T(128)S(1)}, s32[2]{0:T(128)}, u32[]{:S(2)}) copy-start(s32[2]{0:T(128)} %param.9) | copy-start | bytes 28
  8.1 12.2 %copy-start.41 = (s32[2,8]{1,0:T(2,128)S(1)}, s32[2,8]{1,0:T(2,128)}, u32[]{:S(2)}) copy-start(s32[2,8]{1,0:T(2,128)} %param.8) | copy-start | bytes 196
  11.1 16.7 %collective-permute-start.2 = (bf16[256,2048]{0,1:T(8,128)(2,1)S(1)}, bf16[256,2048]{0,1:T(8,128)(2,1)}, u32[]{:S(2)}, u32[]{:S(2)}) collective-permute-start(bf16[256,2048]{0,1:T(8,128)(2,1)S(1)} %copy.112), channel_id=1, source_target_pairs={{1,0},{2,1},{3,2},{4,3},{5,4},{6,5},{7,6},{8,7},{9,8},{10,9},{11,1... | collective-permute-start | bytes 3145736 | tf_op jit(solution)/shard_map/ppermute | solution.py:14
  14.4 50.6 %collective-permute-start = (bf16[256,2048]{0,1:T(8,128)(2,1)S(1)}, bf16[256,2048]{0,1:T(8,128)(2,1)}, u32[]{:S(2)}, u32[]{:S(2)}) collective-permute-start(bf16[256,2048]{0,1:T(8,128)(2,1)S(1)} %copy.112), channel_id=1, source_target_pairs={{63,0},{0,1},{1,2},{2,3},{3,4},{4,5},{5,6},{6,7},{7,8},{8,9},{9,10... | collective-permute-start | bytes 3145736 | tf_op jit(solution)/shard_map/ppermute | solution.py:14
  14.4 23.1 %collective-permute-start.4 = (bf16[256,2048]{1,0:T(8,128)(2,1)}, bf16[256,2048]{1,0:T(8,128)(2,1)}, u32[]{:S(2)}, u32[]{:S(2)}) collective-permute-start(bf16[256,2048]{1,0:T(8,128)(2,1)} %param.7), channel_id=1, source_target_pairs={{63,0},{0,1},{1,2},{2,3},{3,4},{4,5},{5,6},{6,7},{7,8},{8,9},{9,10... | collective-permute-start | bytes 3145736 | tf_op jit(solution)/shard_map/ppermute | solution.py:14
  14.4 25.6 %collective-permute-start.6 = (bf16[256,2048]{1,0:T(8,128)(2,1)}, bf16[256,2048]{1,0:T(8,128)(2,1)}, u32[]{:S(2)}, u32[]{:S(2)}) collective-permute-start(bf16[256,2048]{1,0:T(8,128)(2,1)} %param.7), channel_id=1, source_target_pairs={{1,0},{2,1},{3,2},{4,3},{5,4},{6,5},{7,6},{8,7},{9,8},{10,9},{11,1... | collective-permute-start | bytes 3145736 | tf_op jit(solution)/shard_map/ppermute | solution.py:14
  20.8 7.0 %copy-start.28 = (pred[256,256]{0,1:T(8,128)(4,1)}, pred[256,256]{0,1:T(8,128)(4,1)S(1)}, u32[]{:S(2)}) copy-start(pred[256,256]{0,1:T(8,128)(4,1)S(1)} %copy.108) | copy-start | bytes 196612
  21.1 3.4 %copy-start.10 = (bf16[256,2048]{1,0:T(8,128)(2,1)S(1)}, bf16[256,2048]{1,0:T(8,128)(2,1)}, u32[]{:S(2)}) copy-start(bf16[256,2048]{1,0:T(8,128)(2,1)} %param.6) | copy-start | bytes 3145732
  27.8 49.7 %collective-permute-start.3 = (bf16[256,2048]{0,1:T(8,128)(2,1)}, bf16[256,2048]{0,1:T(8,128)(2,1)}, u32[]{:S(2)}, u32[]{:S(2)}) collective-permute-start(bf16[256,2048]{0,1:T(8,128)(2,1)} %collective-permute-done.2), channel_id=1, source_target_pairs={{1,0},{2,1},{3,2},{4,3},{5,4},{6,5},{7,6},{8,7},{9,8},{10,9},{11,1... | collective-permute-start | bytes 3145736 | tf_op jit(solution)/shard_map/ppermute | solution.py:14
  37.5 35.5 %collective-permute-start.5 = (bf16[256,2048]{1,0:T(8,128)(2,1)}, bf16[256,2048]{1,0:T(8,128)(2,1)}, u32[]{:S(2)}, u32[]{:S(2)}) collective-permute-start(bf16[256,2048]{1,0:T(8,128)(2,1)} %collective-permute-done.4), channel_id=1, source_target_pairs={{63,0},{0,1},{1,2},{2,3},{3,4},{4,5},{5,6},{6,7},{7,8},{8,9},{9,10... | collective-permute-start | bytes 3145736 | tf_op jit(solution)/shard_map/ppermute | solution.py:14
  40.0 35.3 %collective-permute-start.7 = (bf16[256,2048]{1,0:T(8,128)(2,1)}, bf16[256,2048]{1,0:T(8,128)(2,1)}, u32[]{:S(2)}, u32[]{:S(2)}) collective-permute-start(bf16[256,2048]{1,0:T(8,128)(2,1)} %collective-permute-done.6), channel_id=1, source_target_pairs={{1,0},{2,1},{3,2},{4,3},{5,4},{6,5},{7,6},{8,7},{9,8},{10,9},{11,1... | collective-permute-start | bytes 3145736 | tf_op jit(solution)/shard_map/ppermute | solution.py:14
  49.5 60.1 %copy-start.23 = (pred[256,256]{0,1:T(8,128)(4,1)}, pred[256,256]{0,1:T(8,128)(4,1)S(1)}, u32[]{:S(2)}) copy-start(pred[256,256]{0,1:T(8,128)(4,1)S(1)} %copy.138) | copy-start | bytes 196612
  51.8 60.8 %copy-start.20 = (pred[32,8,2,128]{3,1,2,0:T(8,128)(4,1)}, pred[32,8,2,128]{3,1,2,0:T(8,128)(4,1)S(1)}, u32[]{:S(2)}) copy-start(pred[32,8,2,128]{3,1,2,0:T(8,128)(4,1)S(1)} %copy.298) | copy-start | bytes 196612
  52.0 64.7 %copy-start.21 = (pred[32,8,2,128]{3,1,2,0:T(8,128)(4,1)}, pred[32,8,2,128]{3,1,2,0:T(8,128)(4,1)S(1)}, u32[]{:S(2)}) copy-start(pred[32,8,2,128]{3,1,2,0:T(8,128)(4,1)S(1)} %copy.296) | copy-start | bytes 196612
  52.2 67.3 %copy-start.22 = (pred[32,8,2,128]{3,1,2,0:T(8,128)(4,1)}, pred[32,8,2,128]{3,1,2,0:T(8,128)(4,1)S(1)}, u32[]{:S(2)}) copy-start(pred[32,8,2,128]{3,1,2,0:T(8,128)(4,1)S(1)} %copy.297) | copy-start | bytes 196612
  65.0 16.4 %collective-permute-start.1 = (bf16[256,2048]{0,1:T(8,128)(2,1)}, bf16[256,2048]{0,1:T(8,128)(2,1)S(1)}, u32[]{:S(2)}, u32[]{:S(2)}) collective-permute-start(bf16[256,2048]{0,1:T(8,128)(2,1)} %collective-permute-done), channel_id=1, source_target_pairs={{63,0},{0,1},{1,2},{2,3},{3,4},{4,5},{5,6},{6,7},{7,8},{8,9},{9,10... | collective-permute-start | bytes 3145736 | tf_op jit(solution)/shard_map/ppermute | solution.py:14
  109.6 1.0 copy-start.25
  110.6 1.0 copy-start.26
  111.5 1.0 copy-start.37
  111.5 1.0 copy-start.40
  111.6 2.2 %copy-start.5 = (f32[16,256,256]{2,1,0:T(8,128)S(1)}, f32[16,256,256]{2,1,0:T(8,128)}, u32[]{:S(2)}) copy-start(f32[16,256,256]{2,1,0:T(8,128)} %get-tuple-element.60) | copy-start | bytes 12582916
  111.6 2.5 %copy-start.13 = (bf16[256,2048]{0,1:T(8,128)(2,1)S(1)}, bf16[256,2048]{0,1:T(8,128)(2,1)}, u32[]{:S(2)}) copy-start(bf16[256,2048]{0,1:T(8,128)(2,1)} %copy.145) | copy-start | bytes 3145732
  111.6 2.5 %copy-start.30 = (bf16[32,8,2,128]{3,1,2,0:T(8,128)(2,1)S(1)}, bf16[32,8,2,128]{3,1,2,0:T(8,128)(2,1)}, u32[]{:S(2)}) copy-start(bf16[32,8,2,128]{3,1,2,0:T(8,128)(2,1)} %copy.306) | copy-start | bytes 393220
  112.6 4.2 %copy-start.3 = (f32[16,256,256]{2,1,0:T(8,128)S(1)}, f32[16,256,256]{2,1,0:T(8,128)}, u32[]{:S(2)}) copy-start(f32[16,256,256]{2,1,0:T(8,128)} %get-tuple-element.54) | copy-start | bytes 12582916
  112.6 4.2 %copy-start.12 = (bf16[256,2048]{0,1:T(8,128)(2,1)S(1)}, bf16[256,2048]{0,1:T(8,128)(2,1)}, u32[]{:S(2)}) copy-start(bf16[256,2048]{0,1:T(8,128)(2,1)} %copy.149) | copy-start | bytes 3145732
  112.6 4.2 %copy-start.31 = (bf16[32,8,2,128]{3,1,2,0:T(8,128)(2,1)S(1)}, bf16[32,8,2,128]{3,1,2,0:T(8,128)(2,1)}, u32[]{:S(2)}) copy-start(bf16[32,8,2,128]{3,1,2,0:T(8,128)(2,1)} %copy.304) | copy-start | bytes 393220
  116.7 2.8 %copy-start.4 = (f32[16,256,256]{2,1,0:T(8,128)S(1)}, f32[16,256,256]{2,1,0:T(8,128)}, u32[]{:S(2)}) copy-start(f32[16,256,256]{2,1,0:T(8,128)} %get-tuple-element.56) | copy-start | bytes 12582916
  116.7 3.2 %copy-start.11 = (bf16[256,2048]{0,1:T(8,128)(2,1)S(1)}, bf16[256,2048]{0,1:T(8,128)(2,1)}, u32[]{:S(2)}) copy-start(bf16[256,2048]{0,1:T(8,128)(2,1)} %copy.147) | copy-start | bytes 3145732
  116.7 3.2 %copy-start.32 = (bf16[32,8,2,128]{3,1,2,0:T(8,128)(2,1)S(1)}, bf16[32,8,2,128]{3,1,2,0:T(8,128)(2,1)}, u32[]{:S(2)}) copy-start(bf16[32,8,2,128]{3,1,2,0:T(8,128)(2,1)} %copy.305) | copy-start | bytes 393220
  119.5 3.2 %copy-start.6 = (f32[16,256,256]{1,2,0:T(8,128)S(1)}, f32[16,256,256]{1,2,0:T(8,128)}, u32[]{:S(2)}) copy-start(f32[16,256,256]{1,2,0:T(8,128)} %get-tuple-element.58) | copy-start | bytes 12582916
  119.5 3.2 %copy-start.29 = (pred[256,256]{0,1:T(8,128)(4,1)S(1)}, pred[256,256]{0,1:T(8,128)(4,1)}, u32[]{:S(2)}) copy-start(pred[256,256]{0,1:T(8,128)(4,1)} %copy-done.28) | copy-start | bytes 196612
  119.5 3.2 %copy-start.33 = (bf16[32,8,2,128]{3,1,2,0:T(8,128)(2,1)S(1)}, bf16[32,8,2,128]{3,1,2,0:T(8,128)(2,1)}, u32[]{:S(2)}) copy-start(bf16[32,8,2,128]{3,1,2,0:T(8,128)(2,1)} %copy.307) | copy-start | bytes 393220
  122.7 2.7 %copy-start.34 = (bf16[32,8,2,128]{3,1,2,0:T(8,128)(2,1)S(1)}, bf16[32,8,2,128]{3,1,2,0:T(8,128)(2,1)}, u32[]{:S(2)}) copy-start(bf16[32,8,2,128]{3,1,2,0:T(8,128)(2,1)} %copy.302) | copy-start | bytes 393220
  125.4 2.7 %copy-start.35 = (bf16[32,8,2,128]{3,1,2,0:T(8,128)(2,1)S(1)}, bf16[32,8,2,128]{3,1,2,0:T(8,128)(2,1)}, u32[]{:S(2)}) copy-start(bf16[32,8,2,128]{3,1,2,0:T(8,128)(2,1)} %copy.301) | copy-start | bytes 393220
  128.0 2.6 %copy-start.9 = (bf16[256,2048]{0,1:T(8,128)(2,1)S(1)}, bf16[256,2048]{0,1:T(8,128)(2,1)}, u32[]{:S(2)}) copy-start(bf16[256,2048]{0,1:T(8,128)(2,1)} %get-tuple-element.16) | copy-start | bytes 3145732
  128.0 2.6 %copy-start.24 = (pred[256,256]{0,1:T(8,128)(4,1)S(1)}, pred[256,256]{0,1:T(8,128)(4,1)}, u32[]{:S(2)}) copy-start(pred[256,256]{0,1:T(8,128)(4,1)} %copy-done.23) | copy-start | bytes 196612
  128.0 2.7 %copy-start.36 = (bf16[32,8,2,128]{3,1,2,0:T(8,128)(2,1)S(1)}, bf16[32,8,2,128]{3,1,2,0:T(8,128)(2,1)}, u32[]{:S(2)}) copy-start(bf16[32,8,2,128]{3,1,2,0:T(8,128)(2,1)} %copy.300) | copy-start | bytes 393220
  130.7 2.7 %copy-start.7 = (f32[16,256,256]{1,2,0:T(8,128)S(1)}, f32[16,256,256]{1,2,0:T(8,128)}, u32[]{:S(2)}) copy-start(f32[16,256,256]{1,2,0:T(8,128)} %get-tuple-element.58) | copy-start | bytes 12582916
  130.7 2.7 %copy-start.18 = (f32[256,256]{0,1:T(8,128)S(1)}, f32[256,256]{0,1:T(8,128)}, u32[]{:S(2)}) copy-start(f32[256,256]{0,1:T(8,128)} %get-tuple-element.64) | copy-start | bytes 786436
  130.7 2.7 %copy-start.19 = (f32[256,256]{0,1:T(8,128)S(1)}, f32[256,256]{0,1:T(8,128)}, u32[]{:S(2)}) copy-start(f32[256,256]{0,1:T(8,128)} %get-tuple-element.65) | copy-start | bytes 786436
  133.4 6.1 %copy-start.2 = (f32[16,256,256]{2,1,0:T(8,128)S(1)}, f32[16,256,256]{2,1,0:T(8,128)}, u32[]{:S(2)}) copy-start(f32[16,256,256]{2,1,0:T(8,128)} %get-tuple-element.52) | copy-start | bytes 12582916
  133.4 6.1 %copy-start.14 = (f32[256,256]{1,0:T(8,128)S(1)}, f32[256,256]{1,0:T(8,128)}, u32[]{:S(2)}) copy-start(f32[256,256]{1,0:T(8,128)} %get-tuple-element.68) | copy-start | bytes 786436
  133.4 6.1 %copy-start.15 = (f32[256,256]{1,0:T(8,128)S(1)}, f32[256,256]{1,0:T(8,128)}, u32[]{:S(2)}) copy-start(f32[256,256]{1,0:T(8,128)} %get-tuple-element.69) | copy-start | bytes 786436
  133.4 6.1 %copy-start.16 = (f32[256,256]{1,0:T(8,128)S(1)}, f32[256,256]{1,0:T(8,128)}, u32[]{:S(2)}) copy-start(f32[256,256]{1,0:T(8,128)} %get-tuple-element.70) | copy-start | bytes 786436
  133.4 6.1 %copy-start.17 = (f32[256,256]{1,0:T(8,128)S(1)}, f32[256,256]{1,0:T(8,128)}, u32[]{:S(2)}) copy-start(f32[256,256]{1,0:T(8,128)} %get-tuple-element.71) | copy-start | bytes 786436
  139.5 6.0 %copy-start.38 = (f32[16,256]{1,0:T(8,128)S(1)}, f32[16,256]{1,0:T(8,128)}, u32[]{:S(2)}) copy-start(f32[16,256]{1,0:T(8,128)} %get-tuple-element.11) | copy-start | bytes 49156
  139.5 6.0 %copy-start.39 = (f32[16,256]{1,0:T(8,128)S(1)}, f32[16,256]{1,0:T(8,128)}, u32[]{:S(2)}) copy-start(f32[16,256]{1,0:T(8,128)} %get-tuple-element.12) | copy-start | bytes 49156
  139.5 6.0 %copy-start.8 = (bf16[256,2048]{0,1:T(8,128)(2,1)S(1)}, bf16[256,2048]{0,1:T(8,128)(2,1)}, u32[]{:S(2)}) copy-start(bf16[256,2048]{0,1:T(8,128)(2,1)} %copy.151) | copy-start | bytes 3145732
  139.5 6.0 %copy-start.27 = (bf16[32,8,2,128]{3,1,2,0:T(8,128)(2,1)S(1)}, bf16[32,8,2,128]{3,1,2,0:T(8,128)(2,1)}, u32[]{:S(2)}) copy-start(bf16[32,8,2,128]{3,1,2,0:T(8,128)(2,1)} %copy.303) | copy-start | bytes 393220
  145.5 7.8 %copy-start.1 = (bf16[256,2048]{1,0:T(8,128)(2,1)S(1)}, bf16[256,2048]{1,0:T(8,128)(2,1)}, u32[]{:S(2)}) copy-start(bf16[256,2048]{1,0:T(8,128)(2,1)} %param.5) | copy-start | bytes 3145732
Sparse Core Ops, SparseCore 0:
  11.2 92.6 all-gather.1
where the time goes:
time: 161 us; the launch traced here: 160 us
  matrix products  46.5 us (29%)
  local copies, waits for them, and re-layouts  36.5 us (23%)
  starting transfers between devices  25.7 us (16%)
  waiting for transfers between devices  23.7 us (15%)
  between operations  14.1 us (9%)
  other arithmetic  13.7 us (9%)
    ppermute x8, starting transfers between devices, passed_along(): return lax.ppermute(block, axis, route)  25.7 us
    dot_general x8, matrix products, shards(): jnp.einsum('hqk,khd->qhd', rounded.reshape(H, rows_dev, rows_dev), source...  25.1 us
    dot_general x8, matrix products, shards(): jnp.einsum('qhd,khd->hqk', query_heads, source_keys.reshape(rows_dev, H,...  21.4 us
    all_gather x1, waiting for transfers between devices, side_by_side(): result, at, done = (lax.all_gather(both, axis, axis=dim, tiled=True), 0, [])  19.1 us
    reduce_sum x2, other arithmetic, shards(): row_total = row_total + jnp.sum(weights * factor, axis=(3, 4))  12 us
    unnamed x104, local copies, waits for them, and re-layouts  10.7 us
    ppermute x4, local copies, waits for them, and re-layouts, passed_along(): return lax.ppermute(block, axis, route)  9.11 us
    ppermute x8, waiting for transfers between devices, passed_along(): return lax.ppermute(block, axis, route)  4.62 us
  transfers between devices with their start and end apart: 9, of which 2 were waited for; matrix products, arithmetic and copies ran while one was open for 27% of the time, Pallas kernels for 0%

commit v1 on v0

v1 whole, which is shorter than its diff:
```python
import functools
import math

import jax
import jax.numpy as jnp
from jax import lax
from jax.experimental import pallas as pl
from jax.experimental.pallas import tpu as pltpu
from jax.sharding import PartitionSpec as P

H = 16
HD = 128
LMAX = 8
TILE = 128
ROWS = 256
W = 2048
HALF = W // 2
HB = 4
BW = HB * HD
NEG = -1e30
SCALE = math.log2(math.e) / math.sqrt(HD)
PAYLOAD = 3 * HALF + 128
REPLY = HALF + 128
VMEM_LIMIT = 20 * 1024 * 1024

f32 = jnp.float32
bf16 = jnp.bfloat16


def log_multiplicity(links_ref, counts_ref, i, cand, own):
    times = jnp.int32(1 if own else 0)
    for s in range(LMAX):
        hit = (links_ref[i, s] == cand) & (s < counts_ref[i])
        times = times + hit.astype(jnp.int32)
    return jnp.where(times == 0, NEG, jnp.where(times == 1, 0.0, 1.0)).astype(f32)


def attend(q, sources, before=None, reply=None):
    ones = jnp.ones((ROWS, HD), bf16)
    scores = [
        lax.dot_general(q, k, (((1,), (1,)), ((), ())), preferred_element_type=f32)
        for k, _, _ in sources
    ]
    values = [jnp.concatenate([v, ones], axis=1) for _, v, _ in sources]
    result = []
    for i in range(2):
        rows = slice(i * TILE, (i + 1) * TILE)
        blocks = [
            [s[rows, j * TILE : (j + 1) * TILE] * SCALE + bias[i][j] for j in range(2)]
            for s, (_, _, bias) in zip(scores, sources)
        ]
        top = functools.reduce(jnp.maximum, [b for pair in blocks for b in pair])
        m = jnp.max(top, axis=1, keepdims=True)
        if before is not None:
            m = jnp.maximum(m, before[0][rows])
        if reply is not None:
            m = jnp.maximum(m, reply[1][rows])
        both = None
        for pair, v in zip(blocks, values):
            p = jnp.concatenate([jnp.exp2(b - m).astype(bf16) for b in pair], axis=1)
            part = jnp.dot(p, v, preferred_element_type=f32)
            both = part if both is None else both + part
        acc, l = both[:, :HD], both[:, HD:]
        if before is not None:
            a = jnp.exp2(before[0][rows] - m)
            acc = acc + before[2][rows] * a
            l = l + before[1][rows] * a
        if reply is not None:
            a = jnp.exp2(reply[1][rows] - m)
            acc = acc + reply[0][rows].astype(f32) * a
            l = l + a
        result.append((m, l, acc))
    return result


def both_tiles(result, which):
    return jnp.concatenate([result[0][which], result[1][which]], axis=0)


def pack_kernel(links_ref, counts_ref, q_ref, k_ref, v_ref, a_ref, b_ref):
    i = pl.program_id(0) // 2
    g = lax.axis_index("group")
    even = (g % 2) == 0
    lane = lax.broadcasted_iota(jnp.int32, (64, 128), 1)
    near_a = jnp.where(even, 5, 7)
    near_b = jnp.where(even, 7, 5)
    for ref, near, kv, qs in ((a_ref, near_a, 0, HALF), (b_ref, near_b, HALF, 0)):
        ref[:, 0:HALF] = k_ref[:, kv : kv + HALF]
        ref[:, HALF : 2 * HALF] = v_ref[:, kv : kv + HALF]
        ref[:, 2 * HALF : 3 * HALF] = q_ref[:, qs : qs + HALF]
        extra = jnp.zeros((64, 128), f32)
        for n, cand in enumerate((near * 2, near * 2 + 1, 12, 13)):
            bias = log_multiplicity(links_ref, counts_ref, i, cand, False)
            extra = jnp.where(lane == n, bias, extra)
        ref[:, 3 * HALF :] = extra.astype(bf16)


def pack(links, counts, q, k, v):
    rows = pl.BlockSpec((64, W), lambda s: (s, 0))
    out = pl.BlockSpec((64, PAYLOAD), lambda s: (s, 0))
    smem = pl.BlockSpec(memory_space=pltpu.SMEM)
    return pl.pallas_call(
        pack_kernel,
        grid=(4,),
        in_specs=[smem, smem, rows, rows, rows],
        out_specs=[out, out],
        out_shape=[jax.ShapeDtypeStruct((ROWS, PAYLOAD), bf16)] * 2,
        compiler_params=pltpu.CompilerParams(vmem_limit_bytes=VMEM_LIMIT),
        cost_estimate=pl.CostEstimate(flops=0, bytes_accessed=6 * 1024 * 1024, transcendentals=0),
        name="pack",
    )(links, counts, q, k, v)


def remote_kernel(q_ref, bias_ref, k0_ref, v0_ref, k1_ref, v1_ref, out_ref):
    step = pl.program_id(0)
    lane = lax.broadcasted_iota(jnp.int32, (ROWS, 128), 1)
    bias = [
        [
            [
                jnp.broadcast_to(
                    bias_ref[i * TILE : (i + 1) * TILE, 2 * s + j : 2 * s + j + 1].astype(f32),
                    (TILE, TILE),
                )
                for j in range(2)
            ]
            for i in range(2)
        ]
        for s in range(2)
    ]
    stats = jnp.zeros((ROWS, 128), f32)
    rows_out = []
    for h in range(HB):
        c = slice(h * HD, (h + 1) * HD)
        done = attend(
            q_ref[:, c],
            [(k0_ref[:, c], v0_ref[:, c], bias[0]), (k1_ref[:, c], v1_ref[:, c], bias[1])],
        )
        m, l, acc = (both_tiles(done, n) for n in range(3))
        rows_out.append((acc / l).astype(bf16))
        total = m + jnp.log2(l)
        high = total.astype(bf16).astype(f32)
        rest = total - high
        middle = rest.astype(bf16).astype(f32)
        low = rest - middle
        for n, piece in enumerate((high, middle, low)):
            stats = jnp.where(lane == 3 * h + n, piece, stats)
    block = jnp.concatenate(rows_out, axis=1)
    stats = stats.astype(bf16)

    @pl.when(step == 0)
    def _():
        out_ref[:, 0:BW] = block
        out_ref[:, 2 * BW :] = stats

    @pl.when(step == 1)
    def _():
        out_ref[:, BW : 2 * BW] = block
        moved = pltpu.roll(stats.astype(f32), 64, 1)
        out_ref[:, 2 * BW :] = jnp.where(
            lane < 64, out_ref[:, 2 * BW :].astype(f32), moved
        ).astype(bf16)


def remote(asked, k, v, other, half):
    first = half * 2
    cost = 2 * 2 * 2 * ROWS * ROWS * HALF
    return pl.pallas_call(
        remote_kernel,
        grid=(2,),
        in_specs=[
            pl.BlockSpec((ROWS, BW), lambda s: (0, 4 + s)),
            pl.BlockSpec((ROWS, 128), lambda s: (0, 3 * HALF // 128)),
            pl.BlockSpec((ROWS, BW), lambda s: (0, first + s)),
            pl.BlockSpec((ROWS, BW), lambda s: (0, first + s)),
            pl.BlockSpec((ROWS, BW), lambda s: (0, s)),
            pl.BlockSpec((ROWS, BW), lambda s: (0, 2 + s)),
        ],
        out_specs=pl.BlockSpec((ROWS, REPLY), lambda s: (0, 0)),
        out_shape=jax.ShapeDtypeStruct((ROWS, REPLY), bf16),
        compiler_params=pltpu.CompilerParams(vmem_limit_bytes=VMEM_LIMIT),
        cost_estimate=pl.CostEstimate(
            flops=cost, bytes_accessed=3 * 1024 * 1024, transcendentals=ROWS * ROWS * H
        ),
        name="remote",
    )(asked, asked, k, v, other, other)


def local_kernel(plan, has_before, has_reply, last, *refs):
    refs = list(refs)
    links_ref, counts_ref = refs.pop(0), refs.pop(0)
    q_ref = refs.pop(0)
    step = pl.program_id(0)
    g = lax.axis_index("group")
    odd_core = (lax.axis_index("rank") % 2) == 1
    odd_group = (g % 2) == 1
    sources = []
    for role in plan:
        if role == "pairs":
            ka, va, kb, vb = (refs.pop(0) for _ in range(4))
            first_half = step < 2
            k = jnp.where(first_half, ka[...], kb[...])
            v = jnp.where(first_half, va[...], vb[...])
            block = jnp.where(first_half != odd_group, 5, 7)
        else:
            k, v = refs.pop(0)[...], refs.pop(0)[...]
            block = {
                "own": 0,
                "core": jnp.where(odd_core, 2, 3),
                "relay": jnp.where(odd_core, 3, 2),
                "minus": 1,
                "plus": 4,
            }[role]
        bias = [
            [
                log_multiplicity(links_ref, counts_ref, i, block * 2 + j, role == "own" and i == j)
                for j in range(2)
            ]
            for i in range(2)
        ]
        sources.append((k, v, bias))
    if has_before:
        acc_in, ml_in = refs.pop(0), refs.pop(0)
    if has_reply:
        rows_a, stats_a, rows_b, stats_b = (refs.pop(0) for _ in range(4))
        first_half = step < 2
        rows_in = jnp.where(first_half, rows_a[...], rows_b[...])
        stats_in = jnp.where(first_half, stats_a[...].astype(f32), stats_b[...].astype(f32))
        stats_in = jnp.where(step % 2 == 0, stats_in, pltpu.roll(stats_in, 64, 1))
    lane = lax.broadcasted_iota(jnp.int32, (ROWS, 128), 1)
    stats = jnp.zeros((ROWS, 128), f32)
    for h in range(HB):
        c = slice(h * HD, (h + 1) * HD)
        before = reply = None
        if has_before:
            ml = ml_in[...]
            before = (
                ml[:, 2 * h : 2 * h + 1],
                jnp.broadcast_to(ml[:, 2 * h + 1 : 2 * h + 2], (ROWS, HD)),
                acc_in[:, c],
            )
        if has_reply:
            total = (
                stats_in[:, 3 * h : 3 * h + 1]
                + stats_in[:, 3 * h + 1 : 3 * h + 2]
                + stats_in[:, 3 * h + 2 : 3 * h + 3]
            )
            reply = (rows_in[:, c], total)
        done = attend(q_ref[:, c], [(k[:, c], v[:, c], b) for k, v, b in sources], before, reply)
        m, l, acc = (both_tiles(done, n) for n in range(3))
        if last:
            refs[0][:, c] = (acc / l).astype(bf16)
        else:
            refs[0][:, c] = acc
            stats = jnp.where(lane == 2 * h, m, stats)
            stats = jnp.where(lane == 2 * h + 1, l, stats)
    if not last:
        refs[1][...] = stats


def local(links, counts, q, sources, before=None, reply=None, last=False):
    has_reply = reply is not None
    smem = pl.BlockSpec(memory_space=pltpu.SMEM)
    part = lambda row, at: pl.BlockSpec((ROWS, BW), lambda s: (row, at(s)))
    low = lambda s: jnp.minimum(s, 1)
    high = lambda s: jnp.maximum(s - 2, 0)
    straight = lambda s: s
    specs, args, plan = [smem, smem, part(0, straight)], [links, counts, q], []
    for role, arrays in sources:
        plan.append(role)
        if role == "own":
            specs += [part(0, straight)] * 2
            args += list(arrays)
        elif role == "pairs":
            a, b = arrays
            specs += [part(0, low), part(0, lambda s: 2 + low(s))]
            specs += [part(0, high), part(0, lambda s: 2 + high(s))]
            args += [a, a, b, b]
        else:
            specs += [part(0, straight), part(1, straight)]
            args += [arrays, arrays]
    stat = pl.BlockSpec((ROWS, 128), lambda s: (0, s))
    if before is not None:
        specs += [part(0, straight), stat]
        args += list(before)
    if reply is not None:
        a, b = reply
        tail = pl.BlockSpec((ROWS, 128), lambda s: (0, HALF // 128))
        specs += [part(0, low), tail, part(0, high), tail]
        args += [a, a, b, b]
    if last:
        out_specs = part(0, straight)
        out_shape = jax.ShapeDtypeStruct((ROWS, W), bf16)
    else:
        out_specs = [part(0, straight), stat]
        out_shape = [
            jax.ShapeDtypeStruct((ROWS, W), f32),
            jax.ShapeDtypeStruct((ROWS, 4 * 128), f32),
        ]
    return pl.pallas_call(
        functools.partial(local_kernel, tuple(plan), before is not None, has_reply, last),
        grid=(4,),
        in_specs=specs,
        out_specs=out_specs,
        out_shape=out_shape,
        compiler_params=pltpu.CompilerParams(vmem_limit_bytes=VMEM_LIMIT),
        cost_estimate=pl.CostEstimate(
            flops=(400 if has_reply else 4) * ROWS * ROWS * W * len(plan),
            bytes_accessed=(2 + 2 * len(plan)) * 1024 * 1024,
            transcendentals=ROWS * ROWS * H * len(plan),
        ),
        name="local_" + "_".join(plan),
    )(*args)


def shards(q, k, v, links, counts):
    ranks = lax.axis_size("rank")
    along = lambda x, d: lax.ppermute(x, "rank", [(i, (i + d) % ranks) for i in range(ranks)])
    core = lambda x: lax.ppermute(x, "rank", [(i, i ^ 1) for i in range(ranks)])
    to_a = lambda x: lax.ppermute(x, "group", [(i, i ^ 1) for i in range(4)])
    to_b = lambda x: lax.ppermute(x, "group", [(i, 3 - i) for i in range(4)])

    kv = jnp.concatenate([k, v], axis=0)
    pay_a, pay_b = pack(links, counts, q, k, v)
    from_minus = along(kv, 2)
    from_plus = along(kv, -2)
    got_a = to_a(pay_a)
    got_b = to_b(pay_b)
    from_core = core(kv)
    state = local(links, counts, q, [("own", (k, v)), ("core", from_core)])

    got_a, got_b, state = lax.optimization_barrier((got_a, got_b, state))
    part_a = remote(got_a, k, v, got_b, 1)
    back_a = to_a(part_a)
    part_b = remote(got_b, k, v, got_a, 0)
    back_b = to_b(part_b)
    got_a, got_b, part_a, part_b = lax.optimization_barrier((got_a, got_b, part_a, part_b))
    state = local(links, counts, q, [("pairs", (got_a, got_b))], state)

    from_minus, from_plus, state = lax.optimization_barrier((from_minus, from_plus, state))
    odd = (lax.axis_index("rank") % 2) == 1
    relay = core(jnp.where(odd, from_minus, from_plus))
    near = [("minus", from_minus), ("plus", from_plus)]
    state = local(links, counts, q, near, state, (back_b, back_a))
    return local(links, counts, q, [("relay", relay)], state, None, True)


def solution(mesh):
    rows = P(("group", "rank"), None)
    return jax.shard_map(
        shards,
        mesh=mesh,
        in_specs=(rows, rows, rows, rows, P(("group", "rank"))),
        out_specs=rows,
        check_vma=False,
    )
```

time: 161 us -> 95.4 us (0.59)
  matrix products: 46.5 us -> 0 us
  Pallas kernels: 0 us -> 42.3 us
  local copies, waits for them, and re-layouts: 36.5 us -> 7.29 us
  between operations: 14.1 us -> 0.12 us
  other arithmetic: 13.7 us -> 1.91 us
  starting transfers between devices: 25.7 us -> 16.4 us
  waiting for transfers between devices: 23.7 us -> 27.1 us
    dot_general x16 -> x0, matrix products: 46.5 us -> none  [the longest x8 25.1 us: shards(): jnp.einsum('hqk,khd->qhd', rounded.reshape(H, rows_dev, rows_dev), source...]
    pallas_call x0 -> x7, Pallas kernels: none -> 42.3 us  [the longest x4 31.9 us: local(): pl.pallas_call(functools.partial(local_kernel, tuple(plan), before is not...]
    ppermute x8, waiting for transfers between devices: 4.62 us -> 27.1 us  [the longest x2 24.9 us: shards(): to_a = lambda x: lax.ppermute(x, 'group', [(i, i ^ 1) for i in range(4)])]
    all_gather x1 -> x0, waiting for transfers between devices: 19.1 us -> none  [side_by_side(): result, at, done = (lax.all_gather(both, axis, axis=dim, tiled=True), 0, [])]
    reduce_sum x3 -> x0, other arithmetic: 12.1 us -> none  [the longest x2 12 us: shards(): row_total = row_total + jnp.sum(weights * factor, axis=(3, 4))]
    ppermute x8, starting transfers between devices: 25.7 us -> 16.4 us  [the longest x2 6.05 us: shards(): lax.ppermute(x, 'rank', [(i, (i + d) % ranks) for i in range(ranks)])]
    ppermute x4 -> x0, local copies, waits for them, and re-layouts: 9.11 us -> none  [passed_along(): return lax.ppermute(block, axis, route)]
    mul x20 -> x0, local copies, waits for them, and re-layouts: 5.56 us -> none  [the longest x12 4.45 us: shards(): row_total = row_total + jnp.sum(weights * factor, axis=(3, 4))]
  transfers between devices with their start and end apart: 9 -> 8, of which waited for: 2 -> 3; matrix products, arithmetic and copies ran while one was open for 27% -> 2% of each run, Pallas kernels for 0% -> 36%
where the time goes in v1:
time: 95.4 us; the launch traced here: 95.2 us
  Pallas kernels  42.3 us (44%)
  waiting for transfers between devices  27.1 us (28%)
  starting transfers between devices  16.4 us (17%)
  local copies, waits for them, and re-layouts  7.29 us (8%)
  other arithmetic  1.91 us (2%)
    pallas_call x4, Pallas kernels, local(): pl.pallas_call(functools.partial(local_kernel, tuple(plan), before is not...  31.9 us
    ppermute x2, waiting for transfers between devices, shards(): to_a = lambda x: lax.ppermute(x, 'group', [(i, i ^ 1) for i in range(4)])  24.9 us
    pallas_call x2, Pallas kernels, remote(): pl.pallas_call(remote_kernel, grid=(2,), in_specs=[pl.BlockSpec((ROWS, BW...  7.38 us
    unnamed x21, local copies, waits for them, and re-layouts  6.17 us
    ppermute x2, starting transfers between devices, shards(): lax.ppermute(x, 'rank', [(i, (i + d) % ranks) for i in range(ranks)])  6.05 us
    ppermute x2, starting transfers between devices, shards(): core = lambda x: lax.ppermute(x, 'rank', [(i, i ^ 1) for i in range(ranks)])  5.09 us
    ppermute x2, starting transfers between devices, shards(): to_b = lambda x: lax.ppermute(x, 'group', [(i, 3 - i) for i in range(4)])  3.89 us
    pallas_call x1, Pallas kernels, pack(): pl.pallas_call(pack_kernel, grid=(4,), in_specs=[smem, smem, rows, rows,...  3.03 us
  transfers between devices with their start and end apart: 8, of which 3 were waited for; matrix products, arithmetic and copies ran while one was open for 2% of the time, Pallas kernels for 36%

profile of v1, /device:TPU:1, one launch (start us, length us, event | category | flops | bytes accessed | tf_op | source)
XLA Modules:
  0.0 95.2 jit_solution(3041233356836722512)
XLA Ops:
  0.0 0.0 copy-start
  0.0 0.0 copy-start.3
  0.0 0.0 copy-start.5
  0.0 0.0 copy-start.8
  0.0 0.0 copy-start.9
  0.0 2.5 %constant_dynamic-update-slice_fusion.1 = bf16[512,2048]{1,0:T(8,128)(2,1)} fusion(bf16[256,2048]{1,0:T(8,128)(2,1)} %k0_ref.3), kind=kLoop, calls=%fused_computation.2 | loop fusion | bytes 2097152
  2.5 0.0 copy-done.3
  2.5 1.1 %constant_dynamic-update-slice_fusion = bf16[512,2048]{1,0:T(8,128)(2,1)} fusion(bf16[512,2048]{1,0:T(8,128)(2,1)} %constant_dynamic-update-slice_fusion.1, bf16[256,2048]{1,0:T(8,128)(2,1)S(1)} %copy-done.3), kind=kLoop, calls=%fused_computation.1 | loop fusion | bytes 2097152 | tf_op jit(solution)/shard_map/concatenate | solution.py:322
  3.6 3.2 %collective-permute-start.4 = (bf16[512,2048]{1,0:T(8,128)(2,1)}, bf16[512,2048]{1,0:T(8,128)(2,1)}, u32[]{:S(2)}, u32[]{:S(2)}) collective-permute-start(bf16[512,2048]{1,0:T(8,128)(2,1)} %constant_dynamic-update-slice_fusion), channel_id=1, source_target_pairs={{0,1},{1,0},{2,3},{3,2},{4,5},{5,4},{6,7},{7,6},{8,9},{9,8},{10,11... | collective-permute-start | bytes 6291464 | tf_op jit(solution)/shard_map/ppermute | solution.py:318
  6.8 0.0 collective-permute-start
  6.8 6.1 %collective-permute-start.1 = (bf16[512,2048]{1,0:T(8,128)(2,1)}, bf16[512,2048]{1,0:T(8,128)(2,1)}, u32[]{:S(2)}, u32[]{:S(2)}) collective-permute-start(bf16[512,2048]{1,0:T(8,128)(2,1)} %constant_dynamic-update-slice_fusion), channel_id=1, source_target_pairs={{0,62},{1,63},{2,0},{3,1},{4,2},{5,3},{6,4},{7,5},{8,6},{9,7},{10,... | collective-permute-start | bytes 6291464 | tf_op jit(solution)/shard_map/ppermute | solution.py:317
  12.9 0.0 copy-done
  12.9 0.0 copy-done.5
  12.9 0.0 copy-done.8
  12.9 0.0 copy-done.9
  12.9 3.0 %pack.1 = (bf16[256,3200]{1,0:T(8,128)(2,1)}, bf16[256,3200]{1,0:T(8,128)(2,1)}) custom-call(s32[2,8]{1,0:T(2,128)S(1)} %copy-done.8, s32[2]{0:T(128)S(1)} %copy-done.9, bf16[256,2048]{1,0:T(8,128)(2,1)S(1)} %copy-done.5, bf16[256,2048]{1,0:T(8,128)(2,1)S(1)} %copy-done, bf16[256,2048]{1,0:T(8,128)(2,1)S(1)} %copy-done.3), custom_call_target="tpu_custom_call" | custom-call | bytes 6291456 | tf_op jit(solution)/shard_map/pack/pallas_call | solution.py:102
  15.9 1.3 %collective-permute-start.2 = (bf16[256,3200]{1,0:T(8,128)(2,1)}, bf16[256,3200]{1,0:T(8,128)(2,1)S(1)}, u32[]{:S(2)}, u32[]{:S(2)}) collective-permute-start(bf16[256,3200]{1,0:T(8,128)(2,1)} %get-tuple-element.23), channel_id=1, source_target_pairs={{0,64},{64,0},{128,192},{192,128},{1,65},{65,1},{129,193},{193,129... | collective-permute-start | bytes 4915208 | tf_op jit(solution)/shard_map/ppermute | solution.py:319
  17.2 1.9 %collective-permute-start.3 = (bf16[256,3200]{1,0:T(8,128)(2,1)}, bf16[256,3200]{1,0:T(8,128)(2,1)S(1)}, u32[]{:S(2)}, u32[]{:S(2)}) collective-permute-start(bf16[256,3200]{1,0:T(8,128)(2,1)} %get-tuple-element.24), channel_id=1, source_target_pairs={{0,192},{64,128},{128,64},{192,0},{1,193},{65,129},{129,65},{193,1... | collective-permute-start | bytes 4915208 | tf_op jit(solution)/shard_map/ppermute | solution.py:320
  19.1 0.0 collective-permute-done.4.refs_5_.refs_6_
  19.1 0.0 copy-start.1
  19.1 1.2 %copy-done.1 = bf16[256,2048]{1,0:T(8,128)(2,1)S(1)} copy-done((bf16[256,2048]{1,0:T(8,128)(2,1)S(1)}, bf16[256,2048]{1,0:T(8,128)(2,1)}, u32[]{:S(2)}) %copy-start.1) | copy-done | bytes 1048600
  20.4 0.0 copy-start.4
  20.4 1.2 %copy-done.4 = bf16[256,2048]{1,0:T(8,128)(2,1)S(1)} copy-done((bf16[256,2048]{1,0:T(8,128)(2,1)S(1)}, bf16[256,2048]{1,0:T(8,128)(2,1)}, u32[]{:S(2)}) %copy-start.4) | copy-done | bytes 1048600
  21.6 0.0 copy-start.6
  21.6 1.2 %copy-done.6 = bf16[256,2048]{1,0:T(8,128)(2,1)S(1)} copy-done((bf16[256,2048]{1,0:T(8,128)(2,1)S(1)}, bf16[256,2048]{1,0:T(8,128)(2,1)}, u32[]{:S(2)}) %copy-start.6) | copy-done | bytes 1048600
  22.8 0.0 copy-start.2
  22.8 7.7 %local_own_core.1 = (f32[256,2048]{1,0:T(8,128)S(1)}, f32[256,512]{1,0:T(8,128)S(1)}) custom-call(s32[2,8]{1,0:T(2,128)S(1)} %copy-done.8, s32[2]{0:T(128)S(1)} %copy-done.9, bf16[256,2048]{1,0:T(8,128)(2,1)S(1)} %copy-done.6, bf16[256,2048]{1,0:T(8,128)(2,1)S(1)} %copy-done.1, bf16[256,2048]{1,0:T(8,128)(2,1)S(1)} %copy-done.4, ...), custom_call_target="tpu_custom_call" | custom-call | flops 1073741824 | bytes 6291456 | tf_op jit(solution)/shard_map/local_own_core/pallas_call | solution.py:299
  30.5 22.9 %collective-permute-done.2.q_ref.bias_ref.k1_ref.v1_ref.refs_3_.refs_4_ = bf16[256,3200]{1,0:T(8,128)(2,1)S(1)} collective-permute-done((bf16[256,3200]{1,0:T(8,128)(2,1)}, bf16[256,3200]{1,0:T(8,128)(2,1)S(1)}, u32[]{:S(2)}, u32[]{:S(2)}) %collective-permute-start.2) | collective-permute-done | bytes 1638432 | tf_op jit(solution)/shard_map/ppermute | solution.py:319
  53.4 2.2 %collective-permute-done.3.k1_ref.v1_ref.q_ref.bias_ref.refs_5_.refs_6_ = bf16[256,3200]{1,0:T(8,128)(2,1)S(1)} collective-permute-done((bf16[256,3200]{1,0:T(8,128)(2,1)}, bf16[256,3200]{1,0:T(8,128)(2,1)S(1)}, u32[]{:S(2)}, u32[]{:S(2)}) %collective-permute-start.3) | collective-permute-done | bytes 1638432 | tf_op jit(solution)/shard_map/ppermute | solution.py:320
  55.6 0.0 copy-done.2
  55.6 3.7 %remote.3 = bf16[256,1152]{1,0:T(8,128)(2,1)S(1)} custom-call(bf16[256,3200]{1,0:T(8,128)(2,1)S(1)} %collective-permute-done.3.k1_ref.v1_ref.q_ref.bias_ref.refs_5_.refs_6_, bf16[256,3200]{1,0:T(8,128)(2,1)S(1)} %collective-permute-done.3.k1_ref.v1_ref.q_ref.bias_ref.refs_5_.refs_6_, bf16[256,2048]{1,0:T(8,128)(2,1)S(1)} %copy-done.2, ...), custom_call_target="tpu_custom_call" | custom-call | flops 536870912 | bytes 3145728 | tf_op jit(solution)/shard_map/remote/pallas_call | solution.py:167
  59.3 2.0 %collective-permute-start.6 = (bf16[256,1152]{1,0:T(8,128)(2,1)S(1)}, bf16[256,1152]{1,0:T(8,128)(2,1)S(1)}, u32[]{:S(2)}, u32[]{:S(2)}) collective-permute-start(bf16[256,1152]{1,0:T(8,128)(2,1)S(1)} %remote.3), channel_id=1, source_target_pairs={{0,192},{64,128},{128,64},{192,0},{1,193},{65,129},{129,65},{193,1... | collective-permute-start | bytes 1769480 | tf_op jit(solution)/shard_map/ppermute | solution.py:320
  61.3 3.7 %remote.2 = bf16[256,1152]{1,0:T(8,128)(2,1)S(1)} custom-call(bf16[256,3200]{1,0:T(8,128)(2,1)S(1)} %collective-permute-done.2.q_ref.bias_ref.k1_ref.v1_ref.refs_3_.refs_4_, bf16[256,3200]{1,0:T(8,128)(2,1)S(1)} %collective-permute-done.2.q_ref.bias_ref.k1_ref.v1_ref.refs_3_.refs_4_, bf16[256,2048]{1,0:T(8,128)(2,1)S(1)} %copy-done.2, ...), custom_call_target="tpu_custom_call" | custom-call | flops 536870912 | bytes 3145728 | tf_op jit(solution)/shard_map/remote/pallas_call | solution.py:167
  65.0 0.1 collective-permute-start.7
  65.1 7.4 %local_pairs.1 = (f32[256,2048]{1,0:T(8,128)S(1)}, f32[256,512]{1,0:T(8,128)S(1)}) custom-call(s32[2,8]{1,0:T(2,128)S(1)} %copy-done.8, s32[2]{0:T(128)S(1)} %copy-done.9, bf16[256,2048]{1,0:T(8,128)(2,1)S(1)} %copy-done.6, bf16[256,3200]{1,0:T(8,128)(2,1)S(1)} %collective-permute-done.2.q_ref.bias_ref.k1_ref.v1_ref.refs_3_.refs_4_, ...), custom_call_target="tpu_custom_call" | custom-call | flops 536870912 | bytes 4194304 | tf_op jit(solution)/shard_map/local_pairs/pallas_call | solution.py:299
  72.4 0.0 collective-permute-done.refs_3_.refs_4_
  72.4 0.0 collective-permute-done.1.refs_5_.refs_6_
  72.4 0.0 copy-start.7
  72.4 1.9 %broadcast_select_fusion = bf16[512,2048]{1,0:T(8,128)(2,1)S(1)} fusion(bf16[512,2048]{1,0:T(8,128)(2,1)} %collective-permute-done.refs_3_.refs_4_, bf16[512,2048]{1,0:T(8,128)(2,1)} %collective-permute-done.1.refs_5_.refs_6_, pred[]{:T(512)S(6)} %eq.5), kind=kLoop, calls=%fused_computation | loop fusion | flops 1048576 | bytes 6291457 | tf_op jit(solution)/shard_map/jit(_where)/select_n | solution.py:341
  74.4 1.9 %collective-permute-start.5 = (bf16[512,2048]{1,0:T(8,128)(2,1)S(1)}, bf16[512,2048]{1,0:T(8,128)(2,1)S(1)}, u32[]{:S(2)}, u32[]{:S(2)}) collective-permute-start(bf16[512,2048]{1,0:T(8,128)(2,1)S(1)} %broadcast_select_fusion), channel_id=1, source_target_pairs={{0,1},{1,0},{2,3},{3,2},{4,5},{5,4},{6,7},{7,6},{8,9},{9,8},{10,11... | collective-permute-start | bytes 6291464 | tf_op jit(solution)/shard_map/ppermute | solution.py:318
  76.2 0.0 collective-permute-done.6.refs_9_.refs_10_
  76.2 2.0 %collective-permute-done.7.refs_11_.refs_12_ = bf16[256,1152]{1,0:T(8,128)(2,1)S(1)} collective-permute-done((bf16[256,1152]{1,0:T(8,128)(2,1)S(1)}, bf16[256,1152]{1,0:T(8,128)(2,1)S(1)}, u32[]{:S(2)}, u32[]{:S(2)}) %collective-permute-start.7) | collective-permute-done | bytes 589856 | tf_op jit(solution)/shard_map/ppermute | solution.py:319
  78.3 0.0 copy-done.7
  78.3 9.2 %local_minus_plus.1 = (f32[256,2048]{1,0:T(8,128)S(1)}, f32[256,512]{1,0:T(8,128)S(1)}) custom-call(s32[2,8]{1,0:T(2,128)S(1)} %copy-done.8, s32[2]{0:T(128)S(1)} %copy-done.9, bf16[256,2048]{1,0:T(8,128)(2,1)S(1)} %copy-done.7, bf16[512,2048]{1,0:T(8,128)(2,1)} %collective-permute-done.refs_3_.refs_4_, ...), custom_call_target="tpu_custom_call" | custom-call | flops 107374182400 | bytes 6291456 | tf_op jit(solution)/shard_map/local_minus_plus/pallas_call | solution.py:299
  87.5 0.0 collective-permute-done.5.refs_3_.refs_4_
  87.5 7.7 %local_relay.1 = bf16[256,2048]{1,0:T(8,128)(2,1)} custom-call(s32[2,8]{1,0:T(2,128)S(1)} %copy-done.8, s32[2]{0:T(128)S(1)} %copy-done.9, bf16[256,2048]{1,0:T(8,128)(2,1)S(1)} %copy-done.7, bf16[512,2048]{1,0:T(8,128)(2,1)S(1)} %collective-permute-done.5.refs_3_.refs_4_, bf16[512,2048]{1,0:T(8,128)(2,1)S(1)} %collective-permute-done.5.refs_3_.refs_4_, ...), custom_call_target="tpu_custom_call" | custom-call | flops 536870912 | bytes 4194304 | tf_op jit(solution)/shard_map/local_relay/pallas_call | solution.py:299
Async XLA Ops:
  0.0 12.9 %copy-start = (bf16[256,2048]{1,0:T(8,128)(2,1)S(1)}, bf16[256,2048]{1,0:T(8,128)(2,1)}, u32[]{:S(2)}) copy-start(bf16[256,2048]{1,0:T(8,128)(2,1)} %k0_ref.3) | copy-start | bytes 3145732
  0.0 2.5 %copy-start.3 = (bf16[256,2048]{1,0:T(8,128)(2,1)S(1)}, bf16[256,2048]{1,0:T(8,128)(2,1)}, u32[]{:S(2)}) copy-start(bf16[256,2048]{1,0:T(8,128)(2,1)} %v0_ref.3) | copy-start | bytes 3145732
  0.0 12.9 %copy-start.5 = (bf16[256,2048]{1,0:T(8,128)(2,1)S(1)}, bf16[256,2048]{1,0:T(8,128)(2,1)}, u32[]{:S(2)}) copy-start(bf16[256,2048]{1,0:T(8,128)(2,1)} %refs_2_.7) | copy-start | bytes 3145732
  0.0 12.9 %copy-start.8 = (s32[2,8]{1,0:T(2,128)S(1)}, s32[2,8]{1,0:T(2,128)}, u32[]{:S(2)}) copy-start(s32[2,8]{1,0:T(2,128)} %refs_0_.7) | copy-start | bytes 196
  0.0 12.9 %copy-start.9 = (s32[2]{0:T(128)S(1)}, s32[2]{0:T(128)}, u32[]{:S(2)}) copy-start(s32[2]{0:T(128)} %refs_1_.7) | copy-start | bytes 28
  3.6 15.5 %collective-permute-start.4 = (bf16[512,2048]{1,0:T(8,128)(2,1)}, bf16[512,2048]{1,0:T(8,128)(2,1)}, u32[]{:S(2)}, u32[]{:S(2)}) collective-permute-start(bf16[512,2048]{1,0:T(8,128)(2,1)} %constant_dynamic-update-slice_fusion), channel_id=1, source_target_pairs={{0,1},{1,0},{2,3},{3,2},{4,5},{5,4},{6,7},{7,6},{8,9},{9,8},{10,11... | collective-permute-start | bytes 6291464 | tf_op jit(solution)/shard_map/ppermute | solution.py:318
  6.8 65.6 %collective-permute-start = (bf16[512,2048]{1,0:T(8,128)(2,1)}, bf16[512,2048]{1,0:T(8,128)(2,1)}, u32[]{:S(2)}, u32[]{:S(2)}) collective-permute-start(bf16[512,2048]{1,0:T(8,128)(2,1)} %constant_dynamic-update-slice_fusion), channel_id=1, source_target_pairs={{0,2},{1,3},{2,4},{3,5},{4,6},{5,7},{6,8},{7,9},{8,10},{9,11},{10,... | collective-permute-start | bytes 6291464 | tf_op jit(solution)/shard_map/ppermute | solution.py:317
  6.8 65.6 %collective-permute-start.1 = (bf16[512,2048]{1,0:T(8,128)(2,1)}, bf16[512,2048]{1,0:T(8,128)(2,1)}, u32[]{:S(2)}, u32[]{:S(2)}) collective-permute-start(bf16[512,2048]{1,0:T(8,128)(2,1)} %constant_dynamic-update-slice_fusion), channel_id=1, source_target_pairs={{0,62},{1,63},{2,0},{3,1},{4,2},{5,3},{6,4},{7,5},{8,6},{9,7},{10,... | collective-permute-start | bytes 6291464 | tf_op jit(solution)/shard_map/ppermute | solution.py:317
  15.9 37.4 %collective-permute-start.2 = (bf16[256,3200]{1,0:T(8,128)(2,1)}, bf16[256,3200]{1,0:T(8,128)(2,1)S(1)}, u32[]{:S(2)}, u32[]{:S(2)}) collective-permute-start(bf16[256,3200]{1,0:T(8,128)(2,1)} %get-tuple-element.23), channel_id=1, source_target_pairs={{0,64},{64,0},{128,192},{192,128},{1,65},{65,1},{129,193},{193,129... | collective-permute-start | bytes 4915208 | tf_op jit(solution)/shard_map/ppermute | solution.py:319
  17.2 38.3 %collective-permute-start.3 = (bf16[256,3200]{1,0:T(8,128)(2,1)}, bf16[256,3200]{1,0:T(8,128)(2,1)S(1)}, u32[]{:S(2)}, u32[]{:S(2)}) collective-permute-start(bf16[256,3200]{1,0:T(8,128)(2,1)} %get-tuple-element.24), channel_id=1, source_target_pairs={{0,192},{64,128},{128,64},{192,0},{1,193},{65,129},{129,65},{193,1... | collective-permute-start | bytes 4915208 | tf_op jit(solution)/shard_map/ppermute | solution.py:320
  19.1 1.2 %copy-start.1 = (bf16[256,2048]{1,0:T(8,128)(2,1)S(1)}, bf16[256,2048]{1,0:T(8,128)(2,1)}, u32[]{:S(2)}) copy-start(bf16[256,2048]{1,0:T(8,128)(2,1)} %k0_ref.3) | copy-start | bytes 3145732
  20.4 1.2 %copy-start.4 = (bf16[256,2048]{1,0:T(8,128)(2,1)S(1)}, bf16[256,2048]{1,0:T(8,128)(2,1)}, u32[]{:S(2)}) copy-start(bf16[256,2048]{1,0:T(8,128)(2,1)} %v0_ref.3) | copy-start | bytes 3145732
  21.6 1.2 %copy-start.6 = (bf16[256,2048]{1,0:T(8,128)(2,1)S(1)}, bf16[256,2048]{1,0:T(8,128)(2,1)}, u32[]{:S(2)}) copy-start(bf16[256,2048]{1,0:T(8,128)(2,1)} %refs_2_.7) | copy-start | bytes 3145732
  22.8 32.7 %copy-start.2 = (bf16[256,2048]{1,0:T(8,128)(2,1)S(1)}, bf16[256,2048]{1,0:T(8,128)(2,1)}, u32[]{:S(2)}) copy-start(bf16[256,2048]{1,0:T(8,128)(2,1)} %k0_ref.3) | copy-start | bytes 3145732
  59.3 17.0 %collective-permute-start.6 = (bf16[256,1152]{1,0:T(8,128)(2,1)S(1)}, bf16[256,1152]{1,0:T(8,128)(2,1)S(1)}, u32[]{:S(2)}, u32[]{:S(2)}) collective-permute-start(bf16[256,1152]{1,0:T(8,128)(2,1)S(1)} %remote.3), channel_id=1, source_target_pairs={{0,192},{64,128},{128,64},{192,0},{1,193},{65,129},{129,65},{193,1... | collective-permute-start | bytes 1769480 | tf_op jit(solution)/shard_map/ppermute | solution.py:320
  65.0 13.3 %collective-permute-start.7 = (bf16[256,1152]{1,0:T(8,128)(2,1)S(1)}, bf16[256,1152]{1,0:T(8,128)(2,1)S(1)}, u32[]{:S(2)}, u32[]{:S(2)}) collective-permute-start(bf16[256,1152]{1,0:T(8,128)(2,1)S(1)} %remote.2), channel_id=1, source_target_pairs={{0,64},{64,0},{128,192},{192,128},{1,65},{65,1},{129,193},{193,129... | collective-permute-start | bytes 1769480 | tf_op jit(solution)/shard_map/ppermute | solution.py:319
  72.4 5.8 %copy-start.7 = (bf16[256,2048]{1,0:T(8,128)(2,1)S(1)}, bf16[256,2048]{1,0:T(8,128)(2,1)}, u32[]{:S(2)}) copy-start(bf16[256,2048]{1,0:T(8,128)(2,1)} %refs_2_.7) | copy-start | bytes 3145732
  74.4 13.2 %collective-permute-start.5 = (bf16[512,2048]{1,0:T(8,128)(2,1)S(1)}, bf16[512,2048]{1,0:T(8,128)(2,1)S(1)}, u32[]{:S(2)}, u32[]{:S(2)}) collective-permute-start(bf16[512,2048]{1,0:T(8,128)(2,1)S(1)} %broadcast_select_fusion), channel_id=1, source_target_pairs={{0,1},{1,0},{2,3},{3,2},{4,5},{5,4},{6,7},{7,6},{8,9},{9,8},{10,11... | collective-permute-start | bytes 6291464 | tf_op jit(solution)/shard_map/ppermute | solution.py:318

commit v2 on v0

v2 whole, which is shorter than its diff:
```python
import functools
import math

import jax
import jax.numpy as jnp
from jax import lax
from jax.experimental import pallas as pl
from jax.experimental.pallas import tpu as pltpu
from jax.sharding import PartitionSpec as P

H = 16
HD = 128
LMAX = 8
TILE = 128
ROWS = 256
W = 2048
HALF = W // 2
NEG = -1e30
SCALE = math.log2(math.e) / math.sqrt(HD)
PAYLOAD = 3 * ROWS + 16
REPLY = HALF + 32
PACK_LIMIT = 20 * 1024 * 1024
VMEM_LIMIT = 20 * 1024 * 1024

f32 = jnp.float32
bf16 = jnp.bfloat16


def log_multiplicity(links_ref, counts_ref, i, cand, own):
    times = jnp.int32(1 if own else 0)
    for s in range(LMAX):
        hit = (links_ref[i, s] == cand) & (s < counts_ref[i])
        times = times + hit.astype(jnp.int32)
    return jnp.where(times == 0, NEG, jnp.where(times == 1, 0.0, 1.0)).astype(f32)


def bias_row(left, right):
    lane = lax.broadcasted_iota(jnp.int32, (1, ROWS), 1)
    return jnp.where(lane < TILE, left, right)


def score(q, sources):
    raw, tops = [], []
    for k, _, bias in sources:
        s = lax.dot_general(k, q, (((1,), (1,)), ((), ())), preferred_element_type=f32)
        for j in range(2):
            block = s[j * TILE : (j + 1) * TILE]
            raw.append((block, bias[j]))
            tops.append(jnp.max(block, axis=0, keepdims=True) * SCALE + bias[j])
    return raw, tops


def weigh(scored, before=None, reply=None):
    raw, tops = scored
    if before is not None:
        tops = tops + [before[0]]
    if reply is not None:
        tops = tops + [reply[1]]
    m = functools.reduce(jnp.maximum, tops)
    p = [jnp.exp2(block * SCALE + (bias - m)).astype(bf16) for block, bias in raw]
    return m, jnp.concatenate(p, axis=0)


def mix(weighed, sources, before=None, reply=None):
    m, p = weighed
    values = jnp.concatenate([v.T for _, v, _ in sources], axis=1)
    values = jnp.concatenate([values, jnp.ones((16, values.shape[1]), bf16)], axis=0)
    both = jnp.dot(values, p, preferred_element_type=f32)
    acc, l = both[:HD], both[HD : HD + 1]
    if before is not None:
        a = jnp.exp2(before[0] - m)
        acc = acc + before[2] * a
        l = l + before[1] * a
    if reply is not None:
        a = jnp.exp2(reply[1] - m)
        acc = acc + reply[0].astype(f32) * a
        l = l + a
    return m, l, acc


def over_heads(heads, load, store):
    held, scored, weighed = {}, {}, {}
    for t in range(heads + 2):
        if t < heads:
            held[t] = load(t)
            scored[t] = score(*held[t][:2])
        if 0 <= t - 1 < heads:
            weighed[t - 1] = weigh(scored.pop(t - 1), *held[t - 1][2:])
        if t >= 2:
            _, sources, before, reply = held.pop(t - 2)
            store(t - 2, *mix(weighed.pop(t - 2), sources, before, reply))


def pack_kernel(links_ref, counts_ref, q_hbm, k_hbm, v_hbm, kv_ref, a_ref, b_ref, table_ref, sems):
    g = lax.axis_index("group")
    even = (g % 2) == 0
    copies = []

    def begin(src, dst):
        copies.append(pltpu.make_async_copy(src, dst, sems.at[len(copies)]))
        copies[-1].start()

    begin(k_hbm, kv_ref.at[pl.ds(0, ROWS)])
    begin(v_hbm, kv_ref.at[pl.ds(ROWS, ROWS)])
    begin(q_hbm.at[:, pl.ds(HALF, HALF)], a_ref.at[pl.ds(2 * ROWS, ROWS)])
    begin(q_hbm.at[:, pl.ds(0, HALF)], b_ref.at[pl.ds(2 * ROWS, ROWS)])
    for i in range(2):
        for c in range(16):
            table_ref[i, c] = log_multiplicity(links_ref, counts_ref, i, c, c == i)
    row = lax.broadcasted_iota(jnp.int32, (16, 128), 0)
    for ref, near in ((a_ref, jnp.where(even, 5, 7)), (b_ref, jnp.where(even, 7, 5))):
        extra = jnp.zeros((16, 128), f32)
        for i in range(2):
            for n, cand in enumerate((near * 2, near * 2 + 1, 12, 13)):
                extra = jnp.where(row == 4 * i + n, table_ref[i, cand], extra)
        ref[3 * ROWS :, 0:128] = extra.astype(bf16)
        ref[3 * ROWS :, 128:] = jnp.zeros((16, HALF - 128), bf16)
    copies[0].wait()
    for ref, at in ((a_ref, 0), (b_ref, HALF)):
        ref[0:ROWS] = kv_ref[0:ROWS, at : at + HALF]
    copies[1].wait()
    for ref, at in ((a_ref, 0), (b_ref, HALF)):
        ref[ROWS : 2 * ROWS] = kv_ref[ROWS:, at : at + HALF]
    copies[2].wait()
    copies[3].wait()


def pack(links, counts, q, k, v):
    smem = pl.BlockSpec(memory_space=pltpu.SMEM)
    vmem = pl.BlockSpec(memory_space=pltpu.VMEM)
    hbm = pl.BlockSpec(memory_space=pltpu.HBM)
    return pl.pallas_call(
        pack_kernel,
        in_specs=[smem, smem, hbm, hbm, hbm],
        out_specs=[vmem, vmem, vmem, smem],
        out_shape=[
            jax.ShapeDtypeStruct((2 * ROWS, W), bf16),
            jax.ShapeDtypeStruct((PAYLOAD, HALF), bf16),
            jax.ShapeDtypeStruct((PAYLOAD, HALF), bf16),
            jax.ShapeDtypeStruct((2, 16), f32),
        ],
        scratch_shapes=[pltpu.SemaphoreType.DMA((4,))],
        compiler_params=pltpu.CompilerParams(vmem_limit_bytes=PACK_LIMIT),
        cost_estimate=pl.CostEstimate(flops=0, bytes_accessed=8 * 1024 * 1024, transcendentals=0),
        name="pack",
    )(links, counts, q, k, v)


def remote_kernel(half, asked_ref, kv_ref, other_ref, out_ref):
    extra = asked_ref[3 * ROWS :, 0:128].astype(f32)
    bias = [
        jnp.concatenate([extra[n : n + 1], extra[4 + n : 5 + n]], axis=1) for n in range(4)
    ]
    stats = [[], [], []]

    def load(h):
        c = slice(h * HD, (h + 1) * HD)
        own = slice(half * HALF + h * HD, half * HALF + (h + 1) * HD)
        sources = [
            (kv_ref[0:ROWS, own], kv_ref[ROWS:, own], bias[0:2]),
            (other_ref[0:ROWS, c], other_ref[ROWS : 2 * ROWS, c], bias[2:4]),
        ]
        return asked_ref[2 * ROWS : 3 * ROWS, c], sources, None, None

    def store(h, m, l, acc):
        out_ref[h * HD : (h + 1) * HD] = (acc / l).astype(bf16)
        total = m + jnp.log2(l)
        high = total.astype(bf16).astype(f32)
        rest = total - high
        middle = rest.astype(bf16).astype(f32)
        for rows, piece in zip(stats, (high, middle, rest - middle)):
            rows.append(piece)

    over_heads(H // 2, load, store)
    pieces = [jnp.concatenate(rows, axis=0) for rows in stats]
    pieces.append(jnp.zeros_like(pieces[0]))
    out_ref[HALF:] = jnp.concatenate(pieces, axis=0).astype(bf16)


def remote(asked, kv, other, half):
    vmem = pl.BlockSpec(memory_space=pltpu.VMEM)
    return pl.pallas_call(
        functools.partial(remote_kernel, half),
        in_specs=[vmem] * 3,
        out_specs=vmem,
        out_shape=jax.ShapeDtypeStruct((REPLY, ROWS), bf16),
        compiler_params=pltpu.CompilerParams(vmem_limit_bytes=VMEM_LIMIT),
        cost_estimate=pl.CostEstimate(
            flops=800 * ROWS * ROWS * HALF,
            bytes_accessed=1024 * 1024,
            transcendentals=ROWS * ROWS * H,
        ),
        name="remote",
    )(asked, kv, other)


def local_kernel(plan, has_before, has_reply, last, *refs):
    refs = list(refs)
    table_ref, q_ref = refs.pop(0), refs.pop(0)
    odd_core = (lax.axis_index("rank") % 2) == 1
    odd_group = (lax.axis_index("group") % 2) == 1
    sources = []
    for role in plan:
        if role == "pairs":
            arrays = (refs.pop(0), refs.pop(0))
            blocks = (jnp.where(odd_group, 7, 5), jnp.where(odd_group, 5, 7))
        else:
            arrays = refs.pop(0)
            block = {
                "own": 0,
                "core": jnp.where(odd_core, 2, 3),
                "relay": jnp.where(odd_core, 3, 2),
                "first": jnp.where(odd_core, 1, 4),
                "second": jnp.where(odd_core, 4, 1),
            }[role]
            blocks = (block, block)
        bias = [
            [bias_row(table_ref[0, block * 2 + j], table_ref[1, block * 2 + j]) for j in range(2)]
            for block in blocks
        ]
        sources.append((role, arrays, bias))
    if has_before:
        acc_in, ml_in = refs.pop(0), refs.pop(0)
    if has_reply:
        reply_refs = (refs.pop(0), refs.pop(0))
        totals = []
        for ref in reply_refs:
            tail = ref[HALF:].astype(f32)
            totals.append(tail[0:8] + tail[8:16] + tail[16:24])
    tops, sums, copies = [], [], []

    def load(h):
        half, inner = h // (H // 2), h % (H // 2)
        c = slice(h * HD, (h + 1) * HD)
        low = slice(inner * HD, (inner + 1) * HD)
        given = []
        for role, arrays, bias in sources:
            array, at = (arrays[half], low) if role == "pairs" else (arrays, c)
            given.append((array[0:ROWS, at], array[ROWS : 2 * ROWS, at], bias[half]))
        before = reply = None
        if has_before:
            before = (ml_in[h : h + 1], ml_in[H + h : H + h + 1], acc_in[c])
        if has_reply:
            reply = (reply_refs[half][low], totals[half][inner : inner + 1])
        return q_ref[:, c], given, before, reply

    def store(h, m, l, acc):
        c = slice(h * HD, (h + 1) * HD)
        if last:
            out_hbm, out_ref, sems = refs
            out_ref[:, c] = (acc / l).astype(bf16).T
            if h % 2 == 1:
                n, pair = h // 2, slice((h - 1) * HD, (h + 1) * HD)
                copies.append(
                    pltpu.make_async_copy(out_ref.at[:, pair], out_hbm.at[:, pair], sems.at[n])
                )
                copies[-1].start()
        else:
            refs[0][c] = acc
            tops.append(m)
            sums.append(l)

    over_heads(H, load, store)
    for copy in copies:
        copy.wait()
    if not last:
        refs[1][...] = jnp.concatenate(tops + sums, axis=0)


def local(table, q, sources, before=None, reply=None, last=False):
    vmem = pl.BlockSpec(memory_space=pltpu.VMEM)
    plan = tuple(role for role, _ in sources)
    args = [table, q]
    for role, arrays in sources:
        args += list(arrays) if role == "pairs" else [arrays]
    args += list(before or ()) + list(reply or ())
    if last:
        out_specs = pl.BlockSpec(memory_space=pl.ANY)
        out_shape = jax.ShapeDtypeStruct((ROWS, W), bf16)
        scratch = [pltpu.VMEM((ROWS, W), bf16), pltpu.SemaphoreType.DMA((H // 2,))]
    else:
        scratch = []
        out_specs = [vmem, vmem]
        out_shape = [
            jax.ShapeDtypeStruct((W, ROWS), f32),
            jax.ShapeDtypeStruct((2 * H, ROWS), f32),
        ]
    return pl.pallas_call(
        functools.partial(local_kernel, plan, before is not None, reply is not None, last),
        in_specs=[pl.BlockSpec(memory_space=pltpu.SMEM)] + [vmem] * (len(args) - 1),
        out_specs=out_specs,
        out_shape=out_shape,
        scratch_shapes=scratch,
        compiler_params=pltpu.CompilerParams(vmem_limit_bytes=VMEM_LIMIT),
        cost_estimate=pl.CostEstimate(
            flops=4 * ROWS * ROWS * W, bytes_accessed=1024 * 1024, transcendentals=0
        ),
        name="local_" + "_".join(plan),
    )(*args)


def shards(q, k, v, links, counts):
    ranks = lax.axis_size("rank")
    across = lambda x, to: lax.ppermute(x, "rank", [(i, to(i) % ranks) for i in range(ranks)])
    in_hbm = lambda x: pltpu.with_memory_space_constraint(x, pltpu.HBM)
    core = lambda x: across(x, lambda i: i ^ 1)
    to_a = lambda x: lax.ppermute(x, "group", [(i, i ^ 1) for i in range(4)])
    to_b = lambda x: lax.ppermute(x, "group", [(i, 3 - i) for i in range(4)])

    kv, pay_a, pay_b, table = pack(links, counts, *(in_hbm(x) for x in (q, k, v)))
    got_a = to_a(pay_a)
    got_b = to_b(pay_b)
    first = across(kv, lambda i: i + 2 if i % 2 else i - 2)
    from_core = core(kv)
    state = local(table, q, [("own", kv), ("core", from_core)])

    first, state = lax.optimization_barrier((first, state))
    kv_later, first = lax.optimization_barrier((kv, first))
    second = across(kv_later, lambda i: i - 2 if i % 2 else i + 2)
    relay = core(first)

    got_a, got_b, _ = lax.optimization_barrier((got_a, got_b, kv_later))
    part_a = remote(got_a, kv, got_b, 1)
    back_a = to_a(part_a)
    part_b = remote(got_b, kv, got_a, 0)
    back_b = to_b(part_b)
    got_a, got_b, part_a, part_b = lax.optimization_barrier((got_a, got_b, part_a, part_b))
    middle = [("first", first), ("relay", relay), ("pairs", (got_a, got_b))]
    state = local(table, q, middle, state)
    second, state = lax.optimization_barrier((second, state))
    return local(table, q, [("second", second)], state, (back_b, back_a), True)


def solution(mesh):
    rows = P(("group", "rank"), None)
    return jax.shard_map(
        shards,
        mesh=mesh,
        in_specs=(rows, rows, rows, rows, P(("group", "rank"))),
        out_specs=rows,
        check_vma=False,
    )
```

time: 161 us -> 70.2 us (0.44)
  matrix products: 46.5 us -> 0 us
  local copies, waits for them, and re-layouts: 36.5 us -> 1.43 us
  Pallas kernels: 0 us -> 17.4 us
  between operations: 14.1 us -> 0.21 us
  other arithmetic: 13.7 us -> 0 us
  waiting for transfers between devices: 23.7 us -> 32.5 us
  starting transfers between devices: 25.7 us -> 18.1 us
    dot_general x16 -> x0, matrix products: 46.5 us -> none  [the longest x8 25.1 us: shards(): jnp.einsum('hqk,khd->qhd', rounded.reshape(H, rows_dev, rows_dev), source...]
    ppermute x8, waiting for transfers between devices: 4.62 us -> 32.5 us  [the longest x4 29 us: shards(): lax.ppermute(x, 'rank', [(i, to(i) % ranks) for i in range(ranks)])]
    all_gather x1 -> x0, waiting for transfers between devices: 19.1 us -> none  [side_by_side(): result, at, done = (lax.all_gather(both, axis, axis=dim, tiled=True), 0, [])]
    pallas_call x0 -> x6, Pallas kernels: none -> 17.4 us  [the longest x3 11.4 us: local(): pl.pallas_call(functools.partial(local_kernel, plan, before is not None,...]
    reduce_sum x3 -> x0, other arithmetic: 12.1 us -> none  [the longest x2 12 us: shards(): row_total = row_total + jnp.sum(weights * factor, axis=(3, 4))]
    unnamed x104 -> x6, local copies, waits for them, and re-layouts: 10.7 us -> 1.43 us
    ppermute x4 -> x0, local copies, waits for them, and re-layouts: 9.11 us -> none  [passed_along(): return lax.ppermute(block, axis, route)]
    ppermute x8, starting transfers between devices: 25.7 us -> 18.1 us  [the longest x4 13.2 us: shards(): lax.ppermute(x, 'rank', [(i, to(i) % ranks) for i in range(ranks)])]
  transfers between devices with their start and end apart: 9 -> 8, of which waited for: 2 -> 6; matrix products, arithmetic and copies ran while one was open for 27% -> 0% of each run, Pallas kernels for 0% -> 15%
where the time goes in v2:
time: 70.2 us; the launch traced here: 69.8 us
  waiting for transfers between devices  32.5 us (46%)
  starting transfers between devices  18.1 us (26%)
  Pallas kernels  17.4 us (25%)
  local copies, waits for them, and re-layouts  1.43 us (2%)
    ppermute x4, waiting for transfers between devices, shards(): lax.ppermute(x, 'rank', [(i, to(i) % ranks) for i in range(ranks)])  29 us
    ppermute x4, starting transfers between devices, shards(): lax.ppermute(x, 'rank', [(i, to(i) % ranks) for i in range(ranks)])  13.2 us
    pallas_call x3, Pallas kernels, local(): pl.pallas_call(functools.partial(local_kernel, plan, before is not None,...  11.4 us
    ppermute x2, starting transfers between devices, shards(): to_b = lambda x: lax.ppermute(x, 'group', [(i, 3 - i) for i in range(4)])  4.06 us
    pallas_call x1, Pallas kernels, pack(): pl.pallas_call(pack_kernel, in_specs=[smem, smem, hbm, hbm, hbm], out_spe...  3.02 us
    pallas_call x2, Pallas kernels, remote(): pl.pallas_call(functools.partial(remote_kernel, half), in_specs=[vmem] *...  3.01 us
    ppermute x2, waiting for transfers between devices, shards(): to_a = lambda x: lax.ppermute(x, 'group', [(i, i ^ 1) for i in range(4)])  1.87 us
    ppermute x2, waiting for transfers between devices, shards(): to_b = lambda x: lax.ppermute(x, 'group', [(i, 3 - i) for i in range(4)])  1.64 us
  transfers between devices with their start and end apart: 8, of which 6 were waited for; matrix products, arithmetic and copies ran while one was open for 0% of the time, Pallas kernels for 15%

profile of v2, /device:TPU:1, one launch (start us, length us, event | category | flops | bytes accessed | tf_op | source)
XLA Modules:
  0.0 69.8 jit_solution(14619683595667287004)
XLA Ops:
  0.0 0.0 copy-start
  0.0 0.0 copy-start.1
  0.0 0.8 %copy-done.1 = s32[2,8]{1,0:T(2,128)S(1)} copy-done((s32[2,8]{1,0:T(2,128)S(1)}, s32[2,8]{1,0:T(2,128)}, u32[]{:S(2)}) %copy-start.1) | copy-done | bytes 88
  0.8 0.0 copy-start.2
  0.8 0.7 copy-done.2
  1.4 3.0 %pack.1 = (bf16[512,2048]{1,0:T(8,128)(2,1)S(1)}, bf16[784,1024]{1,0:T(8,128)(2,1)S(1)}, bf16[784,1024]{1,0:T(8,128)(2,1)S(1)}, f32[2,16]{1,0:T(2,128)S(1)}) custom-call(s32[2,8]{1,0:T(2,128)S(1)} %copy-done.1, s32[2]{0:T(128)S(1)} %copy-done.2, bf16[256,2048]{1,0:T(8,128)(2,1)} %refs_1_.5, bf16[256,2048]{1,0:T(8,128)(2,1)} %k_hbm.1, bf16[256,2048]{1,0:T(8,128)(2,1)} %v_hbm.1), custom_call_target="tpu_custom_call" | custom-call | bytes 8388608 | tf_op jit(solution)/shard_map/pack/pallas_call | solution.py:132
  4.5 3.3 %collective-permute-start.1 = (bf16[512,2048]{1,0:T(8,128)(2,1)S(1)}, bf16[512,2048]{1,0:T(8,128)(2,1)S(1)}, u32[]{:S(2)}, u32[]{:S(2)}) collective-permute-start(bf16[512,2048]{1,0:T(8,128)(2,1)S(1)} %get-tuple-element.30.refs_2_.kv_ref), channel_id=1, source_target_pairs={{0,1},{1,0},{2,3},{3,2},{4,5},{5,4},{6,7},{7,6},{8,9},{9,8},{10,11... | collective-permute-start | bytes 6291464 | tf_op jit(solution)/shard_map/ppermute | solution.py:304
  7.8 0.0 collective-permute-start
  7.8 0.8 %collective-permute-start.4 = (bf16[784,1024]{1,0:T(8,128)(2,1)S(1)}, bf16[784,1024]{1,0:T(8,128)(2,1)S(1)}, u32[]{:S(2)}, u32[]{:S(2)}) collective-permute-start(bf16[784,1024]{1,0:T(8,128)(2,1)S(1)} %get-tuple-element.32), channel_id=1, source_target_pairs={{0,64},{64,0},{128,192},{192,128},{1,65},{65,1},{129,193},{193,129... | collective-permute-start | bytes 4816904 | tf_op jit(solution)/shard_map/ppermute | solution.py:307
  8.6 1.9 %collective-permute-start.5 = (bf16[784,1024]{1,0:T(8,128)(2,1)S(1)}, bf16[784,1024]{1,0:T(8,128)(2,1)S(1)}, u32[]{:S(2)}, u32[]{:S(2)}) collective-permute-start(bf16[784,1024]{1,0:T(8,128)(2,1)S(1)} %get-tuple-element.33), channel_id=1, source_target_pairs={{0,192},{64,128},{128,64},{192,0},{1,193},{65,129},{129,65},{193,1... | collective-permute-start | bytes 4816904 | tf_op jit(solution)/shard_map/ppermute | solution.py:308
  10.5 1.1 %collective-permute-done.1.refs_3_ = bf16[512,2048]{1,0:T(8,128)(2,1)S(1)} collective-permute-done((bf16[512,2048]{1,0:T(8,128)(2,1)S(1)}, bf16[512,2048]{1,0:T(8,128)(2,1)S(1)}, u32[]{:S(2)}, u32[]{:S(2)}) %collective-permute-start.1) | collective-permute-done | bytes 2097184 | tf_op jit(solution)/shard_map/ppermute | solution.py:304
  11.6 0.0 copy-done
  11.6 3.0 %local_own_core.1 = (f32[2048,256]{1,0:T(8,128)S(1)}, f32[32,256]{1,0:T(8,128)S(1)}) custom-call(f32[2,16]{1,0:T(2,128)S(1)} %get-tuple-element.25.refs_0_, bf16[256,2048]{1,0:T(8,128)(2,1)S(1)} %copy-done, bf16[512,2048]{1,0:T(8,128)(2,1)S(1)} %get-tuple-element.30.refs_2_.kv_ref, bf16[512,2048]{1,0:T(8,128)(2,1)S(1)} %collective-permute-done.1.refs_3_), custom_call_target="tpu_custom_call" | custom-call | flops 536870912 | bytes 1048576 | tf_op jit(solution)/shard_map/local_own_core/pallas_call | solution.py:288
  14.6 22.7 %collective-permute-done.refs_2_ = bf16[512,2048]{1,0:T(8,128)(2,1)S(1)} collective-permute-done((bf16[512,2048]{1,0:T(8,128)(2,1)S(1)}, bf16[512,2048]{1,0:T(8,128)(2,1)S(1)}, u32[]{:S(2)}, u32[]{:S(2)}) %collective-permute-start) | collective-permute-done | bytes 2097184 | tf_op jit(solution)/shard_map/ppermute | solution.py:304
  37.2 1.8 %collective-permute-start.2 = (bf16[512,2048]{1,0:T(8,128)(2,1)S(1)}, bf16[512,2048]{1,0:T(8,128)(2,1)S(1)}, u32[]{:S(2)}, u32[]{:S(2)}) collective-permute-start(bf16[512,2048]{1,0:T(8,128)(2,1)S(1)} %get-tuple-element.30.refs_2_.kv_ref), channel_id=1, source_target_pairs={{0,2},{1,63},{2,4},{3,1},{4,6},{5,3},{6,8},{7,5},{8,10},{9,7},{10,... | collective-permute-start | bytes 6291464 | tf_op jit(solution)/shard_map/ppermute | solution.py:304
  39.0 0.0 collective-permute-done.4.asked_ref.other_ref.refs_4_
  39.0 0.1 collective-permute-done.5.other_ref.asked_ref.refs_5_
  39.1 8.1 %collective-permute-start.3 = (bf16[512,2048]{1,0:T(8,128)(2,1)S(1)}, bf16[512,2048]{1,0:T(8,128)(2,1)S(1)}, u32[]{:S(2)}, u32[]{:S(2)}) collective-permute-start(bf16[512,2048]{1,0:T(8,128)(2,1)S(1)} %collective-permute-done.refs_2_), channel_id=1, source_target_pairs={{0,1},{1,0},{2,3},{3,2},{4,5},{5,4},{6,7},{7,6},{8,9},{9,8},{10,11... | collective-permute-start | bytes 6291464 | tf_op jit(solution)/shard_map/ppermute | solution.py:304
  47.3 1.5 %remote.3 = bf16[1056,256]{1,0:T(8,128)(2,1)S(1)} custom-call(bf16[784,1024]{1,0:T(8,128)(2,1)S(1)} %collective-permute-done.5.other_ref.asked_ref.refs_5_, bf16[512,2048]{1,0:T(8,128)(2,1)S(1)} %get-tuple-element.30.refs_2_.kv_ref, bf16[784,1024]{1,0:T(8,128)(2,1)S(1)} %collective-permute-done.4.asked_ref.other_ref.refs_4_), custom_call_target="tpu_custom_call" | custom-call | flops 53687091200 | bytes 1048576 | tf_op jit(solution)/shard_map/remote/pallas_call | solution.py:182
  48.8 1.5 %remote.2 = bf16[1056,256]{1,0:T(8,128)(2,1)S(1)} custom-call(bf16[784,1024]{1,0:T(8,128)(2,1)S(1)} %collective-permute-done.4.asked_ref.other_ref.refs_4_, bf16[512,2048]{1,0:T(8,128)(2,1)S(1)} %get-tuple-element.30.refs_2_.kv_ref, bf16[784,1024]{1,0:T(8,128)(2,1)S(1)} %collective-permute-done.5.other_ref.asked_ref.refs_5_), custom_call_target="tpu_custom_call" | custom-call | flops 53687091200 | bytes 1048576 | tf_op jit(solution)/shard_map/remote/pallas_call | solution.py:182
  50.3 0.1 collective-permute-start.7
  50.4 2.2 %collective-permute-start.6 = (bf16[1056,256]{1,0:T(8,128)(2,1)S(1)}, bf16[1056,256]{1,0:T(8,128)(2,1)S(1)}, u32[]{:S(2)}, u32[]{:S(2)}) collective-permute-start(bf16[1056,256]{1,0:T(8,128)(2,1)S(1)} %remote.3), channel_id=1, source_target_pairs={{0,192},{64,128},{128,64},{192,0},{1,193},{65,129},{129,65},{193,1... | collective-permute-start | bytes 1622024 | tf_op jit(solution)/shard_map/ppermute | solution.py:308
  52.6 0.0 collective-permute-done.3.refs_3_
  52.6 4.6 %local_first_relay_pairs.1 = (f32[2048,256]{1,0:T(8,128)S(1)}, f32[32,256]{1,0:T(8,128)S(1)}) custom-call(f32[2,16]{1,0:T(2,128)S(1)} %get-tuple-element.25.refs_0_, bf16[256,2048]{1,0:T(8,128)(2,1)S(1)} %copy-done, bf16[512,2048]{1,0:T(8,128)(2,1)S(1)} %collective-permute-done.refs_2_, bf16[512,2048]{1,0:T(8,128)(2,1)S(1)} %collective-permute-done.3.refs_3_, ...), custom_call_target="tpu_custom_call" | custom-call | flops 536870912 | bytes 1048576 | tf_op jit(solution)/shard_map/local_first_relay_pairs/pallas_call | solution.py:288
  57.2 5.2 %collective-permute-done.2.refs_2_ = bf16[512,2048]{1,0:T(8,128)(2,1)S(1)} collective-permute-done((bf16[512,2048]{1,0:T(8,128)(2,1)S(1)}, bf16[512,2048]{1,0:T(8,128)(2,1)S(1)}, u32[]{:S(2)}, u32[]{:S(2)}) %collective-permute-start.2) | collective-permute-done | bytes 2097184 | tf_op jit(solution)/shard_map/ppermute | solution.py:304
  62.4 1.9 %collective-permute-done.7.refs_6_ = bf16[1056,256]{1,0:T(8,128)(2,1)S(1)} collective-permute-done((bf16[1056,256]{1,0:T(8,128)(2,1)S(1)}, bf16[1056,256]{1,0:T(8,128)(2,1)S(1)}, u32[]{:S(2)}, u32[]{:S(2)}) %collective-permute-start.7) | collective-permute-done | bytes 540704 | tf_op jit(solution)/shard_map/ppermute | solution.py:307
  64.3 1.5 %collective-permute-done.6.refs_5_ = bf16[1056,256]{1,0:T(8,128)(2,1)S(1)} collective-permute-done((bf16[1056,256]{1,0:T(8,128)(2,1)S(1)}, bf16[1056,256]{1,0:T(8,128)(2,1)S(1)}, u32[]{:S(2)}, u32[]{:S(2)}) %collective-permute-start.6) | collective-permute-done | bytes 540704 | tf_op jit(solution)/shard_map/ppermute | solution.py:308
  65.8 3.8 %local_second.1 = bf16[256,2048]{1,0:T(8,128)(2,1)} custom-call(f32[2,16]{1,0:T(2,128)S(1)} %get-tuple-element.25.refs_0_, bf16[256,2048]{1,0:T(8,128)(2,1)S(1)} %copy-done, bf16[512,2048]{1,0:T(8,128)(2,1)S(1)} %collective-permute-done.2.refs_2_, f32[2048,256]{1,0:T(8,128)S(1)} %get-tuple-element.43.refs_3_, f32[32,256]{1,0:T(8,128)S(1)} %get-tuple-element.44.refs_4_, ...), custom_call_target="tpu_custom_call" | custom-call | flops 536870912 | bytes 1048576 | tf_op jit(solution)/shard_map/local_second/pallas_call | solution.py:288
Async XLA Ops:
  0.0 11.6 %copy-start = (bf16[256,2048]{1,0:T(8,128)(2,1)S(1)}, bf16[256,2048]{1,0:T(8,128)(2,1)}, u32[]{:S(2)}) copy-start(bf16[256,2048]{1,0:T(8,128)(2,1)} %refs_1_.5) | copy-start | bytes 3145732
  0.0 0.8 %copy-start.1 = (s32[2,8]{1,0:T(2,128)S(1)}, s32[2,8]{1,0:T(2,128)}, u32[]{:S(2)}) copy-start(s32[2,8]{1,0:T(2,128)} %links_ref.1) | copy-start | bytes 196
  0.8 0.7 copy-start.2
  4.5 7.1 %collective-permute-start.1 = (bf16[512,2048]{1,0:T(8,128)(2,1)S(1)}, bf16[512,2048]{1,0:T(8,128)(2,1)S(1)}, u32[]{:S(2)}, u32[]{:S(2)}) collective-permute-start(bf16[512,2048]{1,0:T(8,128)(2,1)S(1)} %get-tuple-element.30.refs_2_.kv_ref), channel_id=1, source_target_pairs={{0,1},{1,0},{2,3},{3,2},{4,5},{5,4},{6,7},{7,6},{8,9},{9,8},{10,11... | collective-permute-start | bytes 6291464 | tf_op jit(solution)/shard_map/ppermute | solution.py:304
  7.8 29.5 %collective-permute-start = (bf16[512,2048]{1,0:T(8,128)(2,1)S(1)}, bf16[512,2048]{1,0:T(8,128)(2,1)S(1)}, u32[]{:S(2)}, u32[]{:S(2)}) collective-permute-start(bf16[512,2048]{1,0:T(8,128)(2,1)S(1)} %get-tuple-element.30.refs_2_.kv_ref), channel_id=1, source_target_pairs={{0,62},{1,3},{2,0},{3,5},{4,2},{5,7},{6,4},{7,9},{8,6},{9,11},{10,... | collective-permute-start | bytes 6291464 | tf_op jit(solution)/shard_map/ppermute | solution.py:304
  7.8 31.2 %collective-permute-start.4 = (bf16[784,1024]{1,0:T(8,128)(2,1)S(1)}, bf16[784,1024]{1,0:T(8,128)(2,1)S(1)}, u32[]{:S(2)}, u32[]{:S(2)}) collective-permute-start(bf16[784,1024]{1,0:T(8,128)(2,1)S(1)} %get-tuple-element.32), channel_id=1, source_target_pairs={{0,64},{64,0},{128,192},{192,128},{1,65},{65,1},{129,193},{193,129... | collective-permute-start | bytes 4816904 | tf_op jit(solution)/shard_map/ppermute | solution.py:307
  8.6 30.6 %collective-permute-start.5 = (bf16[784,1024]{1,0:T(8,128)(2,1)S(1)}, bf16[784,1024]{1,0:T(8,128)(2,1)S(1)}, u32[]{:S(2)}, u32[]{:S(2)}) collective-permute-start(bf16[784,1024]{1,0:T(8,128)(2,1)S(1)} %get-tuple-element.33), channel_id=1, source_target_pairs={{0,192},{64,128},{128,64},{192,0},{1,193},{65,129},{129,65},{193,1... | collective-permute-start | bytes 4816904 | tf_op jit(solution)/shard_map/ppermute | solution.py:308
  37.2 25.2 %collective-permute-start.2 = (bf16[512,2048]{1,0:T(8,128)(2,1)S(1)}, bf16[512,2048]{1,0:T(8,128)(2,1)S(1)}, u32[]{:S(2)}, u32[]{:S(2)}) collective-permute-start(bf16[512,2048]{1,0:T(8,128)(2,1)S(1)} %get-tuple-element.30.refs_2_.kv_ref), channel_id=1, source_target_pairs={{0,2},{1,63},{2,4},{3,1},{4,6},{5,3},{6,8},{7,5},{8,10},{9,7},{10,... | collective-permute-start | bytes 6291464 | tf_op jit(solution)/shard_map/ppermute | solution.py:304
  39.1 13.4 %collective-permute-start.3 = (bf16[512,2048]{1,0:T(8,128)(2,1)S(1)}, bf16[512,2048]{1,0:T(8,128)(2,1)S(1)}, u32[]{:S(2)}, u32[]{:S(2)}) collective-permute-start(bf16[512,2048]{1,0:T(8,128)(2,1)S(1)} %collective-permute-done.refs_2_), channel_id=1, source_target_pairs={{0,1},{1,0},{2,3},{3,2},{4,5},{5,4},{6,7},{7,6},{8,9},{9,8},{10,11... | collective-permute-start | bytes 6291464 | tf_op jit(solution)/shard_map/ppermute | solution.py:304
  50.3 14.0 %collective-permute-start.7 = (bf16[1056,256]{1,0:T(8,128)(2,1)S(1)}, bf16[1056,256]{1,0:T(8,128)(2,1)S(1)}, u32[]{:S(2)}, u32[]{:S(2)}) collective-permute-start(bf16[1056,256]{1,0:T(8,128)(2,1)S(1)} %remote.2), channel_id=1, source_target_pairs={{0,64},{64,0},{128,192},{192,128},{1,65},{65,1},{129,193},{193,129... | collective-permute-start | bytes 1622024 | tf_op jit(solution)/shard_map/ppermute | solution.py:307
  50.4 15.4 %collective-permute-start.6 = (bf16[1056,256]{1,0:T(8,128)(2,1)S(1)}, bf16[1056,256]{1,0:T(8,128)(2,1)S(1)}, u32[]{:S(2)}, u32[]{:S(2)}) collective-permute-start(bf16[1056,256]{1,0:T(8,128)(2,1)S(1)} %remote.3), channel_id=1, source_target_pairs={{0,192},{64,128},{128,64},{192,0},{1,193},{65,129},{129,65},{193,1... | collective-permute-start | bytes 1622024 | tf_op jit(solution)/shard_map/ppermute | solution.py:308

commit v3 on v2

v3 whole, which is shorter than its diff:
```python
import functools
import math

import jax
import jax.numpy as jnp
from jax import lax
from jax.experimental import pallas as pl
from jax.experimental.pallas import tpu as pltpu
from jax.sharding import PartitionSpec as P

H = 16
HD = 128
LMAX = 8
TILE = 128
ROWS = 256
W = 2048
HALF = W // 2
NEG = -1e30
SCALE = math.log2(math.e) / math.sqrt(HD)
PARTS = 2
PH = H // 2 // PARTS
PW = PH * HD
PAYLOAD = 3 * ROWS + 16
REPLY = PW + 16
SPLIT = 4
VMEM_LIMIT = 20 * 1024 * 1024
REMOTE_COST = 200

f32 = jnp.float32
bf16 = jnp.bfloat16


def log_multiplicity(links_ref, counts_ref, i, cand, own):
    times = jnp.int32(1 if own else 0)
    for s in range(LMAX):
        hit = (links_ref[i, s] == cand) & (s < counts_ref[i])
        times = times + hit.astype(jnp.int32)
    return jnp.where(times == 0, NEG, jnp.where(times == 1, 0.0, 1.0)).astype(f32)


def score(q, sources):
    raw, tops = [], []
    for k, _, bias in sources:
        s = lax.dot_general(k, q, (((1,), (1,)), ((), ())), preferred_element_type=f32)
        for j in range(2):
            block = s[j * TILE : (j + 1) * TILE]
            raw.append((block, bias[j]))
            tops.append(jnp.max(block, axis=0, keepdims=True) * SCALE + bias[j])
    return raw, tops


def weigh(scored, before=None, reply=None):
    raw, tops = scored
    if before is not None:
        tops = tops + [before[0]]
    if reply is not None:
        tops = tops + [reply[1]]
    m = functools.reduce(jnp.maximum, tops)
    p = [jnp.exp2(block * SCALE + (bias - m)).astype(bf16) for block, bias in raw]
    return m, jnp.concatenate(p, axis=0)


def mix(weighed, sources, before=None, reply=None):
    m, p = weighed
    values = jnp.concatenate([v.T for _, v, _ in sources], axis=1)
    values = jnp.concatenate([values, jnp.ones((16, values.shape[1]), bf16)], axis=0)
    both = jnp.dot(values, p, preferred_element_type=f32)
    acc, l = both[:HD], both[HD : HD + 1]
    if before is not None:
        a = jnp.exp2(before[0] - m)
        acc = acc + before[2] * a
        l = l + before[1] * a
    if reply is not None:
        a = jnp.exp2(reply[1] - m)
        acc = acc + reply[0].astype(f32) * a
        l = l + a
    return m, l, acc


def over_heads(heads, load, store):
    held, scored, weighed = {}, {}, {}
    for t in range(heads + 2):
        if t < heads:
            held[t] = load(t)
            scored[t] = score(*held[t][:2])
        if 0 <= t - 1 < heads:
            weighed[t - 1] = weigh(scored.pop(t - 1), *held[t - 1][2:])
        if t >= 2:
            _, sources, before, reply = held.pop(t - 2)
            store(t - 2, *mix(weighed.pop(t - 2), sources, before, reply))


def payload_heads(way, part):
    return way * HALF + part * PW, (1 - way) * HALF + part * PW


def pack_kernel(links_hbm, counts_hbm, q_hbm, k_hbm, v_hbm, kv_ref, *refs):
    pay_refs, table_ref = refs[: 2 * PARTS], refs[2 * PARTS]
    links_ref, counts_ref, small_sems, sems = refs[2 * PARTS + 1 :]
    small = [
        pltpu.make_async_copy(links_hbm, links_ref, small_sems.at[0]),
        pltpu.make_async_copy(counts_hbm, counts_ref, small_sems.at[1]),
    ]
    for copy in small:
        copy.start()
    copies = []

    def begin(src, dst):
        copies.append(pltpu.make_async_copy(src, dst, sems.at[len(copies)]))
        copies[-1].start()

    step = ROWS // SPLIT
    for n, hbm in enumerate((k_hbm, v_hbm)):
        for i in range(SPLIT):
            begin(hbm.at[pl.ds(i * step, step)], kv_ref.at[pl.ds(n * ROWS + i * step, step)])
    for n, ref in enumerate(pay_refs):
        column = payload_heads(n // PARTS, n % PARTS)[1]
        begin(q_hbm.at[:, pl.ds(column, PW)], ref.at[pl.ds(2 * ROWS, ROWS)])
    for copy in small:
        copy.wait()
    bias = [
        [log_multiplicity(links_ref, counts_ref, i, c, c == i) for i in range(2)]
        for c in range(16)
    ]
    lane = lax.broadcasted_iota(jnp.int32, (16, ROWS), 1)
    row = lax.broadcasted_iota(jnp.int32, (16, ROWS), 0)
    table = jnp.zeros((16, ROWS), f32)
    for c in range(16):
        table = jnp.where(row == c, jnp.where(lane < TILE, bias[c][0], bias[c][1]), table)
    table_ref[...] = table
    even = (lax.axis_index("group") % 2) == 0
    row = lax.broadcasted_iota(jnp.int32, (16, 128), 0)
    for way in range(2):
        extra = jnp.zeros((16, 128), f32)
        for i in range(2):
            for j in range(2):
                one, three = bias[10 + j][i], bias[14 + j][i]
                near = jnp.where(even, one, three) if way == 0 else jnp.where(even, three, one)
                extra = jnp.where(row == 4 * i + j, near, extra)
                extra = jnp.where(row == 4 * i + 2 + j, bias[12 + j][i], extra)
        for ref in pay_refs[way * PARTS : (way + 1) * PARTS]:
            ref[3 * ROWS :, 0:128] = extra.astype(bf16)
            ref[3 * ROWS :, 128:] = jnp.zeros((16, PW - 128), bf16)
    for part in range(2 * SPLIT):
        copies[part].wait()
        rows = slice(part * step, (part + 1) * step)
        for n, ref in enumerate(pay_refs):
            column = payload_heads(n // PARTS, n % PARTS)[0]
            ref[rows] = kv_ref[rows, column : column + PW]
    for copy in copies[2 * SPLIT :]:
        copy.wait()


def pack(links, counts, q, k, v):
    vmem = pl.BlockSpec(memory_space=pltpu.VMEM)
    hbm = pl.BlockSpec(memory_space=pltpu.HBM)
    args = [pltpu.with_memory_space_constraint(x, pltpu.HBM) for x in (links, counts, q, k, v)]
    out = pl.pallas_call(
        pack_kernel,
        in_specs=[hbm] * 5,
        out_specs=[vmem] * (2 + 2 * PARTS),
        out_shape=[jax.ShapeDtypeStruct((2 * ROWS, W), bf16)]
        + [jax.ShapeDtypeStruct((PAYLOAD, PW), bf16)] * (2 * PARTS)
        + [jax.ShapeDtypeStruct((16, ROWS), f32)],
        scratch_shapes=[
            pltpu.SMEM((2, LMAX), jnp.int32),
            pltpu.SMEM((2,), jnp.int32),
            pltpu.SemaphoreType.DMA((2,)),
            pltpu.SemaphoreType.DMA((2 * SPLIT + 2 * PARTS,)),
        ],
        compiler_params=pltpu.CompilerParams(vmem_limit_bytes=VMEM_LIMIT),
        cost_estimate=pl.CostEstimate(flops=0, bytes_accessed=8 * 1024 * 1024, transcendentals=0),
        name="pack",
    )(*args)
    return out[0], out[1 : 1 + PARTS], out[1 + PARTS : 1 + 2 * PARTS], out[-1]


def remote_kernel(part, kv_ref, a_ref, b_ref, out_a, out_b):
    asked, other, outs = (a_ref, b_ref), (b_ref, a_ref), (out_a, out_b)
    bias, stats = [], []
    for way in range(2):
        extra = asked[way][3 * ROWS :, 0:128].astype(f32)
        bias.append(
            [jnp.concatenate([extra[n : n + 1], extra[4 + n : 5 + n]], axis=1) for n in range(4)]
        )
        stats.append([[], [], []])

    def load(h):
        way, inner = h // PH, h % PH
        c = slice(inner * HD, (inner + 1) * HD)
        first = payload_heads(way, part)[1] + inner * HD
        own = slice(first, first + HD)
        sources = [
            (kv_ref[0:ROWS, own], kv_ref[ROWS:, own], bias[way][0:2]),
            (other[way][0:ROWS, c], other[way][ROWS : 2 * ROWS, c], bias[way][2:4]),
        ]
        return asked[way][2 * ROWS : 3 * ROWS, c], sources, None, None

    def store(h, m, l, acc):
        way, inner = h // PH, h % PH
        outs[way][inner * HD : (inner + 1) * HD] = (acc / l).astype(bf16)
        total = m + jnp.log2(l)
        high = total.astype(bf16).astype(f32)
        rest = total - high
        middle = rest.astype(bf16).astype(f32)
        for rows, piece in zip(stats[way], (high, middle, rest - middle)):
            rows.append(piece)

    over_heads(2 * PH, load, store)
    for way in range(2):
        rows = stats[way][0] + stats[way][1] + stats[way][2]
        rows += [jnp.zeros((1, ROWS), f32)] * (16 - len(rows))
        outs[way][PW:] = jnp.concatenate(rows, axis=0).astype(bf16)


def remote(kv, a, b, part):
    vmem = pl.BlockSpec(memory_space=pltpu.VMEM)
    return pl.pallas_call(
        functools.partial(remote_kernel, part),
        in_specs=[vmem] * 3,
        out_specs=[vmem] * 2,
        out_shape=[jax.ShapeDtypeStruct((REPLY, ROWS), bf16)] * 2,
        compiler_params=pltpu.CompilerParams(vmem_limit_bytes=VMEM_LIMIT),
        cost_estimate=pl.CostEstimate(
            flops=REMOTE_COST * ROWS * ROWS * HALF, bytes_accessed=1024 * 1024, transcendentals=0
        ),
        name=f"remote_{part}",
    )(kv, a, b)


def local_kernel(plan, has_before, has_reply, last, *refs):
    refs = list(refs)
    table_ref, q_ref = refs.pop(0), refs.pop(0)
    odd_core = (lax.axis_index("rank") % 2) == 1
    odd_group = (lax.axis_index("group") % 2) == 1
    sources = []
    for role in plan:
        if role == "pairs":
            arrays = [refs.pop(0) for _ in range(2 * PARTS)]
            blocks = (jnp.where(odd_group, 7, 5), jnp.where(odd_group, 5, 7))
        else:
            arrays = refs.pop(0)
            block = {
                "own": 0,
                "core": jnp.where(odd_core, 2, 3),
                "relay": jnp.where(odd_core, 3, 2),
                "first": jnp.where(odd_core, 1, 4),
                "second": jnp.where(odd_core, 4, 1),
            }[role]
            blocks = (block, block)
        bias = [
            [table_ref[pl.ds(block * 2 + j, 1), :] for j in range(2)] for block in blocks
        ]
        sources.append((role, arrays, bias))
    if has_before:
        acc_in, ml_in = refs.pop(0), refs.pop(0)
    if has_reply:
        reply_refs = [refs.pop(0) for _ in range(2 * PARTS)]
        totals = []
        for ref in reply_refs:
            tail = ref[PW:].astype(f32)
            totals.append(tail[0:PH] + tail[PH : 2 * PH] + tail[2 * PH : 3 * PH])
    tops, sums, copies = [], [], []

    def load(h):
        piece, inner = h // PH, h % PH
        half = h // (H // 2)
        c = slice(h * HD, (h + 1) * HD)
        low = slice(inner * HD, (inner + 1) * HD)
        given = []
        for role, arrays, bias in sources:
            array, at = (arrays[piece], low) if role == "pairs" else (arrays, c)
            given.append((array[0:ROWS, at], array[ROWS : 2 * ROWS, at], bias[half]))
        before = reply = None
        if has_before:
            before = (ml_in[h : h + 1], ml_in[H + h : H + h + 1], acc_in[c])
        if has_reply:
            reply = (reply_refs[piece][low], totals[piece][inner : inner + 1])
        return q_ref[:, c], given, before, reply

    def store(h, m, l, acc):
        c = slice(h * HD, (h + 1) * HD)
        if last:
            out_hbm, out_ref, sems = refs
            out_ref[:, c] = (acc / l).astype(bf16).T
            if h % 2 == 1:
                n, pair = h // 2, slice((h - 1) * HD, (h + 1) * HD)
                copies.append(
                    pltpu.make_async_copy(out_ref.at[:, pair], out_hbm.at[:, pair], sems.at[n])
                )
                copies[-1].start()
        else:
            refs[0][c] = acc
            tops.append(m)
            sums.append(l)

    over_heads(H, load, store)
    for copy in copies:
        copy.wait()
    if not last:
        refs[1][...] = jnp.concatenate(tops + sums, axis=0)


def local(table, q, sources, before=None, reply=None, last=False):
    vmem = pl.BlockSpec(memory_space=pltpu.VMEM)
    plan = tuple(role for role, _ in sources)
    args = [table, q]
    for role, arrays in sources:
        args += list(arrays) if role == "pairs" else [arrays]
    args += list(before or ()) + list(reply or ())
    if last:
        out_specs = pl.BlockSpec(memory_space=pl.ANY)
        out_shape = jax.ShapeDtypeStruct((ROWS, W), bf16)
        scratch = [pltpu.VMEM((ROWS, W), bf16), pltpu.SemaphoreType.DMA((H // 2,))]
    else:
        scratch = []
        out_specs = [vmem, vmem]
        out_shape = [
            jax.ShapeDtypeStruct((W, ROWS), f32),
            jax.ShapeDtypeStruct((2 * H, ROWS), f32),
        ]
    return pl.pallas_call(
        functools.partial(local_kernel, plan, before is not None, reply is not None, last),
        in_specs=[vmem] * len(args),
        out_specs=out_specs,
        out_shape=out_shape,
        scratch_shapes=scratch,
        compiler_params=pltpu.CompilerParams(vmem_limit_bytes=VMEM_LIMIT),
        cost_estimate=pl.CostEstimate(
            flops=4 * ROWS * ROWS * W, bytes_accessed=1024 * 1024, transcendentals=0
        ),
        name="local_" + "_".join(plan),
    )(*args)


def shards(q, k, v, links, counts):
    ranks = lax.axis_size("rank")
    across = lambda x, to: lax.ppermute(x, "rank", [(i, to(i) % ranks) for i in range(ranks)])
    core = lambda x: across(x, lambda i: i ^ 1)
    to_a = lambda x: lax.ppermute(x, "group", [(i, i ^ 1) for i in range(4)])
    to_b = lambda x: lax.ppermute(x, "group", [(i, 3 - i) for i in range(4)])

    kv, pay_a, pay_b, table = pack(links, counts, q, k, v)
    first = across(kv, lambda i: i + 2 if i % 2 else i - 2)
    from_core = core(kv)
    got_a = [to_a(x) for x in pay_a]
    got_b = [to_b(x) for x in pay_b]
    state = local(table, q, [("own", kv), ("core", from_core)])

    back_a, back_b = [None] * PARTS, [None] * PARTS
    got_a[0], got_b[0], state = lax.optimization_barrier((got_a[0], got_b[0], state))
    kv_later, got_a[0], got_b[0] = lax.optimization_barrier((kv, got_a[0], got_b[0]))
    second = across(kv_later, lambda i: i - 2 if i % 2 else i + 2)
    part_a, part_b = remote(kv, got_a[0], got_b[0], 0)
    back_a[0], back_b[0] = to_a(part_a), to_b(part_b)

    first, part_a = lax.optimization_barrier((first, part_a))
    relay = core(first)
    got_a[1], got_b[1], first = lax.optimization_barrier((got_a[1], got_b[1], first))
    part_a, part_b = remote(kv, got_a[1], got_b[1], 1)
    back_a[1], back_b[1] = to_a(part_a), to_b(part_b)

    state, part_a, back_a[0], back_b[0] = lax.optimization_barrier((state, part_a, back_a[0], back_b[0]))
    state = local(table, q, [("first", first), ("pairs", got_a + got_b)], state)
    second, state = lax.optimization_barrier((second, state))
    return local(table, q, [("second", second), ("relay", relay)], state, back_b + back_a, True)


def solution(mesh):
    rows = P(("group", "rank"), None)
    return jax.shard_map(
        shards,
        mesh=mesh,
        in_specs=(rows, rows, rows, rows, P(("group", "rank"))),
        out_specs=rows,
        check_vma=False,
    )
```

time: 70.2 us -> 66.4 us (0.946)
  the two profiles are of different devices: /device:TPU:1 before, /device:TPU:24 now
where the time goes in v3:
time: 66.4 us; the launch traced here: 66.3 us
  waiting for transfers between devices  35 us (53%)
  starting transfers between devices  17.7 us (27%)
  Pallas kernels  13.4 us (20%)
    ppermute x4, waiting for transfers between devices, shards(): to_a = lambda x: lax.ppermute(x, 'group', [(i, i ^ 1) for i in range(4)])  17 us
    ppermute x4, waiting for transfers between devices, shards(): lax.ppermute(x, 'rank', [(i, to(i) % ranks) for i in range(ranks)])  11.1 us
    pallas_call x3, Pallas kernels, local(): pl.pallas_call(functools.partial(local_kernel, plan, before is not None,...  8.55 us
    ppermute x4, starting transfers between devices, shards(): lax.ppermute(x, 'rank', [(i, to(i) % ranks) for i in range(ranks)])  8.22 us
    ppermute x4, starting transfers between devices, shards(): to_b = lambda x: lax.ppermute(x, 'group', [(i, 3 - i) for i in range(4)])  7.01 us
    ppermute x4, waiting for transfers between devices, shards(): to_b = lambda x: lax.ppermute(x, 'group', [(i, 3 - i) for i in range(4)])  6.81 us
    pallas_call x2, Pallas kernels, remote(): pl.pallas_call(functools.partial(remote_kernel, part), in_specs=[vmem] *...  2.83 us
    ppermute x4, starting transfers between devices, shards(): to_a = lambda x: lax.ppermute(x, 'group', [(i, i ^ 1) for i in range(4)])  2.46 us
  transfers between devices with their start and end apart: 12, of which 7 were waited for; matrix products, arithmetic and copies ran while one was open for 0% of the time, Pallas kernels for 12%

profile of v3, /device:TPU:24, one launch (start us, length us, event | category | flops | bytes accessed | tf_op | source)
XLA Modules:
  0.0 66.3 jit_solution(4301184828092299936)
XLA Ops:
  0.0 0.0 copy-start
  0.0 2.0 %pack.1 = (bf16[512,2048]{1,0:T(8,128)(2,1)S(1)}, bf16[784,512]{1,0:T(8,128)(2,1)S(1)}, bf16[784,512]{1,0:T(8,128)(2,1)S(1)}, bf16[784,512]{1,0:T(8,128)(2,1)S(1...) custom-call(s32[2,8]{1,0:T(2,128)} %links_hbm.1, s32[2]{0:T(128)} %counts_hbm.1, bf16[256,2048]{1,0:T(8,128)(2,1)} %refs_1_.5, ...), custom_call_target="tpu_custom_call" | custom-call | bytes 8388608 | tf_op jit(solution)/shard_map/pack/pallas_call | solution.py:158
  2.0 0.1 collective-permute-start.2
  2.1 8.1 %collective-permute-start.6 = (bf16[512,2048]{1,0:T(8,128)(2,1)S(1)}, bf16[512,2048]{1,0:T(8,128)(2,1)S(1)}, u32[]{:S(2)}, u32[]{:S(2)}) collective-permute-start(bf16[512,2048]{1,0:T(8,128)(2,1)S(1)} %get-tuple-element.45.refs_2_.kv_ref), channel_id=1, source_target_pairs={{0,62},{1,3},{2,0},{3,5},{4,2},{5,7},{6,4},{7,9},{8,6},{9,11},{10,... | collective-permute-start | bytes 6291464 | tf_op jit(solution)/shard_map/ppermute | solution.py:338
  10.3 0.7 %collective-permute-start = (bf16[784,512]{1,0:T(8,128)(2,1)S(1)}, bf16[784,512]{1,0:T(8,128)(2,1)S(1)}, u32[]{:S(2)}, u32[]{:S(2)}) collective-permute-start(bf16[784,512]{1,0:T(8,128)(2,1)S(1)} %get-tuple-element.39), channel_id=1, source_target_pairs={{0,64},{64,0},{128,192},{192,128},{1,65},{65,1},{129,193},{193,129... | collective-permute-start | bytes 2408456 | tf_op jit(solution)/shard_map/ppermute | solution.py:340
  11.0 1.1 %collective-permute-start.1 = (bf16[784,512]{1,0:T(8,128)(2,1)S(1)}, bf16[784,512]{1,0:T(8,128)(2,1)S(1)}, u32[]{:S(2)}, u32[]{:S(2)}) collective-permute-start(bf16[784,512]{1,0:T(8,128)(2,1)S(1)} %get-tuple-element.40), channel_id=1, source_target_pairs={{0,192},{64,128},{128,64},{192,0},{1,193},{65,129},{129,65},{193,1... | collective-permute-start | bytes 2408456 | tf_op jit(solution)/shard_map/ppermute | solution.py:341
  12.1 0.2 collective-permute-start.4
  12.3 0.0 collective-permute-done.2.refs_3_
  12.3 2.6 %collective-permute-start.5 = (bf16[784,512]{1,0:T(8,128)(2,1)S(1)}, bf16[784,512]{1,0:T(8,128)(2,1)S(1)}, u32[]{:S(2)}, u32[]{:S(2)}) collective-permute-start(bf16[784,512]{1,0:T(8,128)(2,1)S(1)} %get-tuple-element.47), channel_id=1, source_target_pairs={{0,192},{64,128},{128,64},{192,0},{1,193},{65,129},{129,65},{193,1... | collective-permute-start | bytes 2408456 | tf_op jit(solution)/shard_map/ppermute | solution.py:341
  14.9 0.0 copy-done
  14.9 2.4 %local_own_core.1 = (f32[2048,256]{1,0:T(8,128)S(1)}, f32[32,256]{1,0:T(8,128)S(1)}) custom-call(f32[16,256]{1,0:T(8,128)S(1)} %get-tuple-element.37.refs_0_, bf16[256,2048]{1,0:T(8,128)(2,1)S(1)} %copy-done, bf16[512,2048]{1,0:T(8,128)(2,1)S(1)} %get-tuple-element.45.refs_2_.kv_ref, bf16[512,2048]{1,0:T(8,128)(2,1)S(1)} %collective-permute-done.2.refs_3_), custom_call_target="tpu_custom_call" | custom-call | flops 536870912 | bytes 1048576 | tf_op jit(solution)/shard_map/local_own_core/pallas_call | solution.py:322
  17.4 13.7 %collective-permute-done.a_ref.refs_3_ = bf16[784,512]{1,0:T(8,128)(2,1)S(1)} collective-permute-done((bf16[784,512]{1,0:T(8,128)(2,1)S(1)}, bf16[784,512]{1,0:T(8,128)(2,1)S(1)}, u32[]{:S(2)}, u32[]{:S(2)}) %collective-permute-start) | collective-permute-done | bytes 802848 | tf_op jit(solution)/shard_map/ppermute | solution.py:340
  31.1 2.0 %collective-permute-done.1.b_ref.refs_5_ = bf16[784,512]{1,0:T(8,128)(2,1)S(1)} collective-permute-done((bf16[784,512]{1,0:T(8,128)(2,1)S(1)}, bf16[784,512]{1,0:T(8,128)(2,1)S(1)}, u32[]{:S(2)}, u32[]{:S(2)}) %collective-permute-start.1) | collective-permute-done | bytes 802848 | tf_op jit(solution)/shard_map/ppermute | solution.py:341
  33.1 0.0 collective-permute-start.3
  33.1 1.4 %remote_0.1 = (bf16[528,256]{1,0:T(8,128)(2,1)S(1)}, bf16[528,256]{1,0:T(8,128)(2,1)S(1)}) custom-call(bf16[512,2048]{1,0:T(8,128)(2,1)S(1)} %get-tuple-element.45.refs_2_.kv_ref, bf16[784,512]{1,0:T(8,128)(2,1)S(1)} %collective-permute-done.a_ref.refs_3_, bf16[784,512]{1,0:T(8,128)(2,1)S(1)} %collective-permute-done.1.b_ref.refs_5_), custom_call_target="tpu_custom_call" | custom-call | flops 13421772800 | bytes 1048576 | tf_op jit(solution)/shard_map/remote_0/pallas_call | solution.py:218
  34.5 2.4 %collective-permute-done.6.refs_2_ = bf16[512,2048]{1,0:T(8,128)(2,1)S(1)} collective-permute-done((bf16[512,2048]{1,0:T(8,128)(2,1)S(1)}, bf16[512,2048]{1,0:T(8,128)(2,1)S(1)}, u32[]{:S(2)}, u32[]{:S(2)}) %collective-permute-start.6) | collective-permute-done | bytes 2097184 | tf_op jit(solution)/shard_map/ppermute | solution.py:338
  36.9 0.0 collective-permute-start.9
  36.9 1.4 %collective-permute-start.7 = (bf16[528,256]{1,0:T(8,128)(2,1)S(1)}, bf16[528,256]{1,0:T(8,128)(2,1)S(1)}, u32[]{:S(2)}, u32[]{:S(2)}) collective-permute-start(bf16[528,256]{1,0:T(8,128)(2,1)S(1)} %get-tuple-element.50), channel_id=1, source_target_pairs={{0,64},{64,0},{128,192},{192,128},{1,65},{65,1},{129,193},{193,129... | collective-permute-start | bytes 811016 | tf_op jit(solution)/shard_map/ppermute | solution.py:340
  38.3 3.3 %collective-permute-done.4.a_ref.refs_4_ = bf16[784,512]{1,0:T(8,128)(2,1)S(1)} collective-permute-done((bf16[784,512]{1,0:T(8,128)(2,1)S(1)}, bf16[784,512]{1,0:T(8,128)(2,1)S(1)}, u32[]{:S(2)}, u32[]{:S(2)}) %collective-permute-start.4) | collective-permute-done | bytes 802848 | tf_op jit(solution)/shard_map/ppermute | solution.py:340
  41.6 1.0 %collective-permute-done.5.b_ref.refs_6_ = bf16[784,512]{1,0:T(8,128)(2,1)S(1)} collective-permute-done((bf16[784,512]{1,0:T(8,128)(2,1)S(1)}, bf16[784,512]{1,0:T(8,128)(2,1)S(1)}, u32[]{:S(2)}, u32[]{:S(2)}) %collective-permute-start.5) | collective-permute-done | bytes 802848 | tf_op jit(solution)/shard_map/ppermute | solution.py:341
  42.6 1.2 %collective-permute-start.8 = (bf16[528,256]{1,0:T(8,128)(2,1)S(1)}, bf16[528,256]{1,0:T(8,128)(2,1)S(1)}, u32[]{:S(2)}, u32[]{:S(2)}) collective-permute-start(bf16[528,256]{1,0:T(8,128)(2,1)S(1)} %get-tuple-element.58), channel_id=1, source_target_pairs={{0,192},{64,128},{128,64},{192,0},{1,193},{65,129},{129,65},{193,1... | collective-permute-start | bytes 811016 | tf_op jit(solution)/shard_map/ppermute | solution.py:341
  43.8 1.4 %remote_1.1 = (bf16[528,256]{1,0:T(8,128)(2,1)S(1)}, bf16[528,256]{1,0:T(8,128)(2,1)S(1)}) custom-call(bf16[512,2048]{1,0:T(8,128)(2,1)S(1)} %get-tuple-element.45.refs_2_.kv_ref, bf16[784,512]{1,0:T(8,128)(2,1)S(1)} %collective-permute-done.4.a_ref.refs_4_, bf16[784,512]{1,0:T(8,128)(2,1)S(1)} %collective-permute-done.5.b_ref.refs_6_), custom_call_target="tpu_custom_call" | custom-call | flops 13421772800 | bytes 1048576 | tf_op jit(solution)/shard_map/remote_1/pallas_call | solution.py:218
  45.2 2.1 %collective-permute-start.10 = (bf16[528,256]{1,0:T(8,128)(2,1)S(1)}, bf16[528,256]{1,0:T(8,128)(2,1)S(1)}, u32[]{:S(2)}, u32[]{:S(2)}) collective-permute-start(bf16[528,256]{1,0:T(8,128)(2,1)S(1)} %get-tuple-element.67), channel_id=1, source_target_pairs={{0,192},{64,128},{128,64},{192,0},{1,193},{65,129},{129,65},{193,1... | collective-permute-start | bytes 811016 | tf_op jit(solution)/shard_map/ppermute | solution.py:341
  47.4 3.9 %collective-permute-done.8.refs_6_ = bf16[528,256]{1,0:T(8,128)(2,1)S(1)} collective-permute-done((bf16[528,256]{1,0:T(8,128)(2,1)S(1)}, bf16[528,256]{1,0:T(8,128)(2,1)S(1)}, u32[]{:S(2)}, u32[]{:S(2)}) %collective-permute-start.8) | collective-permute-done | bytes 270368 | tf_op jit(solution)/shard_map/ppermute | solution.py:341
  51.2 0.1 collective-permute-start.11
  51.3 0.0 collective-permute-done.7.refs_8_
  51.3 2.4 %local_first_pairs.1 = (f32[2048,256]{1,0:T(8,128)S(1)}, f32[32,256]{1,0:T(8,128)S(1)}) custom-call(f32[16,256]{1,0:T(8,128)S(1)} %get-tuple-element.37.refs_0_, bf16[256,2048]{1,0:T(8,128)(2,1)S(1)} %copy-done, bf16[512,2048]{1,0:T(8,128)(2,1)S(1)} %collective-permute-done.6.refs_2_, bf16[784,512]{1,0:T(8,128)(2,1)S(1)} %collective-permute-done.a_ref.refs_3_, ...), custom_call_target="tpu_custom_call" | custom-call | flops 536870912 | bytes 1048576 | tf_op jit(solution)/shard_map/local_first_pairs/pallas_call | solution.py:322
  53.7 8.7 %collective-permute-done.3.refs_2_ = bf16[512,2048]{1,0:T(8,128)(2,1)S(1)} collective-permute-done((bf16[512,2048]{1,0:T(8,128)(2,1)S(1)}, bf16[512,2048]{1,0:T(8,128)(2,1)S(1)}, u32[]{:S(2)}, u32[]{:S(2)}) %collective-permute-start.3) | collective-permute-done | bytes 2097184 | tf_op jit(solution)/shard_map/ppermute | solution.py:338
  62.4 0.0 collective-permute-done.10.refs_7_
  62.4 0.0 collective-permute-done.11.refs_9_
  62.4 0.0 collective-permute-done.9.refs_3_
  62.4 3.7 %local_second_relay.1 = bf16[256,2048]{1,0:T(8,128)(2,1)} custom-call(f32[16,256]{1,0:T(8,128)S(1)} %get-tuple-element.37.refs_0_, bf16[256,2048]{1,0:T(8,128)(2,1)S(1)} %copy-done, bf16[512,2048]{1,0:T(8,128)(2,1)S(1)} %collective-permute-done.3.refs_2_, bf16[512,2048]{1,0:T(8,128)(2,1)S(1)} %collective-permute-done.9.refs_3_, ...), custom_call_target="tpu_custom_call" | custom-call | flops 536870912 | bytes 1048576 | tf_op jit(solution)/shard_map/local_second_relay/pallas_call | solution.py:322
Async XLA Ops:
  0.0 14.9 %copy-start = (bf16[256,2048]{1,0:T(8,128)(2,1)S(1)}, bf16[256,2048]{1,0:T(8,128)(2,1)}, u32[]{:S(2)}) copy-start(bf16[256,2048]{1,0:T(8,128)(2,1)} %refs_1_.5) | copy-start | bytes 3145732
  2.0 10.3 %collective-permute-start.2 = (bf16[512,2048]{1,0:T(8,128)(2,1)S(1)}, bf16[512,2048]{1,0:T(8,128)(2,1)S(1)}, u32[]{:S(2)}, u32[]{:S(2)}) collective-permute-start(bf16[512,2048]{1,0:T(8,128)(2,1)S(1)} %get-tuple-element.45.refs_2_.kv_ref), channel_id=1, source_target_pairs={{0,1},{1,0},{2,3},{3,2},{4,5},{5,4},{6,7},{7,6},{8,9},{9,8},{10,11... | collective-permute-start | bytes 6291464 | tf_op jit(solution)/shard_map/ppermute | solution.py:338
  2.1 34.8 %collective-permute-start.6 = (bf16[512,2048]{1,0:T(8,128)(2,1)S(1)}, bf16[512,2048]{1,0:T(8,128)(2,1)S(1)}, u32[]{:S(2)}, u32[]{:S(2)}) collective-permute-start(bf16[512,2048]{1,0:T(8,128)(2,1)S(1)} %get-tuple-element.45.refs_2_.kv_ref), channel_id=1, source_target_pairs={{0,62},{1,3},{2,0},{3,5},{4,2},{5,7},{6,4},{7,9},{8,6},{9,11},{10,... | collective-permute-start | bytes 6291464 | tf_op jit(solution)/shard_map/ppermute | solution.py:338
  10.3 20.8 %collective-permute-start = (bf16[784,512]{1,0:T(8,128)(2,1)S(1)}, bf16[784,512]{1,0:T(8,128)(2,1)S(1)}, u32[]{:S(2)}, u32[]{:S(2)}) collective-permute-start(bf16[784,512]{1,0:T(8,128)(2,1)S(1)} %get-tuple-element.39), channel_id=1, source_target_pairs={{0,64},{64,0},{128,192},{192,128},{1,65},{65,1},{129,193},{193,129... | collective-permute-start | bytes 2408456 | tf_op jit(solution)/shard_map/ppermute | solution.py:340
  11.0 22.0 %collective-permute-start.1 = (bf16[784,512]{1,0:T(8,128)(2,1)S(1)}, bf16[784,512]{1,0:T(8,128)(2,1)S(1)}, u32[]{:S(2)}, u32[]{:S(2)}) collective-permute-start(bf16[784,512]{1,0:T(8,128)(2,1)S(1)} %get-tuple-element.40), channel_id=1, source_target_pairs={{0,192},{64,128},{128,64},{192,0},{1,193},{65,129},{129,65},{193,1... | collective-permute-start | bytes 2408456 | tf_op jit(solution)/shard_map/ppermute | solution.py:341
  12.1 29.6 %collective-permute-start.4 = (bf16[784,512]{1,0:T(8,128)(2,1)S(1)}, bf16[784,512]{1,0:T(8,128)(2,1)S(1)}, u32[]{:S(2)}, u32[]{:S(2)}) collective-permute-start(bf16[784,512]{1,0:T(8,128)(2,1)S(1)} %get-tuple-element.46), channel_id=1, source_target_pairs={{0,64},{64,0},{128,192},{192,128},{1,65},{65,1},{129,193},{193,129... | collective-permute-start | bytes 2408456 | tf_op jit(solution)/shard_map/ppermute | solution.py:340
  12.3 30.3 %collective-permute-start.5 = (bf16[784,512]{1,0:T(8,128)(2,1)S(1)}, bf16[784,512]{1,0:T(8,128)(2,1)S(1)}, u32[]{:S(2)}, u32[]{:S(2)}) collective-permute-start(bf16[784,512]{1,0:T(8,128)(2,1)S(1)} %get-tuple-element.47), channel_id=1, source_target_pairs={{0,192},{64,128},{128,64},{192,0},{1,193},{65,129},{129,65},{193,1... | collective-permute-start | bytes 2408456 | tf_op jit(solution)/shard_map/ppermute | solution.py:341
  33.1 29.4 %collective-permute-start.3 = (bf16[512,2048]{1,0:T(8,128)(2,1)S(1)}, bf16[512,2048]{1,0:T(8,128)(2,1)S(1)}, u32[]{:S(2)}, u32[]{:S(2)}) collective-permute-start(bf16[512,2048]{1,0:T(8,128)(2,1)S(1)} %get-tuple-element.45.refs_2_.kv_ref), channel_id=1, source_target_pairs={{0,2},{1,63},{2,4},{3,1},{4,6},{5,3},{6,8},{7,5},{8,10},{9,7},{10,... | collective-permute-start | bytes 6291464 | tf_op jit(solution)/shard_map/ppermute | solution.py:338
  36.9 25.5 %collective-permute-start.9 = (bf16[512,2048]{1,0:T(8,128)(2,1)S(1)}, bf16[512,2048]{1,0:T(8,128)(2,1)S(1)}, u32[]{:S(2)}, u32[]{:S(2)}) collective-permute-start(bf16[512,2048]{1,0:T(8,128)(2,1)S(1)} %collective-permute-done.6.refs_2_), channel_id=1, source_target_pairs={{0,1},{1,0},{2,3},{3,2},{4,5},{5,4},{6,7},{7,6},{8,9},{9,8},{10,11... | collective-permute-start | bytes 6291464 | tf_op jit(solution)/shard_map/ppermute | solution.py:338
  36.9 14.4 %collective-permute-start.7 = (bf16[528,256]{1,0:T(8,128)(2,1)S(1)}, bf16[528,256]{1,0:T(8,128)(2,1)S(1)}, u32[]{:S(2)}, u32[]{:S(2)}) collective-permute-start(bf16[528,256]{1,0:T(8,128)(2,1)S(1)} %get-tuple-element.50), channel_id=1, source_target_pairs={{0,64},{64,0},{128,192},{192,128},{1,65},{65,1},{129,193},{193,129... | collective-permute-start | bytes 811016 | tf_op jit(solution)/shard_map/ppermute | solution.py:340
  42.6 8.6 %collective-permute-start.8 = (bf16[528,256]{1,0:T(8,128)(2,1)S(1)}, bf16[528,256]{1,0:T(8,128)(2,1)S(1)}, u32[]{:S(2)}, u32[]{:S(2)}) collective-permute-start(bf16[528,256]{1,0:T(8,128)(2,1)S(1)} %get-tuple-element.58), channel_id=1, source_target_pairs={{0,192},{64,128},{128,64},{192,0},{1,193},{65,129},{129,65},{193,1... | collective-permute-start | bytes 811016 | tf_op jit(solution)/shard_map/ppermute | solution.py:341
  45.2 17.2 %collective-permute-start.10 = (bf16[528,256]{1,0:T(8,128)(2,1)S(1)}, bf16[528,256]{1,0:T(8,128)(2,1)S(1)}, u32[]{:S(2)}, u32[]{:S(2)}) collective-permute-start(bf16[528,256]{1,0:T(8,128)(2,1)S(1)} %get-tuple-element.67), channel_id=1, source_target_pairs={{0,192},{64,128},{128,64},{192,0},{1,193},{65,129},{129,65},{193,1... | collective-permute-start | bytes 811016 | tf_op jit(solution)/shard_map/ppermute | solution.py:341
  51.2 11.2 %collective-permute-start.11 = (bf16[528,256]{1,0:T(8,128)(2,1)S(1)}, bf16[528,256]{1,0:T(8,128)(2,1)S(1)}, u32[]{:S(2)}, u32[]{:S(2)}) collective-permute-start(bf16[528,256]{1,0:T(8,128)(2,1)S(1)} %get-tuple-element.57), channel_id=1, source_target_pairs={{0,64},{64,0},{128,192},{192,128},{1,65},{65,1},{129,193},{193,129... | collective-permute-start | bytes 811016 | tf_op jit(solution)/shard_map/ppermute | solution.py:340

commit v4 on v3

--- a/solution.py
+++ b/solution.py
@@ -24,7 +24,7 @@
 REPLY = PW + 16
 SPLIT = 4
 VMEM_LIMIT = 20 * 1024 * 1024
-REMOTE_COST = 200
+REMOTE_COST = (400, 200)
 
 f32 = jnp.float32
 bf16 = jnp.bfloat16
@@ -222,7 +222,7 @@
         out_shape=[jax.ShapeDtypeStruct((REPLY, ROWS), bf16)] * 2,
         compiler_params=pltpu.CompilerParams(vmem_limit_bytes=VMEM_LIMIT),
         cost_estimate=pl.CostEstimate(
-            flops=REMOTE_COST * ROWS * ROWS * HALF, bytes_accessed=1024 * 1024, transcendentals=0
+            flops=REMOTE_COST[part] * ROWS * ROWS * HALF, bytes_accessed=1024 * 1024, transcendentals=0
         ),
         name=f"remote_{part}",
     )(kv, a, b)
@@ -358,6 +358,7 @@
     relay = core(first)
     got_a[1], got_b[1], first = lax.optimization_barrier((got_a[1], got_b[1], first))
     part_a, part_b = remote(kv, got_a[1], got_b[1], 1)
+    part_a, back_a[0] = lax.optimization_barrier((part_a, back_a[0]))
     back_a[1], back_b[1] = to_a(part_a), to_b(part_b)
 
     state, part_a, back_a[0], back_b[0] = lax.optimization_barrier((state, part_a, back_a[0], back_b[0]))

time: 66.4 us -> 65.1 us (0.980)
  the two profiles are of different devices: /device:TPU:24 before, /device:TPU:1 now
where the time goes in v4:
time: 65.1 us; the launch traced here: 65 us
  waiting for transfers between devices  28.4 us (44%)
  starting transfers between devices  23.1 us (35%)
  Pallas kernels  13.4 us (21%)
    ppermute x4, starting transfers between devices, shards(): lax.ppermute(x, 'rank', [(i, to(i) % ranks) for i in range(ranks)])  15.7 us
    ppermute x4, waiting for transfers between devices, shards(): to_a = lambda x: lax.ppermute(x, 'group', [(i, i ^ 1) for i in range(4)])  15.3 us
    ppermute x4, waiting for transfers between devices, shards(): lax.ppermute(x, 'rank', [(i, to(i) % ranks) for i in range(ranks)])  11.1 us
    pallas_call x3, Pallas kernels, local(): pl.pallas_call(functools.partial(local_kernel, plan, before is not None,...  8.54 us
    ppermute x4, starting transfers between devices, shards(): to_b = lambda x: lax.ppermute(x, 'group', [(i, 3 - i) for i in range(4)])  5.23 us
    pallas_call x2, Pallas kernels, remote(): pl.pallas_call(functools.partial(remote_kernel, part), in_specs=[vmem] *...  2.84 us
    ppermute x4, starting transfers between devices, shards(): to_a = lambda x: lax.ppermute(x, 'group', [(i, i ^ 1) for i in range(4)])  2.11 us
    pallas_call x1, Pallas kernels, pack(): pl.pallas_call(pack_kernel, in_specs=[hbm] * 5, out_specs=[vmem] * (2 + 2...  2.03 us
  transfers between devices with their start and end apart: 12, of which 7 were waited for; matrix products, arithmetic and copies ran while one was open for 0% of the time, Pallas kernels for 12%

profile of v4, /device:TPU:1, one launch (start us, length us, event | category | flops | bytes accessed | tf_op | source)
XLA Modules:
  0.0 65.0 jit_solution(4046403022640742100)
XLA Ops:
  0.0 0.0 copy-start
  0.0 2.0 %pack.1 = (bf16[512,2048]{1,0:T(8,128)(2,1)S(1)}, bf16[784,512]{1,0:T(8,128)(2,1)S(1)}, bf16[784,512]{1,0:T(8,128)(2,1)S(1)}, bf16[784,512]{1,0:T(8,128)(2,1)S(1...) custom-call(s32[2,8]{1,0:T(2,128)} %links_hbm.1, s32[2]{0:T(128)} %counts_hbm.1, bf16[256,2048]{1,0:T(8,128)(2,1)} %refs_1_.5, ...), custom_call_target="tpu_custom_call" | custom-call | bytes 8388608 | tf_op jit(solution)/shard_map/pack/pallas_call | solution.py:158
  2.0 3.3 %collective-permute-start.2 = (bf16[512,2048]{1,0:T(8,128)(2,1)S(1)}, bf16[512,2048]{1,0:T(8,128)(2,1)S(1)}, u32[]{:S(2)}, u32[]{:S(2)}) collective-permute-start(bf16[512,2048]{1,0:T(8,128)(2,1)S(1)} %get-tuple-element.47.refs_2_.kv_ref), channel_id=1, source_target_pairs={{0,1},{1,0},{2,3},{3,2},{4,5},{5,4},{6,7},{7,6},{8,9},{9,8},{10,11... | collective-permute-start | bytes 6291464 | tf_op jit(solution)/shard_map/ppermute | solution.py:338
  5.4 0.0 collective-permute-start
  5.4 1.5 %collective-permute-start.1 = (bf16[784,512]{1,0:T(8,128)(2,1)S(1)}, bf16[784,512]{1,0:T(8,128)(2,1)S(1)}, u32[]{:S(2)}, u32[]{:S(2)}) collective-permute-start(bf16[784,512]{1,0:T(8,128)(2,1)S(1)} %get-tuple-element.42), channel_id=1, source_target_pairs={{0,192},{64,128},{128,64},{192,0},{1,193},{65,129},{129,65},{193,1... | collective-permute-start | bytes 2408456 | tf_op jit(solution)/shard_map/ppermute | solution.py:341
  6.9 1.2 %collective-permute-start.6 = (bf16[512,2048]{1,0:T(8,128)(2,1)S(1)}, bf16[512,2048]{1,0:T(8,128)(2,1)S(1)}, u32[]{:S(2)}, u32[]{:S(2)}) collective-permute-start(bf16[512,2048]{1,0:T(8,128)(2,1)S(1)} %get-tuple-element.47.refs_2_.kv_ref), channel_id=1, source_target_pairs={{0,62},{1,3},{2,0},{3,5},{4,2},{5,7},{6,4},{7,9},{8,6},{9,11},{10,... | collective-permute-start | bytes 6291464 | tf_op jit(solution)/shard_map/ppermute | solution.py:338
  8.1 0.4 collective-permute-start.4
  8.5 0.7 %collective-permute-done.2.refs_3_ = bf16[512,2048]{1,0:T(8,128)(2,1)S(1)} collective-permute-done((bf16[512,2048]{1,0:T(8,128)(2,1)S(1)}, bf16[512,2048]{1,0:T(8,128)(2,1)S(1)}, u32[]{:S(2)}, u32[]{:S(2)}) %collective-permute-start.2) | collective-permute-done | bytes 2097184 | tf_op jit(solution)/shard_map/ppermute | solution.py:338
  9.2 1.0 %collective-permute-start.5 = (bf16[784,512]{1,0:T(8,128)(2,1)S(1)}, bf16[784,512]{1,0:T(8,128)(2,1)S(1)}, u32[]{:S(2)}, u32[]{:S(2)}) collective-permute-start(bf16[784,512]{1,0:T(8,128)(2,1)S(1)} %get-tuple-element.49), channel_id=1, source_target_pairs={{0,192},{64,128},{128,64},{192,0},{1,193},{65,129},{129,65},{193,1... | collective-permute-start | bytes 2408456 | tf_op jit(solution)/shard_map/ppermute | solution.py:341
  10.2 0.0 copy-done
  10.2 2.4 %local_own_core.1 = (f32[2048,256]{1,0:T(8,128)S(1)}, f32[32,256]{1,0:T(8,128)S(1)}) custom-call(f32[16,256]{1,0:T(8,128)S(1)} %get-tuple-element.39.refs_0_, bf16[256,2048]{1,0:T(8,128)(2,1)S(1)} %copy-done, bf16[512,2048]{1,0:T(8,128)(2,1)S(1)} %get-tuple-element.47.refs_2_.kv_ref, bf16[512,2048]{1,0:T(8,128)(2,1)S(1)} %collective-permute-done.2.refs_3_), custom_call_target="tpu_custom_call" | custom-call | flops 536870912 | bytes 1048576 | tf_op jit(solution)/shard_map/local_own_core/pallas_call | solution.py:322
  12.6 12.2 %collective-permute-done.a_ref.refs_3_ = bf16[784,512]{1,0:T(8,128)(2,1)S(1)} collective-permute-done((bf16[784,512]{1,0:T(8,128)(2,1)S(1)}, bf16[784,512]{1,0:T(8,128)(2,1)S(1)}, u32[]{:S(2)}, u32[]{:S(2)}) %collective-permute-start) | collective-permute-done | bytes 802848 | tf_op jit(solution)/shard_map/ppermute | solution.py:340
  24.8 1.1 %collective-permute-done.1.b_ref.refs_5_ = bf16[784,512]{1,0:T(8,128)(2,1)S(1)} collective-permute-done((bf16[784,512]{1,0:T(8,128)(2,1)S(1)}, bf16[784,512]{1,0:T(8,128)(2,1)S(1)}, u32[]{:S(2)}, u32[]{:S(2)}) %collective-permute-start.1) | collective-permute-done | bytes 802848 | tf_op jit(solution)/shard_map/ppermute | solution.py:341
  25.9 7.2 %collective-permute-start.3 = (bf16[512,2048]{1,0:T(8,128)(2,1)S(1)}, bf16[512,2048]{1,0:T(8,128)(2,1)S(1)}, u32[]{:S(2)}, u32[]{:S(2)}) collective-permute-start(bf16[512,2048]{1,0:T(8,128)(2,1)S(1)} %get-tuple-element.47.refs_2_.kv_ref), channel_id=1, source_target_pairs={{0,2},{1,63},{2,4},{3,1},{4,6},{5,3},{6,8},{7,5},{8,10},{9,7},{10,... | collective-permute-start | bytes 6291464 | tf_op jit(solution)/shard_map/ppermute | solution.py:338
  33.0 1.4 %remote_0.1 = (bf16[528,256]{1,0:T(8,128)(2,1)S(1)}, bf16[528,256]{1,0:T(8,128)(2,1)S(1)}) custom-call(bf16[512,2048]{1,0:T(8,128)(2,1)S(1)} %get-tuple-element.47.refs_2_.kv_ref, bf16[784,512]{1,0:T(8,128)(2,1)S(1)} %collective-permute-done.a_ref.refs_3_, bf16[784,512]{1,0:T(8,128)(2,1)S(1)} %collective-permute-done.1.b_ref.refs_5_), custom_call_target="tpu_custom_call" | custom-call | flops 26843545600 | bytes 1048576 | tf_op jit(solution)/shard_map/remote_0/pallas_call | solution.py:218
  34.5 5.7 %collective-permute-done.6.refs_2_ = bf16[512,2048]{1,0:T(8,128)(2,1)S(1)} collective-permute-done((bf16[512,2048]{1,0:T(8,128)(2,1)S(1)}, bf16[512,2048]{1,0:T(8,128)(2,1)S(1)}, u32[]{:S(2)}, u32[]{:S(2)}) %collective-permute-start.6) | collective-permute-done | bytes 2097184 | tf_op jit(solution)/shard_map/ppermute | solution.py:338
  40.2 4.0 %collective-permute-start.9 = (bf16[512,2048]{1,0:T(8,128)(2,1)S(1)}, bf16[512,2048]{1,0:T(8,128)(2,1)S(1)}, u32[]{:S(2)}, u32[]{:S(2)}) collective-permute-start(bf16[512,2048]{1,0:T(8,128)(2,1)S(1)} %collective-permute-done.6.refs_2_), channel_id=1, source_target_pairs={{0,1},{1,0},{2,3},{3,2},{4,5},{5,4},{6,7},{7,6},{8,9},{9,8},{10,11... | collective-permute-start | bytes 6291464 | tf_op jit(solution)/shard_map/ppermute | solution.py:338
  44.2 0.9 %collective-permute-start.7 = (bf16[528,256]{1,0:T(8,128)(2,1)S(1)}, bf16[528,256]{1,0:T(8,128)(2,1)S(1)}, u32[]{:S(2)}, u32[]{:S(2)}) collective-permute-start(bf16[528,256]{1,0:T(8,128)(2,1)S(1)} %get-tuple-element.52), channel_id=1, source_target_pairs={{0,64},{64,0},{128,192},{192,128},{1,65},{65,1},{129,193},{193,129... | collective-permute-start | bytes 811016 | tf_op jit(solution)/shard_map/ppermute | solution.py:340
  45.0 0.0 collective-permute-done.4.a_ref.refs_4_
  45.0 0.0 collective-permute-done.5.b_ref.refs_6_
  45.0 0.0 collective-permute-start.8
  45.0 1.4 %remote_1.1 = (bf16[528,256]{1,0:T(8,128)(2,1)S(1)}, bf16[528,256]{1,0:T(8,128)(2,1)S(1)}) custom-call(bf16[512,2048]{1,0:T(8,128)(2,1)S(1)} %get-tuple-element.47.refs_2_.kv_ref, bf16[784,512]{1,0:T(8,128)(2,1)S(1)} %collective-permute-done.4.a_ref.refs_4_, bf16[784,512]{1,0:T(8,128)(2,1)S(1)} %collective-permute-done.5.b_ref.refs_6_), custom_call_target="tpu_custom_call" | custom-call | flops 13421772800 | bytes 1048576 | tf_op jit(solution)/shard_map/remote_1/pallas_call | solution.py:218
  46.5 2.8 %collective-permute-start.10 = (bf16[528,256]{1,0:T(8,128)(2,1)S(1)}, bf16[528,256]{1,0:T(8,128)(2,1)S(1)}, u32[]{:S(2)}, u32[]{:S(2)}) collective-permute-start(bf16[528,256]{1,0:T(8,128)(2,1)S(1)} %get-tuple-element.71), channel_id=1, source_target_pairs={{0,192},{64,128},{128,64},{192,0},{1,193},{65,129},{129,65},{193,1... | collective-permute-start | bytes 811016 | tf_op jit(solution)/shard_map/ppermute | solution.py:341
  49.2 3.1 %collective-permute-done.7.refs_8_ = bf16[528,256]{1,0:T(8,128)(2,1)S(1)} collective-permute-done((bf16[528,256]{1,0:T(8,128)(2,1)S(1)}, bf16[528,256]{1,0:T(8,128)(2,1)S(1)}, u32[]{:S(2)}, u32[]{:S(2)}) %collective-permute-start.7) | collective-permute-done | bytes 270368 | tf_op jit(solution)/shard_map/ppermute | solution.py:340
  52.3 0.9 %collective-permute-start.11 = (bf16[528,256]{1,0:T(8,128)(2,1)S(1)}, bf16[528,256]{1,0:T(8,128)(2,1)S(1)}, u32[]{:S(2)}, u32[]{:S(2)}) collective-permute-start(bf16[528,256]{1,0:T(8,128)(2,1)S(1)} %get-tuple-element.60), channel_id=1, source_target_pairs={{0,64},{64,0},{128,192},{192,128},{1,65},{65,1},{129,193},{193,129... | collective-permute-start | bytes 811016 | tf_op jit(solution)/shard_map/ppermute | solution.py:340
  53.1 0.9 %collective-permute-done.8.refs_6_ = bf16[528,256]{1,0:T(8,128)(2,1)S(1)} collective-permute-done((bf16[528,256]{1,0:T(8,128)(2,1)S(1)}, bf16[528,256]{1,0:T(8,128)(2,1)S(1)}, u32[]{:S(2)}, u32[]{:S(2)}) %collective-permute-start.8) | collective-permute-done | bytes 270368 | tf_op jit(solution)/shard_map/ppermute | solution.py:341
  54.0 2.4 %local_first_pairs.1 = (f32[2048,256]{1,0:T(8,128)S(1)}, f32[32,256]{1,0:T(8,128)S(1)}) custom-call(f32[16,256]{1,0:T(8,128)S(1)} %get-tuple-element.39.refs_0_, bf16[256,2048]{1,0:T(8,128)(2,1)S(1)} %copy-done, bf16[512,2048]{1,0:T(8,128)(2,1)S(1)} %collective-permute-done.6.refs_2_, bf16[784,512]{1,0:T(8,128)(2,1)S(1)} %collective-permute-done.a_ref.refs_3_, ...), custom_call_target="tpu_custom_call" | custom-call | flops 536870912 | bytes 1048576 | tf_op jit(solution)/shard_map/local_first_pairs/pallas_call | solution.py:322
  56.5 4.7 %collective-permute-done.3.refs_2_ = bf16[512,2048]{1,0:T(8,128)(2,1)S(1)} collective-permute-done((bf16[512,2048]{1,0:T(8,128)(2,1)S(1)}, bf16[512,2048]{1,0:T(8,128)(2,1)S(1)}, u32[]{:S(2)}, u32[]{:S(2)}) %collective-permute-start.3) | collective-permute-done | bytes 2097184 | tf_op jit(solution)/shard_map/ppermute | solution.py:338
  61.2 0.0 collective-permute-done.10.refs_7_
  61.2 0.0 collective-permute-done.11.refs_9_
  61.2 0.0 collective-permute-done.9.refs_3_
  61.2 3.7 %local_second_relay.1 = bf16[256,2048]{1,0:T(8,128)(2,1)} custom-call(f32[16,256]{1,0:T(8,128)S(1)} %get-tuple-element.39.refs_0_, bf16[256,2048]{1,0:T(8,128)(2,1)S(1)} %copy-done, bf16[512,2048]{1,0:T(8,128)(2,1)S(1)} %collective-permute-done.3.refs_2_, bf16[512,2048]{1,0:T(8,128)(2,1)S(1)} %collective-permute-done.9.refs_3_, ...), custom_call_target="tpu_custom_call" | custom-call | flops 536870912 | bytes 1048576 | tf_op jit(solution)/shard_map/local_second_relay/pallas_call | solution.py:322
Async XLA Ops:
  0.0 10.2 %copy-start = (bf16[256,2048]{1,0:T(8,128)(2,1)S(1)}, bf16[256,2048]{1,0:T(8,128)(2,1)}, u32[]{:S(2)}) copy-start(bf16[256,2048]{1,0:T(8,128)(2,1)} %refs_1_.5) | copy-start | bytes 3145732
  2.0 7.1 %collective-permute-start.2 = (bf16[512,2048]{1,0:T(8,128)(2,1)S(1)}, bf16[512,2048]{1,0:T(8,128)(2,1)S(1)}, u32[]{:S(2)}, u32[]{:S(2)}) collective-permute-start(bf16[512,2048]{1,0:T(8,128)(2,1)S(1)} %get-tuple-element.47.refs_2_.kv_ref), channel_id=1, source_target_pairs={{0,1},{1,0},{2,3},{3,2},{4,5},{5,4},{6,7},{7,6},{8,9},{9,8},{10,11... | collective-permute-start | bytes 6291464 | tf_op jit(solution)/shard_map/ppermute | solution.py:338
  5.4 19.5 %collective-permute-start = (bf16[784,512]{1,0:T(8,128)(2,1)S(1)}, bf16[784,512]{1,0:T(8,128)(2,1)S(1)}, u32[]{:S(2)}, u32[]{:S(2)}) collective-permute-start(bf16[784,512]{1,0:T(8,128)(2,1)S(1)} %get-tuple-element.41), channel_id=1, source_target_pairs={{0,64},{64,0},{128,192},{192,128},{1,65},{65,1},{129,193},{193,129... | collective-permute-start | bytes 2408456 | tf_op jit(solution)/shard_map/ppermute | solution.py:340
  5.4 20.5 %collective-permute-start.1 = (bf16[784,512]{1,0:T(8,128)(2,1)S(1)}, bf16[784,512]{1,0:T(8,128)(2,1)S(1)}, u32[]{:S(2)}, u32[]{:S(2)}) collective-permute-start(bf16[784,512]{1,0:T(8,128)(2,1)S(1)} %get-tuple-element.42), channel_id=1, source_target_pairs={{0,192},{64,128},{128,64},{192,0},{1,193},{65,129},{129,65},{193,1... | collective-permute-start | bytes 2408456 | tf_op jit(solution)/shard_map/ppermute | solution.py:341
  6.9 33.3 %collective-permute-start.6 = (bf16[512,2048]{1,0:T(8,128)(2,1)S(1)}, bf16[512,2048]{1,0:T(8,128)(2,1)S(1)}, u32[]{:S(2)}, u32[]{:S(2)}) collective-permute-start(bf16[512,2048]{1,0:T(8,128)(2,1)S(1)} %get-tuple-element.47.refs_2_.kv_ref), channel_id=1, source_target_pairs={{0,62},{1,3},{2,0},{3,5},{4,2},{5,7},{6,4},{7,9},{8,6},{9,11},{10,... | collective-permute-start | bytes 6291464 | tf_op jit(solution)/shard_map/ppermute | solution.py:338
  8.1 37.0 %collective-permute-start.4 = (bf16[784,512]{1,0:T(8,128)(2,1)S(1)}, bf16[784,512]{1,0:T(8,128)(2,1)S(1)}, u32[]{:S(2)}, u32[]{:S(2)}) collective-permute-start(bf16[784,512]{1,0:T(8,128)(2,1)S(1)} %get-tuple-element.48), channel_id=1, source_target_pairs={{0,64},{64,0},{128,192},{192,128},{1,65},{65,1},{129,193},{193,129... | collective-permute-start | bytes 2408456 | tf_op jit(solution)/shard_map/ppermute | solution.py:340
  9.2 35.9 %collective-permute-start.5 = (bf16[784,512]{1,0:T(8,128)(2,1)S(1)}, bf16[784,512]{1,0:T(8,128)(2,1)S(1)}, u32[]{:S(2)}, u32[]{:S(2)}) collective-permute-start(bf16[784,512]{1,0:T(8,128)(2,1)S(1)} %get-tuple-element.49), channel_id=1, source_target_pairs={{0,192},{64,128},{128,64},{192,0},{1,193},{65,129},{129,65},{193,1... | collective-permute-start | bytes 2408456 | tf_op jit(solution)/shard_map/ppermute | solution.py:341
  25.9 35.3 %collective-permute-start.3 = (bf16[512,2048]{1,0:T(8,128)(2,1)S(1)}, bf16[512,2048]{1,0:T(8,128)(2,1)S(1)}, u32[]{:S(2)}, u32[]{:S(2)}) collective-permute-start(bf16[512,2048]{1,0:T(8,128)(2,1)S(1)} %get-tuple-element.47.refs_2_.kv_ref), channel_id=1, source_target_pairs={{0,2},{1,63},{2,4},{3,1},{4,6},{5,3},{6,8},{7,5},{8,10},{9,7},{10,... | collective-permute-start | bytes 6291464 | tf_op jit(solution)/shard_map/ppermute | solution.py:338
  40.2 21.0 %collective-permute-start.9 = (bf16[512,2048]{1,0:T(8,128)(2,1)S(1)}, bf16[512,2048]{1,0:T(8,128)(2,1)S(1)}, u32[]{:S(2)}, u32[]{:S(2)}) collective-permute-start(bf16[512,2048]{1,0:T(8,128)(2,1)S(1)} %collective-permute-done.6.refs_2_), channel_id=1, source_target_pairs={{0,1},{1,0},{2,3},{3,2},{4,5},{5,4},{6,7},{7,6},{8,9},{9,8},{10,11... | collective-permute-start | bytes 6291464 | tf_op jit(solution)/shard_map/ppermute | solution.py:338
  44.2 8.1 %collective-permute-start.7 = (bf16[528,256]{1,0:T(8,128)(2,1)S(1)}, bf16[528,256]{1,0:T(8,128)(2,1)S(1)}, u32[]{:S(2)}, u32[]{:S(2)}) collective-permute-start(bf16[528,256]{1,0:T(8,128)(2,1)S(1)} %get-tuple-element.52), channel_id=1, source_target_pairs={{0,64},{64,0},{128,192},{192,128},{1,65},{65,1},{129,193},{193,129... | collective-permute-start | bytes 811016 | tf_op jit(solution)/shard_map/ppermute | solution.py:340
  45.0 9.0 %collective-permute-start.8 = (bf16[528,256]{1,0:T(8,128)(2,1)S(1)}, bf16[528,256]{1,0:T(8,128)(2,1)S(1)}, u32[]{:S(2)}, u32[]{:S(2)}) collective-permute-start(bf16[528,256]{1,0:T(8,128)(2,1)S(1)} %get-tuple-element.62), channel_id=1, source_target_pairs={{0,192},{64,128},{128,64},{192,0},{1,193},{65,129},{129,65},{193,1... | collective-permute-start | bytes 811016 | tf_op jit(solution)/shard_map/ppermute | solution.py:341
  46.5 14.7 %collective-permute-start.10 = (bf16[528,256]{1,0:T(8,128)(2,1)S(1)}, bf16[528,256]{1,0:T(8,128)(2,1)S(1)}, u32[]{:S(2)}, u32[]{:S(2)}) collective-permute-start(bf16[528,256]{1,0:T(8,128)(2,1)S(1)} %get-tuple-element.71), channel_id=1, source_target_pairs={{0,192},{64,128},{128,64},{192,0},{1,193},{65,129},{129,65},{193,1... | collective-permute-start | bytes 811016 | tf_op jit(solution)/shard_map/ppermute | solution.py:341
  52.3 8.9 %collective-permute-start.11 = (bf16[528,256]{1,0:T(8,128)(2,1)S(1)}, bf16[528,256]{1,0:T(8,128)(2,1)S(1)}, u32[]{:S(2)}, u32[]{:S(2)}) collective-permute-start(bf16[528,256]{1,0:T(8,128)(2,1)S(1)} %get-tuple-element.60), channel_id=1, source_target_pairs={{0,64},{64,0},{128,192},{192,128},{1,65},{65,1},{129,193},{193,129... | collective-permute-start | bytes 811016 | tf_op jit(solution)/shard_map/ppermute | solution.py:340

commit v5 on v4

--- a/solution.py
+++ b/solution.py
@@ -24,7 +24,8 @@
 REPLY = PW + 16
 SPLIT = 4
 VMEM_LIMIT = 20 * 1024 * 1024
-REMOTE_COST = (400, 200)
+REMOTE_COST = (400, 8)
+MIDDLE_COST = 22
 
 f32 = jnp.float32
 bf16 = jnp.bfloat16
@@ -235,7 +236,11 @@
     odd_group = (lax.axis_index("group") % 2) == 1
     sources = []
     for role in plan:
-        if role == "pairs":
+        if role == "relay":
+            arrays = [refs.pop(0), refs.pop(0)]
+            block = jnp.where(odd_core, 3, 2)
+            blocks = (block, block)
+        elif role == "pairs":
             arrays = [refs.pop(0) for _ in range(2 * PARTS)]
             blocks = (jnp.where(odd_group, 7, 5), jnp.where(odd_group, 5, 7))
         else:
@@ -243,7 +248,6 @@
             block = {
                 "own": 0,
                 "core": jnp.where(odd_core, 2, 3),
-                "relay": jnp.where(odd_core, 3, 2),
                 "first": jnp.where(odd_core, 1, 4),
                 "second": jnp.where(odd_core, 4, 1),
             }[role]
@@ -269,6 +273,9 @@
         low = slice(inner * HD, (inner + 1) * HD)
         given = []
         for role, arrays, bias in sources:
+            if role == "relay":
+                given.append((arrays[0][:, c], arrays[1][:, c], bias[half]))
+                continue
             array, at = (arrays[piece], low) if role == "pairs" else (arrays, c)
             given.append((array[0:ROWS, at], array[ROWS : 2 * ROWS, at], bias[half]))
         before = reply = None
@@ -301,12 +308,12 @@
         refs[1][...] = jnp.concatenate(tops + sums, axis=0)
 
 
-def local(table, q, sources, before=None, reply=None, last=False):
+def local(table, q, sources, before=None, reply=None, last=False, cost=1):
     vmem = pl.BlockSpec(memory_space=pltpu.VMEM)
     plan = tuple(role for role, _ in sources)
     args = [table, q]
     for role, arrays in sources:
-        args += list(arrays) if role == "pairs" else [arrays]
+        args += list(arrays) if role in ("pairs", "relay") else [arrays]
     args += list(before or ()) + list(reply or ())
     if last:
         out_specs = pl.BlockSpec(memory_space=pl.ANY)
@@ -327,7 +334,7 @@
         scratch_shapes=scratch,
         compiler_params=pltpu.CompilerParams(vmem_limit_bytes=VMEM_LIMIT),
         cost_estimate=pl.CostEstimate(
-            flops=4 * ROWS * ROWS * W, bytes_accessed=1024 * 1024, transcendentals=0
+            flops=4 * cost * ROWS * ROWS * W, bytes_accessed=1024 * 1024, transcendentals=0
         ),
         name="local_" + "_".join(plan),
     )(*args)
@@ -343,28 +350,33 @@
     kv, pay_a, pay_b, table = pack(links, counts, q, k, v)
     first = across(kv, lambda i: i + 2 if i % 2 else i - 2)
     from_core = core(kv)
-    got_a = [to_a(x) for x in pay_a]
-    got_b = [to_b(x) for x in pay_b]
+    got_a = [to_a(pay_a[0]), to_a(pay_a[1])]
+    got_b = [to_b(pay_b[0])]
+    kv_later, from_core = lax.optimization_barrier((kv, from_core))
+    second = across(kv_later, lambda i: i - 2 if i % 2 else i + 2)
     state = local(table, q, [("own", kv), ("core", from_core)])
 
     back_a, back_b = [None] * PARTS, [None] * PARTS
     got_a[0], got_b[0], state = lax.optimization_barrier((got_a[0], got_b[0], state))
-    kv_later, got_a[0], got_b[0] = lax.optimization_barrier((kv, got_a[0], got_b[0]))
-    second = across(kv_later, lambda i: i - 2 if i % 2 else i + 2)
+    pay, got_a[0] = lax.optimization_barrier((pay_b[1], got_a[0]))
+    got_b.append(to_b(pay))
     part_a, part_b = remote(kv, got_a[0], got_b[0], 0)
     back_a[0], back_b[0] = to_a(part_a), to_b(part_b)
 
-    first, part_a = lax.optimization_barrier((first, part_a))
-    relay = core(first)
-    got_a[1], got_b[1], first = lax.optimization_barrier((got_a[1], got_b[1], first))
+    got_a[1], got_b[1], part_a = lax.optimization_barrier((got_a[1], got_b[1], part_a))
     part_a, part_b = remote(kv, got_a[1], got_b[1], 1)
     part_a, back_a[0] = lax.optimization_barrier((part_a, back_a[0]))
+    part_b, back_b[0] = lax.optimization_barrier((part_b, back_b[0]))
     back_a[1], back_b[1] = to_a(part_a), to_b(part_b)
 
-    state, part_a, back_a[0], back_b[0] = lax.optimization_barrier((state, part_a, back_a[0], back_b[0]))
-    state = local(table, q, [("first", first), ("pairs", got_a + got_b)], state)
+    first, part_a, part_b = lax.optimization_barrier((first, part_a, part_b))
+    relay = [core(first[:ROWS]), core(first[ROWS:])]
+    state, part_a = lax.optimization_barrier((state, part_a))
+    middle = [("first", first), ("pairs", got_a + got_b)]
+    state = local(table, q, middle, state, cost=MIDDLE_COST)
     second, state = lax.optimization_barrier((second, state))
-    return local(table, q, [("second", second), ("relay", relay)], state, back_b + back_a, True)
+    near = [("second", second), ("relay", relay)]
+    return local(table, q, near, state, back_b + back_a, True)
 
 
 def solution(mesh):

time: 65.1 us -> 69 us (1.060)
  waiting for transfers between devices: 28.4 us -> 31.9 us
    ppermute x4 -> x5, waiting for transfers between devices: 11.1 us -> 2.95 us  [shards(): lax.ppermute(x, 'rank', [(i, to(i) % ranks) for i in range(ranks)])]
    ppermute x4, waiting for transfers between devices: 15.3 us -> 21.5 us  [shards(): to_a = lambda x: lax.ppermute(x, 'group', [(i, i ^ 1) for i in range(4)])]
    ppermute x4, waiting for transfers between devices: 1.97 us -> 7.51 us  [shards(): to_b = lambda x: lax.ppermute(x, 'group', [(i, 3 - i) for i in range(4)])]
    ppermute x4 -> x5, starting transfers between devices: 15.7 us -> 17.9 us  [shards(): lax.ppermute(x, 'rank', [(i, to(i) % ranks) for i in range(ranks)])]
    ppermute x4, starting transfers between devices: 2.11 us -> 0.5 us  [shards(): to_a = lambda x: lax.ppermute(x, 'group', [(i, i ^ 1) for i in range(4)])]
  transfers between devices with their start and end apart: 12 -> 13, of which waited for: 7 -> 9; matrix products, arithmetic and copies ran while one was open for 0% -> 0% of each run, Pallas kernels for 12% -> 11%
where the time goes in v5:
time: 69 us; the launch traced here: 68.9 us
  waiting for transfers between devices  31.9 us (46%)
  starting transfers between devices  23.2 us (34%)
  Pallas kernels  13.4 us (19%)
    ppermute x4, waiting for transfers between devices, shards(): to_a = lambda x: lax.ppermute(x, 'group', [(i, i ^ 1) for i in range(4)])  21.5 us
    ppermute x5, starting transfers between devices, shards(): lax.ppermute(x, 'rank', [(i, to(i) % ranks) for i in range(ranks)])  17.9 us
    pallas_call x3, Pallas kernels, local(): pl.pallas_call(functools.partial(local_kernel, plan, before is not None,...  8.56 us
    ppermute x4, waiting for transfers between devices, shards(): to_b = lambda x: lax.ppermute(x, 'group', [(i, 3 - i) for i in range(4)])  7.51 us
    ppermute x4, starting transfers between devices, shards(): to_b = lambda x: lax.ppermute(x, 'group', [(i, 3 - i) for i in range(4)])  4.76 us
    ppermute x5, waiting for transfers between devices, shards(): lax.ppermute(x, 'rank', [(i, to(i) % ranks) for i in range(ranks)])  2.95 us
    pallas_call x2, Pallas kernels, remote(): pl.pallas_call(functools.partial(remote_kernel, part), in_specs=[vmem] *...  2.83 us
    pallas_call x1, Pallas kernels, pack(): pl.pallas_call(pack_kernel, in_specs=[hbm] * 5, out_specs=[vmem] * (2 + 2...  2.03 us
  transfers between devices with their start and end apart: 13, of which 9 were waited for; matrix products, arithmetic and copies ran while one was open for 0% of the time, Pallas kernels for 11%

profile of v5, /device:TPU:1, one launch (start us, length us, event | category | flops | bytes accessed | tf_op | source)
XLA Modules:
  0.0 68.9 jit_solution(8651964027153478217)
XLA Ops:
  0.0 0.0 copy-start
  0.0 2.0 %pack.1 = (bf16[512,2048]{1,0:T(8,128)(2,1)S(1)}, bf16[784,512]{1,0:T(8,128)(2,1)S(1)}, bf16[784,512]{1,0:T(8,128)(2,1)S(1)}, bf16[784,512]{1,0:T(8,128)(2,1)S(1...) custom-call(s32[2,8]{1,0:T(2,128)} %links_hbm.1, s32[2]{0:T(128)} %counts_hbm.1, bf16[256,2048]{1,0:T(8,128)(2,1)} %refs_1_.5, ...), custom_call_target="tpu_custom_call" | custom-call | bytes 8388608 | tf_op jit(solution)/shard_map/pack/pallas_call | solution.py:159
  2.0 3.3 %collective-permute-start = (bf16[512,2048]{1,0:T(8,128)(2,1)S(1)}, bf16[512,2048]{1,0:T(8,128)(2,1)S(1)}, u32[]{:S(2)}, u32[]{:S(2)}) collective-permute-start(bf16[512,2048]{1,0:T(8,128)(2,1)S(1)} %get-tuple-element.41.refs_2_.kv_ref), channel_id=1, source_target_pairs={{0,1},{1,0},{2,3},{3,2},{4,5},{5,4},{6,7},{7,6},{8,9},{9,8},{10,11... | collective-permute-start | bytes 6291464 | tf_op jit(solution)/shard_map/ppermute | solution.py:345
  5.4 0.0 collective-permute-start.4
  5.4 1.5 %collective-permute-start.5 = (bf16[784,512]{1,0:T(8,128)(2,1)S(1)}, bf16[784,512]{1,0:T(8,128)(2,1)S(1)}, u32[]{:S(2)}, u32[]{:S(2)}) collective-permute-start(bf16[784,512]{1,0:T(8,128)(2,1)S(1)} %get-tuple-element.45), channel_id=1, source_target_pairs={{0,192},{64,128},{128,64},{192,0},{1,193},{65,129},{129,65},{193,1... | collective-permute-start | bytes 2408456 | tf_op jit(solution)/shard_map/ppermute | solution.py:348
  6.9 1.2 %collective-permute-start.2 = (bf16[512,2048]{1,0:T(8,128)(2,1)S(1)}, bf16[512,2048]{1,0:T(8,128)(2,1)S(1)}, u32[]{:S(2)}, u32[]{:S(2)}) collective-permute-start(bf16[512,2048]{1,0:T(8,128)(2,1)S(1)} %get-tuple-element.41.refs_2_.kv_ref), channel_id=1, source_target_pairs={{0,62},{1,3},{2,0},{3,5},{4,2},{5,7},{6,4},{7,9},{8,6},{9,11},{10,... | collective-permute-start | bytes 6291464 | tf_op jit(solution)/shard_map/ppermute | solution.py:345
  8.1 0.4 collective-permute-start.3
  8.5 0.7 %collective-permute-done.refs_3_ = bf16[512,2048]{1,0:T(8,128)(2,1)S(1)} collective-permute-done((bf16[512,2048]{1,0:T(8,128)(2,1)S(1)}, bf16[512,2048]{1,0:T(8,128)(2,1)S(1)}, u32[]{:S(2)}, u32[]{:S(2)}) %collective-permute-start) | collective-permute-done | bytes 2097184 | tf_op jit(solution)/shard_map/ppermute | solution.py:345
  9.2 6.0 %collective-permute-start.1 = (bf16[512,2048]{1,0:T(8,128)(2,1)S(1)}, bf16[512,2048]{1,0:T(8,128)(2,1)S(1)}, u32[]{:S(2)}, u32[]{:S(2)}) collective-permute-start(bf16[512,2048]{1,0:T(8,128)(2,1)S(1)} %get-tuple-element.41.refs_2_.kv_ref), channel_id=1, source_target_pairs={{0,2},{1,63},{2,4},{3,1},{4,6},{5,3},{6,8},{7,5},{8,10},{9,7},{10,... | collective-permute-start | bytes 6291464 | tf_op jit(solution)/shard_map/ppermute | solution.py:345
  15.2 0.0 copy-done
  15.2 2.4 %local_own_core.1 = (f32[2048,256]{1,0:T(8,128)S(1)}, f32[32,256]{1,0:T(8,128)S(1)}) custom-call(f32[16,256]{1,0:T(8,128)S(1)} %get-tuple-element.39.refs_0_, bf16[256,2048]{1,0:T(8,128)(2,1)S(1)} %copy-done, bf16[512,2048]{1,0:T(8,128)(2,1)S(1)} %get-tuple-element.41.refs_2_.kv_ref, bf16[512,2048]{1,0:T(8,128)(2,1)S(1)} %collective-permute-done.refs_3_), custom_call_target="tpu_custom_call" | custom-call | flops 536870912 | bytes 1048576 | tf_op jit(solution)/shard_map/local_own_core/pallas_call | solution.py:329
  17.6 7.2 %collective-permute-done.4.a_ref.refs_3_ = bf16[784,512]{1,0:T(8,128)(2,1)S(1)} collective-permute-done((bf16[784,512]{1,0:T(8,128)(2,1)S(1)}, bf16[784,512]{1,0:T(8,128)(2,1)S(1)}, u32[]{:S(2)}, u32[]{:S(2)}) %collective-permute-start.4) | collective-permute-done | bytes 802848 | tf_op jit(solution)/shard_map/ppermute | solution.py:347
  24.8 1.1 %collective-permute-done.5.b_ref.refs_5_ = bf16[784,512]{1,0:T(8,128)(2,1)S(1)} collective-permute-done((bf16[784,512]{1,0:T(8,128)(2,1)S(1)}, bf16[784,512]{1,0:T(8,128)(2,1)S(1)}, u32[]{:S(2)}, u32[]{:S(2)}) %collective-permute-start.5) | collective-permute-done | bytes 802848 | tf_op jit(solution)/shard_map/ppermute | solution.py:348
  25.9 1.3 %collective-permute-start.6 = (bf16[784,512]{1,0:T(8,128)(2,1)S(1)}, bf16[784,512]{1,0:T(8,128)(2,1)S(1)}, u32[]{:S(2)}, u32[]{:S(2)}) collective-permute-start(bf16[784,512]{1,0:T(8,128)(2,1)S(1)} %get-tuple-element.50), channel_id=1, source_target_pairs={{0,192},{64,128},{128,64},{192,0},{1,193},{65,129},{129,65},{193,1... | collective-permute-start | bytes 2408456 | tf_op jit(solution)/shard_map/ppermute | solution.py:348
  27.2 1.4 %remote_0.1 = (bf16[528,256]{1,0:T(8,128)(2,1)S(1)}, bf16[528,256]{1,0:T(8,128)(2,1)S(1)}) custom-call(bf16[512,2048]{1,0:T(8,128)(2,1)S(1)} %get-tuple-element.41.refs_2_.kv_ref, bf16[784,512]{1,0:T(8,128)(2,1)S(1)} %collective-permute-done.4.a_ref.refs_3_, bf16[784,512]{1,0:T(8,128)(2,1)S(1)} %collective-permute-done.5.b_ref.refs_5_), custom_call_target="tpu_custom_call" | custom-call | flops 26843545600 | bytes 1048576 | tf_op jit(solution)/shard_map/remote_0/pallas_call | solution.py:219
  28.6 0.1 collective-permute-start.7
  28.7 13.3 %collective-permute-done.3.a_ref.refs_4_ = bf16[784,512]{1,0:T(8,128)(2,1)S(1)} collective-permute-done((bf16[784,512]{1,0:T(8,128)(2,1)S(1)}, bf16[784,512]{1,0:T(8,128)(2,1)S(1)}, u32[]{:S(2)}, u32[]{:S(2)}) %collective-permute-start.3) | collective-permute-done | bytes 802848 | tf_op jit(solution)/shard_map/ppermute | solution.py:347
  42.0 1.0 %collective-permute-start.8 = (bf16[528,256]{1,0:T(8,128)(2,1)S(1)}, bf16[528,256]{1,0:T(8,128)(2,1)S(1)}, u32[]{:S(2)}, u32[]{:S(2)}) collective-permute-start(bf16[528,256]{1,0:T(8,128)(2,1)S(1)} %get-tuple-element.59), channel_id=1, source_target_pairs={{0,192},{64,128},{128,64},{192,0},{1,193},{65,129},{129,65},{193,1... | collective-permute-start | bytes 811016 | tf_op jit(solution)/shard_map/ppermute | solution.py:348
  43.0 2.5 %collective-permute-done.6.b_ref.refs_6_ = bf16[784,512]{1,0:T(8,128)(2,1)S(1)} collective-permute-done((bf16[784,512]{1,0:T(8,128)(2,1)S(1)}, bf16[784,512]{1,0:T(8,128)(2,1)S(1)}, u32[]{:S(2)}, u32[]{:S(2)}) %collective-permute-start.6) | collective-permute-done | bytes 802848 | tf_op jit(solution)/shard_map/ppermute | solution.py:348
  45.5 1.4 %remote_1.1 = (bf16[528,256]{1,0:T(8,128)(2,1)S(1)}, bf16[528,256]{1,0:T(8,128)(2,1)S(1)}) custom-call(bf16[512,2048]{1,0:T(8,128)(2,1)S(1)} %get-tuple-element.41.refs_2_.kv_ref, bf16[784,512]{1,0:T(8,128)(2,1)S(1)} %collective-permute-done.3.a_ref.refs_4_, bf16[784,512]{1,0:T(8,128)(2,1)S(1)} %collective-permute-done.6.b_ref.refs_6_), custom_call_target="tpu_custom_call" | custom-call | flops 536870912 | bytes 1048576 | tf_op jit(solution)/shard_map/remote_1/pallas_call | solution.py:219
  46.9 0.9 %collective-permute-done.7.refs_9_ = bf16[528,256]{1,0:T(8,128)(2,1)S(1)} collective-permute-done((bf16[528,256]{1,0:T(8,128)(2,1)S(1)}, bf16[528,256]{1,0:T(8,128)(2,1)S(1)}, u32[]{:S(2)}, u32[]{:S(2)}) %collective-permute-start.7) | collective-permute-done | bytes 270368 | tf_op jit(solution)/shard_map/ppermute | solution.py:347
  47.8 4.0 %collective-permute-done.8.refs_7_ = bf16[528,256]{1,0:T(8,128)(2,1)S(1)} collective-permute-done((bf16[528,256]{1,0:T(8,128)(2,1)S(1)}, bf16[528,256]{1,0:T(8,128)(2,1)S(1)}, u32[]{:S(2)}, u32[]{:S(2)}) %collective-permute-start.8) | collective-permute-done | bytes 270368 | tf_op jit(solution)/shard_map/ppermute | solution.py:348
  51.8 1.0 %collective-permute-start.11 = (bf16[528,256]{1,0:T(8,128)(2,1)S(1)}, bf16[528,256]{1,0:T(8,128)(2,1)S(1)}, u32[]{:S(2)}, u32[]{:S(2)}) collective-permute-start(bf16[528,256]{1,0:T(8,128)(2,1)S(1)} %get-tuple-element.60), channel_id=1, source_target_pairs={{0,192},{64,128},{128,64},{192,0},{1,193},{65,129},{129,65},{193,1... | collective-permute-start | bytes 811016 | tf_op jit(solution)/shard_map/ppermute | solution.py:348
  52.8 0.0 collective-permute-start.12
  52.8 1.1 %collective-permute-done.2.refs_2_ = bf16[512,2048]{1,0:T(8,128)(2,1)S(1)} collective-permute-done((bf16[512,2048]{1,0:T(8,128)(2,1)S(1)}, bf16[512,2048]{1,0:T(8,128)(2,1)S(1)}, u32[]{:S(2)}, u32[]{:S(2)}) %collective-permute-start.2) | collective-permute-done | bytes 2097184 | tf_op jit(solution)/shard_map/ppermute | solution.py:345
  53.9 0.1 fusion
  54.0 7.2 %collective-permute-start.10 = (bf16[256,2048]{1,0:T(8,128)(2,1)S(1)}, bf16[256,2048]{1,0:T(8,128)(2,1)S(1)}, u32[]{:S(2)}, u32[]{:S(2)}) collective-permute-start(bf16[256,2048]{1,0:T(8,128)(2,1)S(1)} %get-tuple-element.73), channel_id=1, source_target_pairs={{0,1},{1,0},{2,3},{3,2},{4,5},{5,4},{6,7},{7,6},{8,9},{9,8},{10,11... | collective-permute-start | bytes 3145736 | tf_op jit(solution)/shard_map/ppermute | solution.py:345
  61.3 0.1 collective-permute-start.9
  61.4 2.5 %local_first_pairs.1 = (f32[2048,256]{1,0:T(8,128)S(1)}, f32[32,256]{1,0:T(8,128)S(1)}) custom-call(f32[16,256]{1,0:T(8,128)S(1)} %get-tuple-element.39.refs_0_, bf16[256,2048]{1,0:T(8,128)(2,1)S(1)} %copy-done, bf16[512,2048]{1,0:T(8,128)(2,1)S(1)} %collective-permute-done.2.refs_2_, bf16[784,512]{1,0:T(8,128)(2,1)S(1)} %collective-permute-done.4.a_ref.refs_3_, ...), custom_call_target="tpu_custom_call" | custom-call | flops 11811160064 | bytes 1048576 | tf_op jit(solution)/shard_map/local_first_pairs/pallas_call | solution.py:329
  63.9 0.0 collective-permute-done.1.refs_2_
  63.9 0.0 collective-permute-done.11.refs_8_
  63.9 0.0 collective-permute-done.12.refs_10_
  63.9 0.0 collective-permute-done.10.refs_4_
  63.9 1.2 %collective-permute-done.9.refs_3_ = bf16[256,2048]{1,0:T(8,128)(2,1)S(1)} collective-permute-done((bf16[256,2048]{1,0:T(8,128)(2,1)S(1)}, bf16[256,2048]{1,0:T(8,128)(2,1)S(1)}, u32[]{:S(2)}, u32[]{:S(2)}) %collective-permute-start.9) | collective-permute-done | bytes 1048608 | tf_op jit(solution)/shard_map/ppermute | solution.py:345
  65.1 3.7 %local_second_relay.1 = bf16[256,2048]{1,0:T(8,128)(2,1)} custom-call(f32[16,256]{1,0:T(8,128)S(1)} %get-tuple-element.39.refs_0_, bf16[256,2048]{1,0:T(8,128)(2,1)S(1)} %copy-done, bf16[512,2048]{1,0:T(8,128)(2,1)S(1)} %collective-permute-done.1.refs_2_, bf16[256,2048]{1,0:T(8,128)(2,1)S(1)} %collective-permute-done.9.refs_3_, ...), custom_call_target="tpu_custom_call" | custom-call | flops 536870912 | bytes 1048576 | tf_op jit(solution)/shard_map/local_second_relay/pallas_call | solution.py:329
Async XLA Ops:
  0.0 15.2 %copy-start = (bf16[256,2048]{1,0:T(8,128)(2,1)S(1)}, bf16[256,2048]{1,0:T(8,128)(2,1)}, u32[]{:S(2)}) copy-start(bf16[256,2048]{1,0:T(8,128)(2,1)} %refs_1_.5) | copy-start | bytes 3145732
  2.0 7.1 %collective-permute-start = (bf16[512,2048]{1,0:T(8,128)(2,1)S(1)}, bf16[512,2048]{1,0:T(8,128)(2,1)S(1)}, u32[]{:S(2)}, u32[]{:S(2)}) collective-permute-start(bf16[512,2048]{1,0:T(8,128)(2,1)S(1)} %get-tuple-element.41.refs_2_.kv_ref), channel_id=1, source_target_pairs={{0,1},{1,0},{2,3},{3,2},{4,5},{5,4},{6,7},{7,6},{8,9},{9,8},{10,11... | collective-permute-start | bytes 6291464 | tf_op jit(solution)/shard_map/ppermute | solution.py:345
  5.4 19.5 %collective-permute-start.4 = (bf16[784,512]{1,0:T(8,128)(2,1)S(1)}, bf16[784,512]{1,0:T(8,128)(2,1)S(1)}, u32[]{:S(2)}, u32[]{:S(2)}) collective-permute-start(bf16[784,512]{1,0:T(8,128)(2,1)S(1)} %get-tuple-element.44), channel_id=1, source_target_pairs={{0,64},{64,0},{128,192},{192,128},{1,65},{65,1},{129,193},{193,129... | collective-permute-start | bytes 2408456 | tf_op jit(solution)/shard_map/ppermute | solution.py:347
  5.4 20.5 %collective-permute-start.5 = (bf16[784,512]{1,0:T(8,128)(2,1)S(1)}, bf16[784,512]{1,0:T(8,128)(2,1)S(1)}, u32[]{:S(2)}, u32[]{:S(2)}) collective-permute-start(bf16[784,512]{1,0:T(8,128)(2,1)S(1)} %get-tuple-element.45), channel_id=1, source_target_pairs={{0,192},{64,128},{128,64},{192,0},{1,193},{65,129},{129,65},{193,1... | collective-permute-start | bytes 2408456 | tf_op jit(solution)/shard_map/ppermute | solution.py:348
  6.9 47.0 %collective-permute-start.2 = (bf16[512,2048]{1,0:T(8,128)(2,1)S(1)}, bf16[512,2048]{1,0:T(8,128)(2,1)S(1)}, u32[]{:S(2)}, u32[]{:S(2)}) collective-permute-start(bf16[512,2048]{1,0:T(8,128)(2,1)S(1)} %get-tuple-element.41.refs_2_.kv_ref), channel_id=1, source_target_pairs={{0,62},{1,3},{2,0},{3,5},{4,2},{5,7},{6,4},{7,9},{8,6},{9,11},{10,... | collective-permute-start | bytes 6291464 | tf_op jit(solution)/shard_map/ppermute | solution.py:345
  8.1 34.0 %collective-permute-start.3 = (bf16[784,512]{1,0:T(8,128)(2,1)S(1)}, bf16[784,512]{1,0:T(8,128)(2,1)S(1)}, u32[]{:S(2)}, u32[]{:S(2)}) collective-permute-start(bf16[784,512]{1,0:T(8,128)(2,1)S(1)} %get-tuple-element.42), channel_id=1, source_target_pairs={{0,64},{64,0},{128,192},{192,128},{1,65},{65,1},{129,193},{193,129... | collective-permute-start | bytes 2408456 | tf_op jit(solution)/shard_map/ppermute | solution.py:347
  9.2 54.7 %collective-permute-start.1 = (bf16[512,2048]{1,0:T(8,128)(2,1)S(1)}, bf16[512,2048]{1,0:T(8,128)(2,1)S(1)}, u32[]{:S(2)}, u32[]{:S(2)}) collective-permute-start(bf16[512,2048]{1,0:T(8,128)(2,1)S(1)} %get-tuple-element.41.refs_2_.kv_ref), channel_id=1, source_target_pairs={{0,2},{1,63},{2,4},{3,1},{4,6},{5,3},{6,8},{7,5},{8,10},{9,7},{10,... | collective-permute-start | bytes 6291464 | tf_op jit(solution)/shard_map/ppermute | solution.py:345
  25.9 19.6 %collective-permute-start.6 = (bf16[784,512]{1,0:T(8,128)(2,1)S(1)}, bf16[784,512]{1,0:T(8,128)(2,1)S(1)}, u32[]{:S(2)}, u32[]{:S(2)}) collective-permute-start(bf16[784,512]{1,0:T(8,128)(2,1)S(1)} %get-tuple-element.50), channel_id=1, source_target_pairs={{0,192},{64,128},{128,64},{192,0},{1,193},{65,129},{129,65},{193,1... | collective-permute-start | bytes 2408456 | tf_op jit(solution)/shard_map/ppermute | solution.py:348
  28.6 19.2 %collective-permute-start.7 = (bf16[528,256]{1,0:T(8,128)(2,1)S(1)}, bf16[528,256]{1,0:T(8,128)(2,1)S(1)}, u32[]{:S(2)}, u32[]{:S(2)}) collective-permute-start(bf16[528,256]{1,0:T(8,128)(2,1)S(1)} %get-tuple-element.53), channel_id=1, source_target_pairs={{0,64},{64,0},{128,192},{192,128},{1,65},{65,1},{129,193},{193,129... | collective-permute-start | bytes 811016 | tf_op jit(solution)/shard_map/ppermute | solution.py:347
  42.0 9.8 %collective-permute-start.8 = (bf16[528,256]{1,0:T(8,128)(2,1)S(1)}, bf16[528,256]{1,0:T(8,128)(2,1)S(1)}, u32[]{:S(2)}, u32[]{:S(2)}) collective-permute-start(bf16[528,256]{1,0:T(8,128)(2,1)S(1)} %get-tuple-element.59), channel_id=1, source_target_pairs={{0,192},{64,128},{128,64},{192,0},{1,193},{65,129},{129,65},{193,1... | collective-permute-start | bytes 811016 | tf_op jit(solution)/shard_map/ppermute | solution.py:348
  51.8 12.1 %collective-permute-start.11 = (bf16[528,256]{1,0:T(8,128)(2,1)S(1)}, bf16[528,256]{1,0:T(8,128)(2,1)S(1)}, u32[]{:S(2)}, u32[]{:S(2)}) collective-permute-start(bf16[528,256]{1,0:T(8,128)(2,1)S(1)} %get-tuple-element.60), channel_id=1, source_target_pairs={{0,192},{64,128},{128,64},{192,0},{1,193},{65,129},{129,65},{193,1... | collective-permute-start | bytes 811016 | tf_op jit(solution)/shard_map/ppermute | solution.py:348
  52.8 11.1 %collective-permute-start.12 = (bf16[528,256]{1,0:T(8,128)(2,1)S(1)}, bf16[528,256]{1,0:T(8,128)(2,1)S(1)}, u32[]{:S(2)}, u32[]{:S(2)}) collective-permute-start(bf16[528,256]{1,0:T(8,128)(2,1)S(1)} %get-tuple-element.57), channel_id=1, source_target_pairs={{0,64},{64,0},{128,192},{192,128},{1,65},{65,1},{129,193},{193,129... | collective-permute-start | bytes 811016 | tf_op jit(solution)/shard_map/ppermute | solution.py:347
  54.0 9.8 %collective-permute-start.10 = (bf16[256,2048]{1,0:T(8,128)(2,1)S(1)}, bf16[256,2048]{1,0:T(8,128)(2,1)S(1)}, u32[]{:S(2)}, u32[]{:S(2)}) collective-permute-start(bf16[256,2048]{1,0:T(8,128)(2,1)S(1)} %get-tuple-element.73), channel_id=1, source_target_pairs={{0,1},{1,0},{2,3},{3,2},{4,5},{5,4},{6,7},{7,6},{8,9},{9,8},{10,11... | collective-permute-start | bytes 3145736 | tf_op jit(solution)/shard_map/ppermute | solution.py:345
  61.3 3.8 %collective-permute-start.9 = (bf16[256,2048]{1,0:T(8,128)(2,1)S(1)}, bf16[256,2048]{1,0:T(8,128)(2,1)S(1)}, u32[]{:S(2)}, u32[]{:S(2)}) collective-permute-start(bf16[256,2048]{1,0:T(8,128)(2,1)S(1)} %get-tuple-element.74), channel_id=1, source_target_pairs={{0,1},{1,0},{2,3},{3,2},{4,5},{5,4},{6,7},{7,6},{8,9},{9,8},{10,11... | collective-permute-start | bytes 3145736 | tf_op jit(solution)/shard_map/ppermute | solution.py:345

commit v6 on v4

--- a/solution.py
+++ b/solution.py
@@ -25,6 +25,7 @@
 SPLIT = 4
 VMEM_LIMIT = 20 * 1024 * 1024
 REMOTE_COST = (400, 200)
+MIDDLE_COST = 1
 
 f32 = jnp.float32
 bf16 = jnp.bfloat16
@@ -235,7 +236,11 @@
     odd_group = (lax.axis_index("group") % 2) == 1
     sources = []
     for role in plan:
-        if role == "pairs":
+        if role == "relay":
+            arrays = [refs.pop(0), refs.pop(0)]
+            block = jnp.where(odd_core, 3, 2)
+            blocks = (block, block)
+        elif role == "pairs":
             arrays = [refs.pop(0) for _ in range(2 * PARTS)]
             blocks = (jnp.where(odd_group, 7, 5), jnp.where(odd_group, 5, 7))
         else:
@@ -243,7 +248,6 @@
             block = {
                 "own": 0,
                 "core": jnp.where(odd_core, 2, 3),
-                "relay": jnp.where(odd_core, 3, 2),
                 "first": jnp.where(odd_core, 1, 4),
                 "second": jnp.where(odd_core, 4, 1),
             }[role]
@@ -269,6 +273,9 @@
         low = slice(inner * HD, (inner + 1) * HD)
         given = []
         for role, arrays, bias in sources:
+            if role == "relay":
+                given.append((arrays[0][:, c], arrays[1][:, c], bias[half]))
+                continue
             array, at = (arrays[piece], low) if role == "pairs" else (arrays, c)
             given.append((array[0:ROWS, at], array[ROWS : 2 * ROWS, at], bias[half]))
         before = reply = None
@@ -283,12 +290,8 @@
         if last:
             out_hbm, out_ref, sems = refs
             out_ref[:, c] = (acc / l).astype(bf16).T
-            if h % 2 == 1:
-                n, pair = h // 2, slice((h - 1) * HD, (h + 1) * HD)
-                copies.append(
-                    pltpu.make_async_copy(out_ref.at[:, pair], out_hbm.at[:, pair], sems.at[n])
-                )
-                copies[-1].start()
+            copies.append(pltpu.make_async_copy(out_ref.at[:, c], out_hbm.at[:, c], sems.at[h]))
+            copies[-1].start()
         else:
             refs[0][c] = acc
             tops.append(m)
@@ -301,17 +304,17 @@
         refs[1][...] = jnp.concatenate(tops + sums, axis=0)
 
 
-def local(table, q, sources, before=None, reply=None, last=False):
+def local(table, q, sources, before=None, reply=None, last=False, cost=1):
     vmem = pl.BlockSpec(memory_space=pltpu.VMEM)
     plan = tuple(role for role, _ in sources)
     args = [table, q]
     for role, arrays in sources:
-        args += list(arrays) if role == "pairs" else [arrays]
+        args += list(arrays) if role in ("pairs", "relay") else [arrays]
     args += list(before or ()) + list(reply or ())
     if last:
         out_specs = pl.BlockSpec(memory_space=pl.ANY)
         out_shape = jax.ShapeDtypeStruct((ROWS, W), bf16)
-        scratch = [pltpu.VMEM((ROWS, W), bf16), pltpu.SemaphoreType.DMA((H // 2,))]
+        scratch = [pltpu.VMEM((ROWS, W), bf16), pltpu.SemaphoreType.DMA((H,))]
     else:
         scratch = []
         out_specs = [vmem, vmem]
@@ -327,7 +330,7 @@
         scratch_shapes=scratch,
         compiler_params=pltpu.CompilerParams(vmem_limit_bytes=VMEM_LIMIT),
         cost_estimate=pl.CostEstimate(
-            flops=4 * ROWS * ROWS * W, bytes_accessed=1024 * 1024, transcendentals=0
+            flops=4 * cost * ROWS * ROWS * W, bytes_accessed=1024 * 1024, transcendentals=0
         ),
         name="local_" + "_".join(plan),
     )(*args)
@@ -355,16 +358,17 @@
     back_a[0], back_b[0] = to_a(part_a), to_b(part_b)
 
     first, part_a = lax.optimization_barrier((first, part_a))
-    relay = core(first)
+    relay = [core(first[:ROWS]), core(first[ROWS:])]
     got_a[1], got_b[1], first = lax.optimization_barrier((got_a[1], got_b[1], first))
     part_a, part_b = remote(kv, got_a[1], got_b[1], 1)
     part_a, back_a[0] = lax.optimization_barrier((part_a, back_a[0]))
     back_a[1], back_b[1] = to_a(part_a), to_b(part_b)
 
     state, part_a, back_a[0], back_b[0] = lax.optimization_barrier((state, part_a, back_a[0], back_b[0]))
-    state = local(table, q, [("first", first), ("pairs", got_a + got_b)], state)
+    middle = [("first", first), ("relay", relay), ("pairs", got_a + got_b)]
+    state = local(table, q, middle, state, cost=MIDDLE_COST)
     second, state = lax.optimization_barrier((second, state))
-    return local(table, q, [("second", second), ("relay", relay)], state, back_b + back_a, True)
+    return local(table, q, [("second", second)], state, back_b + back_a, True)
 
 
 def solution(mesh):

time: 65.1 us -> 64.7 us (level)
  starting transfers between devices: 23.1 us -> 19.1 us
  waiting for transfers between devices: 28.4 us -> 31 us
  Pallas kernels: 13.4 us -> 14.1 us
    ppermute x4, waiting for transfers between devices: 1.97 us -> 4.16 us  [shards(): to_b = lambda x: lax.ppermute(x, 'group', [(i, 3 - i) for i in range(4)])]
    ppermute x4 -> x5, starting transfers between devices: 15.7 us -> 13.5 us  [shards(): lax.ppermute(x, 'rank', [(i, to(i) % ranks) for i in range(ranks)])]
    ppermute x4, starting transfers between devices: 2.11 us -> 0.5 us  [shards(): to_a = lambda x: lax.ppermute(x, 'group', [(i, i ^ 1) for i in range(4)])]
    ppermute x4 -> x5, waiting for transfers between devices: 11.1 us -> 12.7 us  [shards(): lax.ppermute(x, 'rank', [(i, to(i) % ranks) for i in range(ranks)])]
    ppermute x4, waiting for transfers between devices: 15.3 us -> 14.2 us  [shards(): to_a = lambda x: lax.ppermute(x, 'group', [(i, i ^ 1) for i in range(4)])]
    pallas_call x3, Pallas kernels: 8.54 us -> 9.23 us  [local(): pl.pallas_call(functools.partial(local_kernel, plan, before is not None,...]
  transfers between devices with their start and end apart: 12 -> 13, of which waited for: 7 -> 8; matrix products, arithmetic and copies ran while one was open for 0% -> 0% of each run, Pallas kernels for 12% -> 14%
where the time goes in v6:
time: 64.7 us; the launch traced here: 64.6 us
  waiting for transfers between devices  31 us (48%)
  starting transfers between devices  19.1 us (30%)
  Pallas kernels  14.1 us (22%)
    ppermute x4, waiting for transfers between devices, shards(): to_a = lambda x: lax.ppermute(x, 'group', [(i, i ^ 1) for i in range(4)])  14.2 us
    ppermute x5, starting transfers between devices, shards(): lax.ppermute(x, 'rank', [(i, to(i) % ranks) for i in range(ranks)])  13.5 us
    ppermute x5, waiting for transfers between devices, shards(): lax.ppermute(x, 'rank', [(i, to(i) % ranks) for i in range(ranks)])  12.7 us
    pallas_call x3, Pallas kernels, local(): pl.pallas_call(functools.partial(local_kernel, plan, before is not None,...  9.23 us
    ppermute x4, starting transfers between devices, shards(): to_b = lambda x: lax.ppermute(x, 'group', [(i, 3 - i) for i in range(4)])  5.1 us
    ppermute x4, waiting for transfers between devices, shards(): to_b = lambda x: lax.ppermute(x, 'group', [(i, 3 - i) for i in range(4)])  4.16 us
    pallas_call x2, Pallas kernels, remote(): pl.pallas_call(functools.partial(remote_kernel, part), in_specs=[vmem] *...  2.83 us
    pallas_call x1, Pallas kernels, pack(): pl.pallas_call(pack_kernel, in_specs=[hbm] * 5, out_specs=[vmem] * (2 + 2...  2.03 us
  transfers between devices with their start and end apart: 13, of which 8 were waited for; matrix products, arithmetic and copies ran while one was open for 0% of the time, Pallas kernels for 14%

profile of v6, /device:TPU:1, one launch (start us, length us, event | category | flops | bytes accessed | tf_op | source)
XLA Modules:
  0.0 64.6 jit_solution(7789471583118309143)
XLA Ops:
  0.0 0.0 copy-start
  0.0 2.0 %pack.1 = (bf16[512,2048]{1,0:T(8,128)(2,1)S(1)}, bf16[784,512]{1,0:T(8,128)(2,1)S(1)}, bf16[784,512]{1,0:T(8,128)(2,1)S(1)}, bf16[784,512]{1,0:T(8,128)(2,1)S(1...) custom-call(s32[2,8]{1,0:T(2,128)} %links_hbm.1, s32[2]{0:T(128)} %counts_hbm.1, bf16[256,2048]{1,0:T(8,128)(2,1)} %refs_1_.5, ...), custom_call_target="tpu_custom_call" | custom-call | bytes 8388608 | tf_op jit(solution)/shard_map/pack/pallas_call | solution.py:159
  2.0 3.3 %collective-permute-start.2 = (bf16[512,2048]{1,0:T(8,128)(2,1)S(1)}, bf16[512,2048]{1,0:T(8,128)(2,1)S(1)}, u32[]{:S(2)}, u32[]{:S(2)}) collective-permute-start(bf16[512,2048]{1,0:T(8,128)(2,1)S(1)} %get-tuple-element.47.refs_2_.kv_ref), channel_id=1, source_target_pairs={{0,1},{1,0},{2,3},{3,2},{4,5},{5,4},{6,7},{7,6},{8,9},{9,8},{10,11... | collective-permute-start | bytes 6291464 | tf_op jit(solution)/shard_map/ppermute | solution.py:341
  5.4 0.0 collective-permute-start
  5.4 1.5 %collective-permute-start.1 = (bf16[784,512]{1,0:T(8,128)(2,1)S(1)}, bf16[784,512]{1,0:T(8,128)(2,1)S(1)}, u32[]{:S(2)}, u32[]{:S(2)}) collective-permute-start(bf16[784,512]{1,0:T(8,128)(2,1)S(1)} %get-tuple-element.42), channel_id=1, source_target_pairs={{0,192},{64,128},{128,64},{192,0},{1,193},{65,129},{129,65},{193,1... | collective-permute-start | bytes 2408456 | tf_op jit(solution)/shard_map/ppermute | solution.py:344
  6.9 1.2 %collective-permute-start.6 = (bf16[512,2048]{1,0:T(8,128)(2,1)S(1)}, bf16[512,2048]{1,0:T(8,128)(2,1)S(1)}, u32[]{:S(2)}, u32[]{:S(2)}) collective-permute-start(bf16[512,2048]{1,0:T(8,128)(2,1)S(1)} %get-tuple-element.47.refs_2_.kv_ref), channel_id=1, source_target_pairs={{0,62},{1,3},{2,0},{3,5},{4,2},{5,7},{6,4},{7,9},{8,6},{9,11},{10,... | collective-permute-start | bytes 6291464 | tf_op jit(solution)/shard_map/ppermute | solution.py:341
  8.1 0.4 collective-permute-start.4
  8.5 0.7 %collective-permute-done.2.refs_3_ = bf16[512,2048]{1,0:T(8,128)(2,1)S(1)} collective-permute-done((bf16[512,2048]{1,0:T(8,128)(2,1)S(1)}, bf16[512,2048]{1,0:T(8,128)(2,1)S(1)}, u32[]{:S(2)}, u32[]{:S(2)}) %collective-permute-start.2) | collective-permute-done | bytes 2097184 | tf_op jit(solution)/shard_map/ppermute | solution.py:341
  9.2 1.0 %collective-permute-start.5 = (bf16[784,512]{1,0:T(8,128)(2,1)S(1)}, bf16[784,512]{1,0:T(8,128)(2,1)S(1)}, u32[]{:S(2)}, u32[]{:S(2)}) collective-permute-start(bf16[784,512]{1,0:T(8,128)(2,1)S(1)} %get-tuple-element.49), channel_id=1, source_target_pairs={{0,192},{64,128},{128,64},{192,0},{1,193},{65,129},{129,65},{193,1... | collective-permute-start | bytes 2408456 | tf_op jit(solution)/shard_map/ppermute | solution.py:344
  10.2 0.0 copy-done
  10.2 2.4 %local_own_core.1 = (f32[2048,256]{1,0:T(8,128)S(1)}, f32[32,256]{1,0:T(8,128)S(1)}) custom-call(f32[16,256]{1,0:T(8,128)S(1)} %get-tuple-element.39.refs_0_, bf16[256,2048]{1,0:T(8,128)(2,1)S(1)} %copy-done, bf16[512,2048]{1,0:T(8,128)(2,1)S(1)} %get-tuple-element.47.refs_2_.kv_ref, bf16[512,2048]{1,0:T(8,128)(2,1)S(1)} %collective-permute-done.2.refs_3_), custom_call_target="tpu_custom_call" | custom-call | flops 536870912 | bytes 1048576 | tf_op jit(solution)/shard_map/local_own_core/pallas_call | solution.py:325
  12.6 12.3 %collective-permute-done.a_ref.refs_5_ = bf16[784,512]{1,0:T(8,128)(2,1)S(1)} collective-permute-done((bf16[784,512]{1,0:T(8,128)(2,1)S(1)}, bf16[784,512]{1,0:T(8,128)(2,1)S(1)}, u32[]{:S(2)}, u32[]{:S(2)}) %collective-permute-start) | collective-permute-done | bytes 802848 | tf_op jit(solution)/shard_map/ppermute | solution.py:343
  24.8 1.1 %collective-permute-done.1.b_ref.refs_7_ = bf16[784,512]{1,0:T(8,128)(2,1)S(1)} collective-permute-done((bf16[784,512]{1,0:T(8,128)(2,1)S(1)}, bf16[784,512]{1,0:T(8,128)(2,1)S(1)}, u32[]{:S(2)}, u32[]{:S(2)}) %collective-permute-start.1) | collective-permute-done | bytes 802848 | tf_op jit(solution)/shard_map/ppermute | solution.py:344
  25.9 7.2 %collective-permute-start.3 = (bf16[512,2048]{1,0:T(8,128)(2,1)S(1)}, bf16[512,2048]{1,0:T(8,128)(2,1)S(1)}, u32[]{:S(2)}, u32[]{:S(2)}) collective-permute-start(bf16[512,2048]{1,0:T(8,128)(2,1)S(1)} %get-tuple-element.47.refs_2_.kv_ref), channel_id=1, source_target_pairs={{0,2},{1,63},{2,4},{3,1},{4,6},{5,3},{6,8},{7,5},{8,10},{9,7},{10,... | collective-permute-start | bytes 6291464 | tf_op jit(solution)/shard_map/ppermute | solution.py:341
  33.0 1.4 %remote_0.1 = (bf16[528,256]{1,0:T(8,128)(2,1)S(1)}, bf16[528,256]{1,0:T(8,128)(2,1)S(1)}) custom-call(bf16[512,2048]{1,0:T(8,128)(2,1)S(1)} %get-tuple-element.47.refs_2_.kv_ref, bf16[784,512]{1,0:T(8,128)(2,1)S(1)} %collective-permute-done.a_ref.refs_5_, bf16[784,512]{1,0:T(8,128)(2,1)S(1)} %collective-permute-done.1.b_ref.refs_7_), custom_call_target="tpu_custom_call" | custom-call | flops 26843545600 | bytes 1048576 | tf_op jit(solution)/shard_map/remote_0/pallas_call | solution.py:219
  34.5 0.1 collective-permute-start.9
  34.6 5.6 %collective-permute-done.6.refs_2_ = bf16[512,2048]{1,0:T(8,128)(2,1)S(1)} collective-permute-done((bf16[512,2048]{1,0:T(8,128)(2,1)S(1)}, bf16[512,2048]{1,0:T(8,128)(2,1)S(1)}, u32[]{:S(2)}, u32[]{:S(2)}) %collective-permute-start.6) | collective-permute-done | bytes 2097184 | tf_op jit(solution)/shard_map/ppermute | solution.py:341
  40.2 1.9 %collective-permute-done.4.a_ref.refs_6_ = bf16[784,512]{1,0:T(8,128)(2,1)S(1)} collective-permute-done((bf16[784,512]{1,0:T(8,128)(2,1)S(1)}, bf16[784,512]{1,0:T(8,128)(2,1)S(1)}, u32[]{:S(2)}, u32[]{:S(2)}) %collective-permute-start.4) | collective-permute-done | bytes 802848 | tf_op jit(solution)/shard_map/ppermute | solution.py:343
  42.0 1.1 %collective-permute-done.5.b_ref.refs_8_ = bf16[784,512]{1,0:T(8,128)(2,1)S(1)} collective-permute-done((bf16[784,512]{1,0:T(8,128)(2,1)S(1)}, bf16[784,512]{1,0:T(8,128)(2,1)S(1)}, u32[]{:S(2)}, u32[]{:S(2)}) %collective-permute-start.5) | collective-permute-done | bytes 802848 | tf_op jit(solution)/shard_map/ppermute | solution.py:344
  43.1 1.3 %collective-permute-start.10 = (bf16[528,256]{1,0:T(8,128)(2,1)S(1)}, bf16[528,256]{1,0:T(8,128)(2,1)S(1)}, u32[]{:S(2)}, u32[]{:S(2)}) collective-permute-start(bf16[528,256]{1,0:T(8,128)(2,1)S(1)} %get-tuple-element.62), channel_id=1, source_target_pairs={{0,192},{64,128},{128,64},{192,0},{1,193},{65,129},{129,65},{193,1... | collective-permute-start | bytes 811016 | tf_op jit(solution)/shard_map/ppermute | solution.py:344
  44.4 0.1 fusion
  44.5 1.6 %collective-permute-start.8 = (bf16[256,2048]{1,0:T(8,128)(2,1)S(1)}, bf16[256,2048]{1,0:T(8,128)(2,1)S(1)}, u32[]{:S(2)}, u32[]{:S(2)}) collective-permute-start(bf16[256,2048]{1,0:T(8,128)(2,1)S(1)} %get-tuple-element.73), channel_id=1, source_target_pairs={{0,1},{1,0},{2,3},{3,2},{4,5},{5,4},{6,7},{7,6},{8,9},{9,8},{10,11... | collective-permute-start | bytes 3145736 | tf_op jit(solution)/shard_map/ppermute | solution.py:341
  46.1 0.3 collective-permute-start.7
  46.4 1.4 %remote_1.1 = (bf16[528,256]{1,0:T(8,128)(2,1)S(1)}, bf16[528,256]{1,0:T(8,128)(2,1)S(1)}) custom-call(bf16[512,2048]{1,0:T(8,128)(2,1)S(1)} %get-tuple-element.47.refs_2_.kv_ref, bf16[784,512]{1,0:T(8,128)(2,1)S(1)} %collective-permute-done.4.a_ref.refs_6_, bf16[784,512]{1,0:T(8,128)(2,1)S(1)} %collective-permute-done.5.b_ref.refs_8_), custom_call_target="tpu_custom_call" | custom-call | flops 13421772800 | bytes 1048576 | tf_op jit(solution)/shard_map/remote_1/pallas_call | solution.py:219
  47.8 0.0 collective-permute-done.9.refs_7_
  47.8 1.3 %collective-permute-start.11 = (bf16[528,256]{1,0:T(8,128)(2,1)S(1)}, bf16[528,256]{1,0:T(8,128)(2,1)S(1)}, u32[]{:S(2)}, u32[]{:S(2)}) collective-permute-start(bf16[528,256]{1,0:T(8,128)(2,1)S(1)} %get-tuple-element.71), channel_id=1, source_target_pairs={{0,192},{64,128},{128,64},{192,0},{1,193},{65,129},{129,65},{193,1... | collective-permute-start | bytes 811016 | tf_op jit(solution)/shard_map/ppermute | solution.py:344
  49.2 2.0 %collective-permute-done.10.refs_5_ = bf16[528,256]{1,0:T(8,128)(2,1)S(1)} collective-permute-done((bf16[528,256]{1,0:T(8,128)(2,1)S(1)}, bf16[528,256]{1,0:T(8,128)(2,1)S(1)}, u32[]{:S(2)}, u32[]{:S(2)}) %collective-permute-start.10) | collective-permute-done | bytes 270368 | tf_op jit(solution)/shard_map/ppermute | solution.py:344
  51.2 0.0 collective-permute-start.12
  51.2 0.0 collective-permute-done.8.refs_4_
  51.2 0.0 collective-permute-done.7.refs_3_
  51.2 3.6 %local_first_relay_pairs.1 = (f32[2048,256]{1,0:T(8,128)S(1)}, f32[32,256]{1,0:T(8,128)S(1)}) custom-call(f32[16,256]{1,0:T(8,128)S(1)} %get-tuple-element.39.refs_0_, bf16[256,2048]{1,0:T(8,128)(2,1)S(1)} %copy-done, bf16[512,2048]{1,0:T(8,128)(2,1)S(1)} %collective-permute-done.6.refs_2_, bf16[256,2048]{1,0:T(8,128)(2,1)S(1)} %collective-permute-done.7.refs_3_, ...), custom_call_target="tpu_custom_call" | custom-call | flops 536870912 | bytes 1048576 | tf_op jit(solution)/shard_map/local_first_relay_pairs/pallas_call | solution.py:325
  54.8 6.4 %collective-permute-done.3.refs_2_ = bf16[512,2048]{1,0:T(8,128)(2,1)S(1)} collective-permute-done((bf16[512,2048]{1,0:T(8,128)(2,1)S(1)}, bf16[512,2048]{1,0:T(8,128)(2,1)S(1)}, u32[]{:S(2)}, u32[]{:S(2)}) %collective-permute-start.3) | collective-permute-done | bytes 2097184 | tf_op jit(solution)/shard_map/ppermute | solution.py:341
  61.2 0.0 collective-permute-done.11.refs_6_
  61.2 0.0 collective-permute-done.12.refs_8_
  61.2 3.2 %local_second.1 = bf16[256,2048]{1,0:T(8,128)(2,1)} custom-call(f32[16,256]{1,0:T(8,128)S(1)} %get-tuple-element.39.refs_0_, bf16[256,2048]{1,0:T(8,128)(2,1)S(1)} %copy-done, bf16[512,2048]{1,0:T(8,128)(2,1)S(1)} %collective-permute-done.3.refs_2_, f32[2048,256]{1,0:T(8,128)S(1)} %get-tuple-element.68.refs_3_, f32[32,256]{1,0:T(8,128)S(1)} %get-tuple-element.69.refs_4_, ...), custom_call_target="tpu_custom_call" | custom-call | flops 536870912 | bytes 1048576 | tf_op jit(solution)/shard_map/local_second/pallas_call | solution.py:325
Async XLA Ops:
  0.0 10.2 %copy-start = (bf16[256,2048]{1,0:T(8,128)(2,1)S(1)}, bf16[256,2048]{1,0:T(8,128)(2,1)}, u32[]{:S(2)}) copy-start(bf16[256,2048]{1,0:T(8,128)(2,1)} %refs_1_.5) | copy-start | bytes 3145732
  2.0 7.1 %collective-permute-start.2 = (bf16[512,2048]{1,0:T(8,128)(2,1)S(1)}, bf16[512,2048]{1,0:T(8,128)(2,1)S(1)}, u32[]{:S(2)}, u32[]{:S(2)}) collective-permute-start(bf16[512,2048]{1,0:T(8,128)(2,1)S(1)} %get-tuple-element.47.refs_2_.kv_ref), channel_id=1, source_target_pairs={{0,1},{1,0},{2,3},{3,2},{4,5},{5,4},{6,7},{7,6},{8,9},{9,8},{10,11... | collective-permute-start | bytes 6291464 | tf_op jit(solution)/shard_map/ppermute | solution.py:341
  5.4 19.5 %collective-permute-start = (bf16[784,512]{1,0:T(8,128)(2,1)S(1)}, bf16[784,512]{1,0:T(8,128)(2,1)S(1)}, u32[]{:S(2)}, u32[]{:S(2)}) collective-permute-start(bf16[784,512]{1,0:T(8,128)(2,1)S(1)} %get-tuple-element.41), channel_id=1, source_target_pairs={{0,64},{64,0},{128,192},{192,128},{1,65},{65,1},{129,193},{193,129... | collective-permute-start | bytes 2408456 | tf_op jit(solution)/shard_map/ppermute | solution.py:343
  5.4 20.5 %collective-permute-start.1 = (bf16[784,512]{1,0:T(8,128)(2,1)S(1)}, bf16[784,512]{1,0:T(8,128)(2,1)S(1)}, u32[]{:S(2)}, u32[]{:S(2)}) collective-permute-start(bf16[784,512]{1,0:T(8,128)(2,1)S(1)} %get-tuple-element.42), channel_id=1, source_target_pairs={{0,192},{64,128},{128,64},{192,0},{1,193},{65,129},{129,65},{193,1... | collective-permute-start | bytes 2408456 | tf_op jit(solution)/shard_map/ppermute | solution.py:344
  6.9 33.3 %collective-permute-start.6 = (bf16[512,2048]{1,0:T(8,128)(2,1)S(1)}, bf16[512,2048]{1,0:T(8,128)(2,1)S(1)}, u32[]{:S(2)}, u32[]{:S(2)}) collective-permute-start(bf16[512,2048]{1,0:T(8,128)(2,1)S(1)} %get-tuple-element.47.refs_2_.kv_ref), channel_id=1, source_target_pairs={{0,62},{1,3},{2,0},{3,5},{4,2},{5,7},{6,4},{7,9},{8,6},{9,11},{10,... | collective-permute-start | bytes 6291464 | tf_op jit(solution)/shard_map/ppermute | solution.py:341
  8.1 34.0 %collective-permute-start.4 = (bf16[784,512]{1,0:T(8,128)(2,1)S(1)}, bf16[784,512]{1,0:T(8,128)(2,1)S(1)}, u32[]{:S(2)}, u32[]{:S(2)}) collective-permute-start(bf16[784,512]{1,0:T(8,128)(2,1)S(1)} %get-tuple-element.48), channel_id=1, source_target_pairs={{0,64},{64,0},{128,192},{192,128},{1,65},{65,1},{129,193},{193,129... | collective-permute-start | bytes 2408456 | tf_op jit(solution)/shard_map/ppermute | solution.py:343
  9.2 33.9 %collective-permute-start.5 = (bf16[784,512]{1,0:T(8,128)(2,1)S(1)}, bf16[784,512]{1,0:T(8,128)(2,1)S(1)}, u32[]{:S(2)}, u32[]{:S(2)}) collective-permute-start(bf16[784,512]{1,0:T(8,128)(2,1)S(1)} %get-tuple-element.49), channel_id=1, source_target_pairs={{0,192},{64,128},{128,64},{192,0},{1,193},{65,129},{129,65},{193,1... | collective-permute-start | bytes 2408456 | tf_op jit(solution)/shard_map/ppermute | solution.py:344
  25.9 35.3 %collective-permute-start.3 = (bf16[512,2048]{1,0:T(8,128)(2,1)S(1)}, bf16[512,2048]{1,0:T(8,128)(2,1)S(1)}, u32[]{:S(2)}, u32[]{:S(2)}) collective-permute-start(bf16[512,2048]{1,0:T(8,128)(2,1)S(1)} %get-tuple-element.47.refs_2_.kv_ref), channel_id=1, source_target_pairs={{0,2},{1,63},{2,4},{3,1},{4,6},{5,3},{6,8},{7,5},{8,10},{9,7},{10,... | collective-permute-start | bytes 6291464 | tf_op jit(solution)/shard_map/ppermute | solution.py:341
  34.5 13.3 %collective-permute-start.9 = (bf16[528,256]{1,0:T(8,128)(2,1)S(1)}, bf16[528,256]{1,0:T(8,128)(2,1)S(1)}, u32[]{:S(2)}, u32[]{:S(2)}) collective-permute-start(bf16[528,256]{1,0:T(8,128)(2,1)S(1)} %get-tuple-element.52), channel_id=1, source_target_pairs={{0,64},{64,0},{128,192},{192,128},{1,65},{65,1},{129,193},{193,129... | collective-permute-start | bytes 811016 | tf_op jit(solution)/shard_map/ppermute | solution.py:343
  43.1 8.1 %collective-permute-start.10 = (bf16[528,256]{1,0:T(8,128)(2,1)S(1)}, bf16[528,256]{1,0:T(8,128)(2,1)S(1)}, u32[]{:S(2)}, u32[]{:S(2)}) collective-permute-start(bf16[528,256]{1,0:T(8,128)(2,1)S(1)} %get-tuple-element.62), channel_id=1, source_target_pairs={{0,192},{64,128},{128,64},{192,0},{1,193},{65,129},{129,65},{193,1... | collective-permute-start | bytes 811016 | tf_op jit(solution)/shard_map/ppermute | solution.py:344
  44.5 6.7 %collective-permute-start.8 = (bf16[256,2048]{1,0:T(8,128)(2,1)S(1)}, bf16[256,2048]{1,0:T(8,128)(2,1)S(1)}, u32[]{:S(2)}, u32[]{:S(2)}) collective-permute-start(bf16[256,2048]{1,0:T(8,128)(2,1)S(1)} %get-tuple-element.73), channel_id=1, source_target_pairs={{0,1},{1,0},{2,3},{3,2},{4,5},{5,4},{6,7},{7,6},{8,9},{9,8},{10,11... | collective-permute-start | bytes 3145736 | tf_op jit(solution)/shard_map/ppermute | solution.py:341
  46.1 5.1 %collective-permute-start.7 = (bf16[256,2048]{1,0:T(8,128)(2,1)S(1)}, bf16[256,2048]{1,0:T(8,128)(2,1)S(1)}, u32[]{:S(2)}, u32[]{:S(2)}) collective-permute-start(bf16[256,2048]{1,0:T(8,128)(2,1)S(1)} %get-tuple-element.74), channel_id=1, source_target_pairs={{0,1},{1,0},{2,3},{3,2},{4,5},{5,4},{6,7},{7,6},{8,9},{9,8},{10,11... | collective-permute-start | bytes 3145736 | tf_op jit(solution)/shard_map/ppermute | solution.py:341
  47.8 13.4 %collective-permute-start.11 = (bf16[528,256]{1,0:T(8,128)(2,1)S(1)}, bf16[528,256]{1,0:T(8,128)(2,1)S(1)}, u32[]{:S(2)}, u32[]{:S(2)}) collective-permute-start(bf16[528,256]{1,0:T(8,128)(2,1)S(1)} %get-tuple-element.71), channel_id=1, source_target_pairs={{0,192},{64,128},{128,64},{192,0},{1,193},{65,129},{129,65},{193,1... | collective-permute-start | bytes 811016 | tf_op jit(solution)/shard_map/ppermute | solution.py:344
  51.2 10.0 %collective-permute-start.12 = (bf16[528,256]{1,0:T(8,128)(2,1)S(1)}, bf16[528,256]{1,0:T(8,128)(2,1)S(1)}, u32[]{:S(2)}, u32[]{:S(2)}) collective-permute-start(bf16[528,256]{1,0:T(8,128)(2,1)S(1)} %get-tuple-element.60), channel_id=1, source_target_pairs={{0,64},{64,0},{128,192},{192,128},{1,65},{65,1},{129,193},{193,129... | collective-permute-start | bytes 811016 | tf_op jit(solution)/shard_map/ppermute | solution.py:343

commit v7 on v6

--- a/solution.py
+++ b/solution.py
@@ -52,8 +52,7 @@
 
 def weigh(scored, before=None, reply=None):
     raw, tops = scored
-    if before is not None:
-        tops = tops + [before[0]]
+    tops = tops + [before[0] if before is not None else jnp.full_like(tops[0], 0.5 * NEG)]
     if reply is not None:
         tops = tops + [reply[1]]
     m = functools.reduce(jnp.maximum, tops)
@@ -199,6 +198,7 @@
 
     def store(h, m, l, acc):
         way, inner = h // PH, h % PH
+        l = jnp.maximum(l, 1e-30)
         outs[way][inner * HD : (inner + 1) * HD] = (acc / l).astype(bf16)
         total = m + jnp.log2(l)
         high = total.astype(bf16).astype(f32)

time: 64.7 us -> 64.7 us (level)
  transfers between devices with their start and end apart: 13 -> 13, of which waited for: 8 -> 9; matrix products, arithmetic and copies ran while one was open for 0% -> 0% of each run, Pallas kernels for 14% -> 14%
where the time goes in v7:
time: 64.7 us; the launch traced here: 64.6 us
  waiting for transfers between devices  31 us (48%)
  starting transfers between devices  19.1 us (30%)
  Pallas kernels  14.1 us (22%)
    ppermute x4, waiting for transfers between devices, shards(): to_a = lambda x: lax.ppermute(x, 'group', [(i, i ^ 1) for i in range(4)])  14.2 us
    ppermute x5, starting transfers between devices, shards(): lax.ppermute(x, 'rank', [(i, to(i) % ranks) for i in range(ranks)])  13.5 us
    ppermute x5, waiting for transfers between devices, shards(): lax.ppermute(x, 'rank', [(i, to(i) % ranks) for i in range(ranks)])  12.7 us
    pallas_call x3, Pallas kernels, local(): pl.pallas_call(functools.partial(local_kernel, plan, before is not None,...  9.24 us
    ppermute x4, starting transfers between devices, shards(): to_b = lambda x: lax.ppermute(x, 'group', [(i, 3 - i) for i in range(4)])  5.1 us
    ppermute x4, waiting for transfers between devices, shards(): to_b = lambda x: lax.ppermute(x, 'group', [(i, 3 - i) for i in range(4)])  4.17 us
    pallas_call x2, Pallas kernels, remote(): pl.pallas_call(functools.partial(remote_kernel, part), in_specs=[vmem] *...  2.8 us
    pallas_call x1, Pallas kernels, pack(): pl.pallas_call(pack_kernel, in_specs=[hbm] * 5, out_specs=[vmem] * (2 + 2...  2.03 us
  transfers between devices with their start and end apart: 13, of which 9 were waited for; matrix products, arithmetic and copies ran while one was open for 0% of the time, Pallas kernels for 14%

profile of v7, /device:TPU:1, one launch (start us, length us, event | category | flops | bytes accessed | tf_op | source)
XLA Modules:
  0.0 64.6 jit_solution(2521224572313607249)
XLA Ops:
  0.0 0.0 copy-start
  0.0 2.0 %pack.1 = (bf16[512,2048]{1,0:T(8,128)(2,1)S(1)}, bf16[784,512]{1,0:T(8,128)(2,1)S(1)}, bf16[784,512]{1,0:T(8,128)(2,1)S(1)}, bf16[784,512]{1,0:T(8,128)(2,1)S(1...) custom-call(s32[2,8]{1,0:T(2,128)} %links_hbm.1, s32[2]{0:T(128)} %counts_hbm.1, bf16[256,2048]{1,0:T(8,128)(2,1)} %refs_1_.5, ...), custom_call_target="tpu_custom_call" | custom-call | bytes 8388608 | tf_op jit(solution)/shard_map/pack/pallas_call | solution.py:158
  2.0 3.3 %collective-permute-start.2 = (bf16[512,2048]{1,0:T(8,128)(2,1)S(1)}, bf16[512,2048]{1,0:T(8,128)(2,1)S(1)}, u32[]{:S(2)}, u32[]{:S(2)}) collective-permute-start(bf16[512,2048]{1,0:T(8,128)(2,1)S(1)} %get-tuple-element.47.refs_2_.kv_ref), channel_id=1, source_target_pairs={{0,1},{1,0},{2,3},{3,2},{4,5},{5,4},{6,7},{7,6},{8,9},{9,8},{10,11... | collective-permute-start | bytes 6291464 | tf_op jit(solution)/shard_map/ppermute | solution.py:341
  5.4 0.0 collective-permute-start
  5.4 1.5 %collective-permute-start.1 = (bf16[784,512]{1,0:T(8,128)(2,1)S(1)}, bf16[784,512]{1,0:T(8,128)(2,1)S(1)}, u32[]{:S(2)}, u32[]{:S(2)}) collective-permute-start(bf16[784,512]{1,0:T(8,128)(2,1)S(1)} %get-tuple-element.42), channel_id=1, source_target_pairs={{0,192},{64,128},{128,64},{192,0},{1,193},{65,129},{129,65},{193,1... | collective-permute-start | bytes 2408456 | tf_op jit(solution)/shard_map/ppermute | solution.py:344
  6.9 1.2 %collective-permute-start.6 = (bf16[512,2048]{1,0:T(8,128)(2,1)S(1)}, bf16[512,2048]{1,0:T(8,128)(2,1)S(1)}, u32[]{:S(2)}, u32[]{:S(2)}) collective-permute-start(bf16[512,2048]{1,0:T(8,128)(2,1)S(1)} %get-tuple-element.47.refs_2_.kv_ref), channel_id=1, source_target_pairs={{0,62},{1,3},{2,0},{3,5},{4,2},{5,7},{6,4},{7,9},{8,6},{9,11},{10,... | collective-permute-start | bytes 6291464 | tf_op jit(solution)/shard_map/ppermute | solution.py:341
  8.1 0.4 collective-permute-start.4
  8.5 0.7 %collective-permute-done.2.refs_3_ = bf16[512,2048]{1,0:T(8,128)(2,1)S(1)} collective-permute-done((bf16[512,2048]{1,0:T(8,128)(2,1)S(1)}, bf16[512,2048]{1,0:T(8,128)(2,1)S(1)}, u32[]{:S(2)}, u32[]{:S(2)}) %collective-permute-start.2) | collective-permute-done | bytes 2097184 | tf_op jit(solution)/shard_map/ppermute | solution.py:341
  9.2 1.0 %collective-permute-start.5 = (bf16[784,512]{1,0:T(8,128)(2,1)S(1)}, bf16[784,512]{1,0:T(8,128)(2,1)S(1)}, u32[]{:S(2)}, u32[]{:S(2)}) collective-permute-start(bf16[784,512]{1,0:T(8,128)(2,1)S(1)} %get-tuple-element.49), channel_id=1, source_target_pairs={{0,192},{64,128},{128,64},{192,0},{1,193},{65,129},{129,65},{193,1... | collective-permute-start | bytes 2408456 | tf_op jit(solution)/shard_map/ppermute | solution.py:344
  10.2 0.0 copy-done
  10.2 2.4 %local_own_core.1 = (f32[2048,256]{1,0:T(8,128)S(1)}, f32[32,256]{1,0:T(8,128)S(1)}) custom-call(f32[16,256]{1,0:T(8,128)S(1)} %get-tuple-element.39.refs_0_, bf16[256,2048]{1,0:T(8,128)(2,1)S(1)} %copy-done, bf16[512,2048]{1,0:T(8,128)(2,1)S(1)} %get-tuple-element.47.refs_2_.kv_ref, bf16[512,2048]{1,0:T(8,128)(2,1)S(1)} %collective-permute-done.2.refs_3_), custom_call_target="tpu_custom_call" | custom-call | flops 536870912 | bytes 1048576 | tf_op jit(solution)/shard_map/local_own_core/pallas_call | solution.py:325
  12.6 12.2 %collective-permute-done.a_ref.refs_5_ = bf16[784,512]{1,0:T(8,128)(2,1)S(1)} collective-permute-done((bf16[784,512]{1,0:T(8,128)(2,1)S(1)}, bf16[784,512]{1,0:T(8,128)(2,1)S(1)}, u32[]{:S(2)}, u32[]{:S(2)}) %collective-permute-start) | collective-permute-done | bytes 802848 | tf_op jit(solution)/shard_map/ppermute | solution.py:343
  24.8 1.1 %collective-permute-done.1.b_ref.refs_7_ = bf16[784,512]{1,0:T(8,128)(2,1)S(1)} collective-permute-done((bf16[784,512]{1,0:T(8,128)(2,1)S(1)}, bf16[784,512]{1,0:T(8,128)(2,1)S(1)}, u32[]{:S(2)}, u32[]{:S(2)}) %collective-permute-start.1) | collective-permute-done | bytes 802848 | tf_op jit(solution)/shard_map/ppermute | solution.py:344
  25.9 7.2 %collective-permute-start.3 = (bf16[512,2048]{1,0:T(8,128)(2,1)S(1)}, bf16[512,2048]{1,0:T(8,128)(2,1)S(1)}, u32[]{:S(2)}, u32[]{:S(2)}) collective-permute-start(bf16[512,2048]{1,0:T(8,128)(2,1)S(1)} %get-tuple-element.47.refs_2_.kv_ref), channel_id=1, source_target_pairs={{0,2},{1,63},{2,4},{3,1},{4,6},{5,3},{6,8},{7,5},{8,10},{9,7},{10,... | collective-permute-start | bytes 6291464 | tf_op jit(solution)/shard_map/ppermute | solution.py:341
  33.0 1.4 %remote_0.1 = (bf16[528,256]{1,0:T(8,128)(2,1)S(1)}, bf16[528,256]{1,0:T(8,128)(2,1)S(1)}) custom-call(bf16[512,2048]{1,0:T(8,128)(2,1)S(1)} %get-tuple-element.47.refs_2_.kv_ref, bf16[784,512]{1,0:T(8,128)(2,1)S(1)} %collective-permute-done.a_ref.refs_5_, bf16[784,512]{1,0:T(8,128)(2,1)S(1)} %collective-permute-done.1.b_ref.refs_7_), custom_call_target="tpu_custom_call" | custom-call | flops 26843545600 | bytes 1048576 | tf_op jit(solution)/shard_map/remote_0/pallas_call | solution.py:219
  34.5 0.1 collective-permute-start.9
  34.6 5.6 %collective-permute-done.6.refs_2_ = bf16[512,2048]{1,0:T(8,128)(2,1)S(1)} collective-permute-done((bf16[512,2048]{1,0:T(8,128)(2,1)S(1)}, bf16[512,2048]{1,0:T(8,128)(2,1)S(1)}, u32[]{:S(2)}, u32[]{:S(2)}) %collective-permute-start.6) | collective-permute-done | bytes 2097184 | tf_op jit(solution)/shard_map/ppermute | solution.py:341
  40.2 1.9 %collective-permute-done.4.a_ref.refs_6_ = bf16[784,512]{1,0:T(8,128)(2,1)S(1)} collective-permute-done((bf16[784,512]{1,0:T(8,128)(2,1)S(1)}, bf16[784,512]{1,0:T(8,128)(2,1)S(1)}, u32[]{:S(2)}, u32[]{:S(2)}) %collective-permute-start.4) | collective-permute-done | bytes 802848 | tf_op jit(solution)/shard_map/ppermute | solution.py:343
  42.0 1.1 %collective-permute-done.5.b_ref.refs_8_ = bf16[784,512]{1,0:T(8,128)(2,1)S(1)} collective-permute-done((bf16[784,512]{1,0:T(8,128)(2,1)S(1)}, bf16[784,512]{1,0:T(8,128)(2,1)S(1)}, u32[]{:S(2)}, u32[]{:S(2)}) %collective-permute-start.5) | collective-permute-done | bytes 802848 | tf_op jit(solution)/shard_map/ppermute | solution.py:344
  43.1 1.3 %collective-permute-start.10 = (bf16[528,256]{1,0:T(8,128)(2,1)S(1)}, bf16[528,256]{1,0:T(8,128)(2,1)S(1)}, u32[]{:S(2)}, u32[]{:S(2)}) collective-permute-start(bf16[528,256]{1,0:T(8,128)(2,1)S(1)} %get-tuple-element.62), channel_id=1, source_target_pairs={{0,192},{64,128},{128,64},{192,0},{1,193},{65,129},{129,65},{193,1... | collective-permute-start | bytes 811016 | tf_op jit(solution)/shard_map/ppermute | solution.py:344
  44.4 0.1 fusion
  44.5 1.6 %collective-permute-start.8 = (bf16[256,2048]{1,0:T(8,128)(2,1)S(1)}, bf16[256,2048]{1,0:T(8,128)(2,1)S(1)}, u32[]{:S(2)}, u32[]{:S(2)}) collective-permute-start(bf16[256,2048]{1,0:T(8,128)(2,1)S(1)} %get-tuple-element.73), channel_id=1, source_target_pairs={{0,1},{1,0},{2,3},{3,2},{4,5},{5,4},{6,7},{7,6},{8,9},{9,8},{10,11... | collective-permute-start | bytes 3145736 | tf_op jit(solution)/shard_map/ppermute | solution.py:341
  46.1 0.3 collective-permute-start.7
  46.4 1.4 %remote_1.1 = (bf16[528,256]{1,0:T(8,128)(2,1)S(1)}, bf16[528,256]{1,0:T(8,128)(2,1)S(1)}) custom-call(bf16[512,2048]{1,0:T(8,128)(2,1)S(1)} %get-tuple-element.47.refs_2_.kv_ref, bf16[784,512]{1,0:T(8,128)(2,1)S(1)} %collective-permute-done.4.a_ref.refs_6_, bf16[784,512]{1,0:T(8,128)(2,1)S(1)} %collective-permute-done.5.b_ref.refs_8_), custom_call_target="tpu_custom_call" | custom-call | flops 13421772800 | bytes 1048576 | tf_op jit(solution)/shard_map/remote_1/pallas_call | solution.py:219
  47.8 0.1 collective-permute-done.9.refs_7_
  47.8 1.3 %collective-permute-start.11 = (bf16[528,256]{1,0:T(8,128)(2,1)S(1)}, bf16[528,256]{1,0:T(8,128)(2,1)S(1)}, u32[]{:S(2)}, u32[]{:S(2)}) collective-permute-start(bf16[528,256]{1,0:T(8,128)(2,1)S(1)} %get-tuple-element.71), channel_id=1, source_target_pairs={{0,192},{64,128},{128,64},{192,0},{1,193},{65,129},{129,65},{193,1... | collective-permute-start | bytes 811016 | tf_op jit(solution)/shard_map/ppermute | solution.py:344
  49.2 2.0 %collective-permute-done.10.refs_5_ = bf16[528,256]{1,0:T(8,128)(2,1)S(1)} collective-permute-done((bf16[528,256]{1,0:T(8,128)(2,1)S(1)}, bf16[528,256]{1,0:T(8,128)(2,1)S(1)}, u32[]{:S(2)}, u32[]{:S(2)}) %collective-permute-start.10) | collective-permute-done | bytes 270368 | tf_op jit(solution)/shard_map/ppermute | solution.py:344
  51.2 0.0 collective-permute-start.12
  51.2 0.0 collective-permute-done.8.refs_4_
  51.2 0.0 collective-permute-done.7.refs_3_
  51.2 3.6 %local_first_relay_pairs.1 = (f32[2048,256]{1,0:T(8,128)S(1)}, f32[32,256]{1,0:T(8,128)S(1)}) custom-call(f32[16,256]{1,0:T(8,128)S(1)} %get-tuple-element.39.refs_0_, bf16[256,2048]{1,0:T(8,128)(2,1)S(1)} %copy-done, bf16[512,2048]{1,0:T(8,128)(2,1)S(1)} %collective-permute-done.6.refs_2_, bf16[256,2048]{1,0:T(8,128)(2,1)S(1)} %collective-permute-done.7.refs_3_, ...), custom_call_target="tpu_custom_call" | custom-call | flops 536870912 | bytes 1048576 | tf_op jit(solution)/shard_map/local_first_relay_pairs/pallas_call | solution.py:325
  54.8 6.4 %collective-permute-done.3.refs_2_ = bf16[512,2048]{1,0:T(8,128)(2,1)S(1)} collective-permute-done((bf16[512,2048]{1,0:T(8,128)(2,1)S(1)}, bf16[512,2048]{1,0:T(8,128)(2,1)S(1)}, u32[]{:S(2)}, u32[]{:S(2)}) %collective-permute-start.3) | collective-permute-done | bytes 2097184 | tf_op jit(solution)/shard_map/ppermute | solution.py:341
  61.2 0.0 collective-permute-done.11.refs_6_
  61.2 0.0 collective-permute-done.12.refs_8_
  61.2 3.2 %local_second.1 = bf16[256,2048]{1,0:T(8,128)(2,1)} custom-call(f32[16,256]{1,0:T(8,128)S(1)} %get-tuple-element.39.refs_0_, bf16[256,2048]{1,0:T(8,128)(2,1)S(1)} %copy-done, bf16[512,2048]{1,0:T(8,128)(2,1)S(1)} %collective-permute-done.3.refs_2_, f32[2048,256]{1,0:T(8,128)S(1)} %get-tuple-element.68.refs_3_, f32[32,256]{1,0:T(8,128)S(1)} %get-tuple-element.69.refs_4_, ...), custom_call_target="tpu_custom_call" | custom-call | flops 536870912 | bytes 1048576 | tf_op jit(solution)/shard_map/local_second/pallas_call | solution.py:325
Async XLA Ops:
  0.0 10.2 %copy-start = (bf16[256,2048]{1,0:T(8,128)(2,1)S(1)}, bf16[256,2048]{1,0:T(8,128)(2,1)}, u32[]{:S(2)}) copy-start(bf16[256,2048]{1,0:T(8,128)(2,1)} %refs_1_.5) | copy-start | bytes 3145732
  2.0 7.1 %collective-permute-start.2 = (bf16[512,2048]{1,0:T(8,128)(2,1)S(1)}, bf16[512,2048]{1,0:T(8,128)(2,1)S(1)}, u32[]{:S(2)}, u32[]{:S(2)}) collective-permute-start(bf16[512,2048]{1,0:T(8,128)(2,1)S(1)} %get-tuple-element.47.refs_2_.kv_ref), channel_id=1, source_target_pairs={{0,1},{1,0},{2,3},{3,2},{4,5},{5,4},{6,7},{7,6},{8,9},{9,8},{10,11... | collective-permute-start | bytes 6291464 | tf_op jit(solution)/shard_map/ppermute | solution.py:341
  5.4 19.5 %collective-permute-start = (bf16[784,512]{1,0:T(8,128)(2,1)S(1)}, bf16[784,512]{1,0:T(8,128)(2,1)S(1)}, u32[]{:S(2)}, u32[]{:S(2)}) collective-permute-start(bf16[784,512]{1,0:T(8,128)(2,1)S(1)} %get-tuple-element.41), channel_id=1, source_target_pairs={{0,64},{64,0},{128,192},{192,128},{1,65},{65,1},{129,193},{193,129... | collective-permute-start | bytes 2408456 | tf_op jit(solution)/shard_map/ppermute | solution.py:343
  5.4 20.5 %collective-permute-start.1 = (bf16[784,512]{1,0:T(8,128)(2,1)S(1)}, bf16[784,512]{1,0:T(8,128)(2,1)S(1)}, u32[]{:S(2)}, u32[]{:S(2)}) collective-permute-start(bf16[784,512]{1,0:T(8,128)(2,1)S(1)} %get-tuple-element.42), channel_id=1, source_target_pairs={{0,192},{64,128},{128,64},{192,0},{1,193},{65,129},{129,65},{193,1... | collective-permute-start | bytes 2408456 | tf_op jit(solution)/shard_map/ppermute | solution.py:344
  6.9 33.3 %collective-permute-start.6 = (bf16[512,2048]{1,0:T(8,128)(2,1)S(1)}, bf16[512,2048]{1,0:T(8,128)(2,1)S(1)}, u32[]{:S(2)}, u32[]{:S(2)}) collective-permute-start(bf16[512,2048]{1,0:T(8,128)(2,1)S(1)} %get-tuple-element.47.refs_2_.kv_ref), channel_id=1, source_target_pairs={{0,62},{1,3},{2,0},{3,5},{4,2},{5,7},{6,4},{7,9},{8,6},{9,11},{10,... | collective-permute-start | bytes 6291464 | tf_op jit(solution)/shard_map/ppermute | solution.py:341
  8.1 34.0 %collective-permute-start.4 = (bf16[784,512]{1,0:T(8,128)(2,1)S(1)}, bf16[784,512]{1,0:T(8,128)(2,1)S(1)}, u32[]{:S(2)}, u32[]{:S(2)}) collective-permute-start(bf16[784,512]{1,0:T(8,128)(2,1)S(1)} %get-tuple-element.48), channel_id=1, source_target_pairs={{0,64},{64,0},{128,192},{192,128},{1,65},{65,1},{129,193},{193,129... | collective-permute-start | bytes 2408456 | tf_op jit(solution)/shard_map/ppermute | solution.py:343
  9.2 33.9 %collective-permute-start.5 = (bf16[784,512]{1,0:T(8,128)(2,1)S(1)}, bf16[784,512]{1,0:T(8,128)(2,1)S(1)}, u32[]{:S(2)}, u32[]{:S(2)}) collective-permute-start(bf16[784,512]{1,0:T(8,128)(2,1)S(1)} %get-tuple-element.49), channel_id=1, source_target_pairs={{0,192},{64,128},{128,64},{192,0},{1,193},{65,129},{129,65},{193,1... | collective-permute-start | bytes 2408456 | tf_op jit(solution)/shard_map/ppermute | solution.py:344
  25.9 35.3 %collective-permute-start.3 = (bf16[512,2048]{1,0:T(8,128)(2,1)S(1)}, bf16[512,2048]{1,0:T(8,128)(2,1)S(1)}, u32[]{:S(2)}, u32[]{:S(2)}) collective-permute-start(bf16[512,2048]{1,0:T(8,128)(2,1)S(1)} %get-tuple-element.47.refs_2_.kv_ref), channel_id=1, source_target_pairs={{0,2},{1,63},{2,4},{3,1},{4,6},{5,3},{6,8},{7,5},{8,10},{9,7},{10,... | collective-permute-start | bytes 6291464 | tf_op jit(solution)/shard_map/ppermute | solution.py:341
  34.5 13.4 %collective-permute-start.9 = (bf16[528,256]{1,0:T(8,128)(2,1)S(1)}, bf16[528,256]{1,0:T(8,128)(2,1)S(1)}, u32[]{:S(2)}, u32[]{:S(2)}) collective-permute-start(bf16[528,256]{1,0:T(8,128)(2,1)S(1)} %get-tuple-element.52), channel_id=1, source_target_pairs={{0,64},{64,0},{128,192},{192,128},{1,65},{65,1},{129,193},{193,129... | collective-permute-start | bytes 811016 | tf_op jit(solution)/shard_map/ppermute | solution.py:343
  43.1 8.1 %collective-permute-start.10 = (bf16[528,256]{1,0:T(8,128)(2,1)S(1)}, bf16[528,256]{1,0:T(8,128)(2,1)S(1)}, u32[]{:S(2)}, u32[]{:S(2)}) collective-permute-start(bf16[528,256]{1,0:T(8,128)(2,1)S(1)} %get-tuple-element.62), channel_id=1, source_target_pairs={{0,192},{64,128},{128,64},{192,0},{1,193},{65,129},{129,65},{193,1... | collective-permute-start | bytes 811016 | tf_op jit(solution)/shard_map/ppermute | solution.py:344
  44.5 6.7 %collective-permute-start.8 = (bf16[256,2048]{1,0:T(8,128)(2,1)S(1)}, bf16[256,2048]{1,0:T(8,128)(2,1)S(1)}, u32[]{:S(2)}, u32[]{:S(2)}) collective-permute-start(bf16[256,2048]{1,0:T(8,128)(2,1)S(1)} %get-tuple-element.73), channel_id=1, source_target_pairs={{0,1},{1,0},{2,3},{3,2},{4,5},{5,4},{6,7},{7,6},{8,9},{9,8},{10,11... | collective-permute-start | bytes 3145736 | tf_op jit(solution)/shard_map/ppermute | solution.py:341
  46.1 5.1 %collective-permute-start.7 = (bf16[256,2048]{1,0:T(8,128)(2,1)S(1)}, bf16[256,2048]{1,0:T(8,128)(2,1)S(1)}, u32[]{:S(2)}, u32[]{:S(2)}) collective-permute-start(bf16[256,2048]{1,0:T(8,128)(2,1)S(1)} %get-tuple-element.74), channel_id=1, source_target_pairs={{0,1},{1,0},{2,3},{3,2},{4,5},{5,4},{6,7},{7,6},{8,9},{9,8},{10,11... | collective-permute-start | bytes 3145736 | tf_op jit(solution)/shard_map/ppermute | solution.py:341
  47.8 13.4 %collective-permute-start.11 = (bf16[528,256]{1,0:T(8,128)(2,1)S(1)}, bf16[528,256]{1,0:T(8,128)(2,1)S(1)}, u32[]{:S(2)}, u32[]{:S(2)}) collective-permute-start(bf16[528,256]{1,0:T(8,128)(2,1)S(1)} %get-tuple-element.71), channel_id=1, source_target_pairs={{0,192},{64,128},{128,64},{192,0},{1,193},{65,129},{129,65},{193,1... | collective-permute-start | bytes 811016 | tf_op jit(solution)/shard_map/ppermute | solution.py:344
  51.2 10.0 %collective-permute-start.12 = (bf16[528,256]{1,0:T(8,128)(2,1)S(1)}, bf16[528,256]{1,0:T(8,128)(2,1)S(1)}, u32[]{:S(2)}, u32[]{:S(2)}) collective-permute-start(bf16[528,256]{1,0:T(8,128)(2,1)S(1)} %get-tuple-element.60), channel_id=1, source_target_pairs={{0,64},{64,0},{128,192},{192,128},{1,65},{65,1},{129,193},{193,129... | collective-permute-start | bytes 811016 | tf_op jit(solution)/shard_map/ppermute | solution.py:343

commit v8 on v7

--- a/solution.py
+++ b/solution.py
@@ -348,12 +348,12 @@
     from_core = core(kv)
     got_a = [to_a(x) for x in pay_a]
     got_b = [to_b(x) for x in pay_b]
+
+    back_a, back_b = [None] * PARTS, [None] * PARTS
+    kv_later, got_a[0], from_core = lax.optimization_barrier((kv, got_a[0], from_core))
+    second = across(kv_later, lambda i: i - 2 if i % 2 else i + 2)
     state = local(table, q, [("own", kv), ("core", from_core)])
-
-    back_a, back_b = [None] * PARTS, [None] * PARTS
-    got_a[0], got_b[0], state = lax.optimization_barrier((got_a[0], got_b[0], state))
-    kv_later, got_a[0], got_b[0] = lax.optimization_barrier((kv, got_a[0], got_b[0]))
-    second = across(kv_later, lambda i: i - 2 if i % 2 else i + 2)
+    got_b[0], state = lax.optimization_barrier((got_b[0], state))
     part_a, part_b = remote(kv, got_a[0], got_b[0], 0)
     back_a[0], back_b[0] = to_a(part_a), to_b(part_b)
 

time: 64.7 us -> 64.7 us (level)
  starting transfers between devices: 19.1 us -> 21 us
  waiting for transfers between devices: 31 us -> 29.2 us
    ppermute x4, waiting for transfers between devices: 14.2 us -> 18.4 us  [shards(): to_a = lambda x: lax.ppermute(x, 'group', [(i, i ^ 1) for i in range(4)])]
    ppermute x5, waiting for transfers between devices: 12.7 us -> 8.7 us  [shards(): lax.ppermute(x, 'rank', [(i, to(i) % ranks) for i in range(ranks)])]
    ppermute x4, waiting for transfers between devices: 4.17 us -> 2.06 us  [shards(): to_b = lambda x: lax.ppermute(x, 'group', [(i, 3 - i) for i in range(4)])]
    ppermute x5, starting transfers between devices: 13.5 us -> 15.2 us  [shards(): lax.ppermute(x, 'rank', [(i, to(i) % ranks) for i in range(ranks)])]
  transfers between devices with their start and end apart: 13 -> 13, of which waited for: 9 -> 6; matrix products, arithmetic and copies ran while one was open for 0% -> 0% of each run, Pallas kernels for 14% -> 14%
where the time goes in v8:
time: 64.7 us; the launch traced here: 64.6 us
  waiting for transfers between devices  29.2 us (45%)
  starting transfers between devices  21 us (32%)
  Pallas kernels  14.1 us (22%)
    ppermute x4, waiting for transfers between devices, shards(): to_a = lambda x: lax.ppermute(x, 'group', [(i, i ^ 1) for i in range(4)])  18.4 us
    ppermute x5, starting transfers between devices, shards(): lax.ppermute(x, 'rank', [(i, to(i) % ranks) for i in range(ranks)])  15.2 us
    pallas_call x3, Pallas kernels, local(): pl.pallas_call(functools.partial(local_kernel, plan, before is not None,...  9.23 us
    ppermute x5, waiting for transfers between devices, shards(): lax.ppermute(x, 'rank', [(i, to(i) % ranks) for i in range(ranks)])  8.7 us
    ppermute x4, starting transfers between devices, shards(): to_b = lambda x: lax.ppermute(x, 'group', [(i, 3 - i) for i in range(4)])  5.24 us
    pallas_call x2, Pallas kernels, remote(): pl.pallas_call(functools.partial(remote_kernel, part), in_specs=[vmem] *...  2.8 us
    ppermute x4, waiting for transfers between devices, shards(): to_b = lambda x: lax.ppermute(x, 'group', [(i, 3 - i) for i in range(4)])  2.06 us
    pallas_call x1, Pallas kernels, pack(): pl.pallas_call(pack_kernel, in_specs=[hbm] * 5, out_specs=[vmem] * (2 + 2...  2.03 us
  transfers between devices with their start and end apart: 13, of which 6 were waited for; matrix products, arithmetic and copies ran while one was open for 0% of the time, Pallas kernels for 14%

profile of v8, /device:TPU:1, one launch (start us, length us, event | category | flops | bytes accessed | tf_op | source)
XLA Modules:
  0.0 64.6 jit_solution(1286770690259200812)
XLA Ops:
  0.0 0.0 copy-start
  0.0 2.0 %pack.1 = (bf16[512,2048]{1,0:T(8,128)(2,1)S(1)}, bf16[784,512]{1,0:T(8,128)(2,1)S(1)}, bf16[784,512]{1,0:T(8,128)(2,1)S(1)}, bf16[784,512]{1,0:T(8,128)(2,1)S(1...) custom-call(s32[2,8]{1,0:T(2,128)} %links_hbm.1, s32[2]{0:T(128)} %counts_hbm.1, bf16[256,2048]{1,0:T(8,128)(2,1)} %refs_1_.5, ...), custom_call_target="tpu_custom_call" | custom-call | bytes 8388608 | tf_op jit(solution)/shard_map/pack/pallas_call | solution.py:158
  2.0 3.3 %collective-permute-start.1 = (bf16[512,2048]{1,0:T(8,128)(2,1)S(1)}, bf16[512,2048]{1,0:T(8,128)(2,1)S(1)}, u32[]{:S(2)}, u32[]{:S(2)}) collective-permute-start(bf16[512,2048]{1,0:T(8,128)(2,1)S(1)} %get-tuple-element.41.refs_2_.kv_ref), channel_id=1, source_target_pairs={{0,1},{1,0},{2,3},{3,2},{4,5},{5,4},{6,7},{7,6},{8,9},{9,8},{10,11... | collective-permute-start | bytes 6291464 | tf_op jit(solution)/shard_map/ppermute | solution.py:341
  5.4 0.0 collective-permute-start
  5.4 1.5 %collective-permute-start.6 = (bf16[784,512]{1,0:T(8,128)(2,1)S(1)}, bf16[784,512]{1,0:T(8,128)(2,1)S(1)}, u32[]{:S(2)}, u32[]{:S(2)}) collective-permute-start(bf16[784,512]{1,0:T(8,128)(2,1)S(1)} %get-tuple-element.45), channel_id=1, source_target_pairs={{0,192},{64,128},{128,64},{192,0},{1,193},{65,129},{129,65},{193,1... | collective-permute-start | bytes 2408456 | tf_op jit(solution)/shard_map/ppermute | solution.py:344
  6.9 1.2 %collective-permute-start.5 = (bf16[512,2048]{1,0:T(8,128)(2,1)S(1)}, bf16[512,2048]{1,0:T(8,128)(2,1)S(1)}, u32[]{:S(2)}, u32[]{:S(2)}) collective-permute-start(bf16[512,2048]{1,0:T(8,128)(2,1)S(1)} %get-tuple-element.41.refs_2_.kv_ref), channel_id=1, source_target_pairs={{0,62},{1,3},{2,0},{3,5},{4,2},{5,7},{6,4},{7,9},{8,6},{9,11},{10,... | collective-permute-start | bytes 6291464 | tf_op jit(solution)/shard_map/ppermute | solution.py:341
  8.1 0.4 collective-permute-start.3
  8.5 16.4 %collective-permute-done.a_ref.refs_5_ = bf16[784,512]{1,0:T(8,128)(2,1)S(1)} collective-permute-done((bf16[784,512]{1,0:T(8,128)(2,1)S(1)}, bf16[784,512]{1,0:T(8,128)(2,1)S(1)}, u32[]{:S(2)}, u32[]{:S(2)}) %collective-permute-start) | collective-permute-done | bytes 802848 | tf_op jit(solution)/shard_map/ppermute | solution.py:343
  24.8 1.0 %collective-permute-start.4 = (bf16[784,512]{1,0:T(8,128)(2,1)S(1)}, bf16[784,512]{1,0:T(8,128)(2,1)S(1)}, u32[]{:S(2)}, u32[]{:S(2)}) collective-permute-start(bf16[784,512]{1,0:T(8,128)(2,1)S(1)} %get-tuple-element.43), channel_id=1, source_target_pairs={{0,192},{64,128},{128,64},{192,0},{1,193},{65,129},{129,65},{193,1... | collective-permute-start | bytes 2408456 | tf_op jit(solution)/shard_map/ppermute | solution.py:344
  25.8 0.0 collective-permute-done.1.refs_3_
  25.8 7.8 %collective-permute-start.2 = (bf16[512,2048]{1,0:T(8,128)(2,1)S(1)}, bf16[512,2048]{1,0:T(8,128)(2,1)S(1)}, u32[]{:S(2)}, u32[]{:S(2)}) collective-permute-start(bf16[512,2048]{1,0:T(8,128)(2,1)S(1)} %get-tuple-element.41.refs_2_.kv_ref), channel_id=1, source_target_pairs={{0,2},{1,63},{2,4},{3,1},{4,6},{5,3},{6,8},{7,5},{8,10},{9,7},{10,... | collective-permute-start | bytes 6291464 | tf_op jit(solution)/shard_map/ppermute | solution.py:341
  33.6 0.0 copy-done
  33.6 2.4 %local_own_core.1 = (f32[2048,256]{1,0:T(8,128)S(1)}, f32[32,256]{1,0:T(8,128)S(1)}) custom-call(f32[16,256]{1,0:T(8,128)S(1)} %get-tuple-element.38.refs_0_, bf16[256,2048]{1,0:T(8,128)(2,1)S(1)} %copy-done, bf16[512,2048]{1,0:T(8,128)(2,1)S(1)} %get-tuple-element.41.refs_2_.kv_ref, bf16[512,2048]{1,0:T(8,128)(2,1)S(1)} %collective-permute-done.1.refs_3_), custom_call_target="tpu_custom_call" | custom-call | flops 536870912 | bytes 1048576 | tf_op jit(solution)/shard_map/local_own_core/pallas_call | solution.py:325
  36.0 0.0 collective-permute-done.6.b_ref.refs_7_
  36.0 1.4 %remote_0.1 = (bf16[528,256]{1,0:T(8,128)(2,1)S(1)}, bf16[528,256]{1,0:T(8,128)(2,1)S(1)}) custom-call(bf16[512,2048]{1,0:T(8,128)(2,1)S(1)} %get-tuple-element.41.refs_2_.kv_ref, bf16[784,512]{1,0:T(8,128)(2,1)S(1)} %collective-permute-done.a_ref.refs_5_, bf16[784,512]{1,0:T(8,128)(2,1)S(1)} %collective-permute-done.6.b_ref.refs_7_), custom_call_target="tpu_custom_call" | custom-call | flops 26843545600 | bytes 1048576 | tf_op jit(solution)/shard_map/remote_0/pallas_call | solution.py:219
  37.4 0.1 collective-permute-start.9
  37.5 2.4 %collective-permute-done.5.refs_2_ = bf16[512,2048]{1,0:T(8,128)(2,1)S(1)} collective-permute-done((bf16[512,2048]{1,0:T(8,128)(2,1)S(1)}, bf16[512,2048]{1,0:T(8,128)(2,1)S(1)}, u32[]{:S(2)}, u32[]{:S(2)}) %collective-permute-start.5) | collective-permute-done | bytes 2097184 | tf_op jit(solution)/shard_map/ppermute | solution.py:341
  40.0 2.1 %collective-permute-done.3.a_ref.refs_6_ = bf16[784,512]{1,0:T(8,128)(2,1)S(1)} collective-permute-done((bf16[784,512]{1,0:T(8,128)(2,1)S(1)}, bf16[784,512]{1,0:T(8,128)(2,1)S(1)}, u32[]{:S(2)}, u32[]{:S(2)}) %collective-permute-start.3) | collective-permute-done | bytes 802848 | tf_op jit(solution)/shard_map/ppermute | solution.py:343
  42.0 2.0 %collective-permute-done.4.b_ref.refs_8_ = bf16[784,512]{1,0:T(8,128)(2,1)S(1)} collective-permute-done((bf16[784,512]{1,0:T(8,128)(2,1)S(1)}, bf16[784,512]{1,0:T(8,128)(2,1)S(1)}, u32[]{:S(2)}, u32[]{:S(2)}) %collective-permute-start.4) | collective-permute-done | bytes 802848 | tf_op jit(solution)/shard_map/ppermute | solution.py:344
  44.1 1.0 %collective-permute-start.10 = (bf16[528,256]{1,0:T(8,128)(2,1)S(1)}, bf16[528,256]{1,0:T(8,128)(2,1)S(1)}, u32[]{:S(2)}, u32[]{:S(2)}) collective-permute-start(bf16[528,256]{1,0:T(8,128)(2,1)S(1)} %get-tuple-element.60), channel_id=1, source_target_pairs={{0,192},{64,128},{128,64},{192,0},{1,193},{65,129},{129,65},{193,1... | collective-permute-start | bytes 811016 | tf_op jit(solution)/shard_map/ppermute | solution.py:344
  45.1 0.1 fusion
  45.2 2.6 %collective-permute-start.8 = (bf16[256,2048]{1,0:T(8,128)(2,1)S(1)}, bf16[256,2048]{1,0:T(8,128)(2,1)S(1)}, u32[]{:S(2)}, u32[]{:S(2)}) collective-permute-start(bf16[256,2048]{1,0:T(8,128)(2,1)S(1)} %get-tuple-element.71), channel_id=1, source_target_pairs={{0,1},{1,0},{2,3},{3,2},{4,5},{5,4},{6,7},{7,6},{8,9},{9,8},{10,11... | collective-permute-start | bytes 3145736 | tf_op jit(solution)/shard_map/ppermute | solution.py:341
  47.9 0.3 collective-permute-start.7
  48.1 1.4 %remote_1.1 = (bf16[528,256]{1,0:T(8,128)(2,1)S(1)}, bf16[528,256]{1,0:T(8,128)(2,1)S(1)}) custom-call(bf16[512,2048]{1,0:T(8,128)(2,1)S(1)} %get-tuple-element.41.refs_2_.kv_ref, bf16[784,512]{1,0:T(8,128)(2,1)S(1)} %collective-permute-done.3.a_ref.refs_6_, bf16[784,512]{1,0:T(8,128)(2,1)S(1)} %collective-permute-done.4.b_ref.refs_8_), custom_call_target="tpu_custom_call" | custom-call | flops 13421772800 | bytes 1048576 | tf_op jit(solution)/shard_map/remote_1/pallas_call | solution.py:219
  49.5 0.0 collective-permute-done.9.refs_7_
  49.5 1.8 %collective-permute-start.11 = (bf16[528,256]{1,0:T(8,128)(2,1)S(1)}, bf16[528,256]{1,0:T(8,128)(2,1)S(1)}, u32[]{:S(2)}, u32[]{:S(2)}) collective-permute-start(bf16[528,256]{1,0:T(8,128)(2,1)S(1)} %get-tuple-element.69), channel_id=1, source_target_pairs={{0,192},{64,128},{128,64},{192,0},{1,193},{65,129},{129,65},{193,1... | collective-permute-start | bytes 811016 | tf_op jit(solution)/shard_map/ppermute | solution.py:344
  51.3 0.0 collective-permute-done.10.refs_5_
  51.3 0.0 collective-permute-start.12
  51.3 0.0 collective-permute-done.8.refs_4_
  51.3 0.3 collective-permute-done.7.refs_3_
  51.6 3.6 %local_first_relay_pairs.1 = (f32[2048,256]{1,0:T(8,128)S(1)}, f32[32,256]{1,0:T(8,128)S(1)}) custom-call(f32[16,256]{1,0:T(8,128)S(1)} %get-tuple-element.38.refs_0_, bf16[256,2048]{1,0:T(8,128)(2,1)S(1)} %copy-done, bf16[512,2048]{1,0:T(8,128)(2,1)S(1)} %collective-permute-done.5.refs_2_, bf16[256,2048]{1,0:T(8,128)(2,1)S(1)} %collective-permute-done.7.refs_3_, ...), custom_call_target="tpu_custom_call" | custom-call | flops 536870912 | bytes 1048576 | tf_op jit(solution)/shard_map/local_first_relay_pairs/pallas_call | solution.py:325
  55.2 6.0 %collective-permute-done.2.refs_2_ = bf16[512,2048]{1,0:T(8,128)(2,1)S(1)} collective-permute-done((bf16[512,2048]{1,0:T(8,128)(2,1)S(1)}, bf16[512,2048]{1,0:T(8,128)(2,1)S(1)}, u32[]{:S(2)}, u32[]{:S(2)}) %collective-permute-start.2) | collective-permute-done | bytes 2097184 | tf_op jit(solution)/shard_map/ppermute | solution.py:341
  61.2 0.0 collective-permute-done.11.refs_6_
  61.2 0.0 collective-permute-done.12.refs_8_
  61.2 3.2 %local_second.1 = bf16[256,2048]{1,0:T(8,128)(2,1)} custom-call(f32[16,256]{1,0:T(8,128)S(1)} %get-tuple-element.38.refs_0_, bf16[256,2048]{1,0:T(8,128)(2,1)S(1)} %copy-done, bf16[512,2048]{1,0:T(8,128)(2,1)S(1)} %collective-permute-done.2.refs_2_, f32[2048,256]{1,0:T(8,128)S(1)} %get-tuple-element.66.refs_3_, f32[32,256]{1,0:T(8,128)S(1)} %get-tuple-element.67.refs_4_, ...), custom_call_target="tpu_custom_call" | custom-call | flops 536870912 | bytes 1048576 | tf_op jit(solution)/shard_map/local_second/pallas_call | solution.py:325
Async XLA Ops:
  0.0 33.6 %copy-start = (bf16[256,2048]{1,0:T(8,128)(2,1)S(1)}, bf16[256,2048]{1,0:T(8,128)(2,1)}, u32[]{:S(2)}) copy-start(bf16[256,2048]{1,0:T(8,128)(2,1)} %refs_1_.5) | copy-start | bytes 3145732
  2.0 23.8 %collective-permute-start.1 = (bf16[512,2048]{1,0:T(8,128)(2,1)S(1)}, bf16[512,2048]{1,0:T(8,128)(2,1)S(1)}, u32[]{:S(2)}, u32[]{:S(2)}) collective-permute-start(bf16[512,2048]{1,0:T(8,128)(2,1)S(1)} %get-tuple-element.41.refs_2_.kv_ref), channel_id=1, source_target_pairs={{0,1},{1,0},{2,3},{3,2},{4,5},{5,4},{6,7},{7,6},{8,9},{9,8},{10,11... | collective-permute-start | bytes 6291464 | tf_op jit(solution)/shard_map/ppermute | solution.py:341
  5.4 19.5 %collective-permute-start = (bf16[784,512]{1,0:T(8,128)(2,1)S(1)}, bf16[784,512]{1,0:T(8,128)(2,1)S(1)}, u32[]{:S(2)}, u32[]{:S(2)}) collective-permute-start(bf16[784,512]{1,0:T(8,128)(2,1)S(1)} %get-tuple-element.40), channel_id=1, source_target_pairs={{0,64},{64,0},{128,192},{192,128},{1,65},{65,1},{129,193},{193,129... | collective-permute-start | bytes 2408456 | tf_op jit(solution)/shard_map/ppermute | solution.py:343
  5.4 30.6 %collective-permute-start.6 = (bf16[784,512]{1,0:T(8,128)(2,1)S(1)}, bf16[784,512]{1,0:T(8,128)(2,1)S(1)}, u32[]{:S(2)}, u32[]{:S(2)}) collective-permute-start(bf16[784,512]{1,0:T(8,128)(2,1)S(1)} %get-tuple-element.45), channel_id=1, source_target_pairs={{0,192},{64,128},{128,64},{192,0},{1,193},{65,129},{129,65},{193,1... | collective-permute-start | bytes 2408456 | tf_op jit(solution)/shard_map/ppermute | solution.py:344
  6.9 33.1 %collective-permute-start.5 = (bf16[512,2048]{1,0:T(8,128)(2,1)S(1)}, bf16[512,2048]{1,0:T(8,128)(2,1)S(1)}, u32[]{:S(2)}, u32[]{:S(2)}) collective-permute-start(bf16[512,2048]{1,0:T(8,128)(2,1)S(1)} %get-tuple-element.41.refs_2_.kv_ref), channel_id=1, source_target_pairs={{0,62},{1,3},{2,0},{3,5},{4,2},{5,7},{6,4},{7,9},{8,6},{9,11},{10,... | collective-permute-start | bytes 6291464 | tf_op jit(solution)/shard_map/ppermute | solution.py:341
  8.1 34.0 %collective-permute-start.3 = (bf16[784,512]{1,0:T(8,128)(2,1)S(1)}, bf16[784,512]{1,0:T(8,128)(2,1)S(1)}, u32[]{:S(2)}, u32[]{:S(2)}) collective-permute-start(bf16[784,512]{1,0:T(8,128)(2,1)S(1)} %get-tuple-element.42), channel_id=1, source_target_pairs={{0,64},{64,0},{128,192},{192,128},{1,65},{65,1},{129,193},{193,129... | collective-permute-start | bytes 2408456 | tf_op jit(solution)/shard_map/ppermute | solution.py:343
  24.8 19.3 %collective-permute-start.4 = (bf16[784,512]{1,0:T(8,128)(2,1)S(1)}, bf16[784,512]{1,0:T(8,128)(2,1)S(1)}, u32[]{:S(2)}, u32[]{:S(2)}) collective-permute-start(bf16[784,512]{1,0:T(8,128)(2,1)S(1)} %get-tuple-element.43), channel_id=1, source_target_pairs={{0,192},{64,128},{128,64},{192,0},{1,193},{65,129},{129,65},{193,1... | collective-permute-start | bytes 2408456 | tf_op jit(solution)/shard_map/ppermute | solution.py:344
  25.8 35.3 %collective-permute-start.2 = (bf16[512,2048]{1,0:T(8,128)(2,1)S(1)}, bf16[512,2048]{1,0:T(8,128)(2,1)S(1)}, u32[]{:S(2)}, u32[]{:S(2)}) collective-permute-start(bf16[512,2048]{1,0:T(8,128)(2,1)S(1)} %get-tuple-element.41.refs_2_.kv_ref), channel_id=1, source_target_pairs={{0,2},{1,63},{2,4},{3,1},{4,6},{5,3},{6,8},{7,5},{8,10},{9,7},{10,... | collective-permute-start | bytes 6291464 | tf_op jit(solution)/shard_map/ppermute | solution.py:341
  37.4 12.1 %collective-permute-start.9 = (bf16[528,256]{1,0:T(8,128)(2,1)S(1)}, bf16[528,256]{1,0:T(8,128)(2,1)S(1)}, u32[]{:S(2)}, u32[]{:S(2)}) collective-permute-start(bf16[528,256]{1,0:T(8,128)(2,1)S(1)} %get-tuple-element.50), channel_id=1, source_target_pairs={{0,64},{64,0},{128,192},{192,128},{1,65},{65,1},{129,193},{193,129... | collective-permute-start | bytes 811016 | tf_op jit(solution)/shard_map/ppermute | solution.py:343
  44.1 7.2 %collective-permute-start.10 = (bf16[528,256]{1,0:T(8,128)(2,1)S(1)}, bf16[528,256]{1,0:T(8,128)(2,1)S(1)}, u32[]{:S(2)}, u32[]{:S(2)}) collective-permute-start(bf16[528,256]{1,0:T(8,128)(2,1)S(1)} %get-tuple-element.60), channel_id=1, source_target_pairs={{0,192},{64,128},{128,64},{192,0},{1,193},{65,129},{129,65},{193,1... | collective-permute-start | bytes 811016 | tf_op jit(solution)/shard_map/ppermute | solution.py:344
  45.2 6.1 %collective-permute-start.8 = (bf16[256,2048]{1,0:T(8,128)(2,1)S(1)}, bf16[256,2048]{1,0:T(8,128)(2,1)S(1)}, u32[]{:S(2)}, u32[]{:S(2)}) collective-permute-start(bf16[256,2048]{1,0:T(8,128)(2,1)S(1)} %get-tuple-element.71), channel_id=1, source_target_pairs={{0,1},{1,0},{2,3},{3,2},{4,5},{5,4},{6,7},{7,6},{8,9},{9,8},{10,11... | collective-permute-start | bytes 3145736 | tf_op jit(solution)/shard_map/ppermute | solution.py:341
  47.9 3.8 %collective-permute-start.7 = (bf16[256,2048]{1,0:T(8,128)(2,1)S(1)}, bf16[256,2048]{1,0:T(8,128)(2,1)S(1)}, u32[]{:S(2)}, u32[]{:S(2)}) collective-permute-start(bf16[256,2048]{1,0:T(8,128)(2,1)S(1)} %get-tuple-element.72), channel_id=1, source_target_pairs={{0,1},{1,0},{2,3},{3,2},{4,5},{5,4},{6,7},{7,6},{8,9},{9,8},{10,11... | collective-permute-start | bytes 3145736 | tf_op jit(solution)/shard_map/ppermute | solution.py:341
  49.5 11.6 %collective-permute-start.11 = (bf16[528,256]{1,0:T(8,128)(2,1)S(1)}, bf16[528,256]{1,0:T(8,128)(2,1)S(1)}, u32[]{:S(2)}, u32[]{:S(2)}) collective-permute-start(bf16[528,256]{1,0:T(8,128)(2,1)S(1)} %get-tuple-element.69), channel_id=1, source_target_pairs={{0,192},{64,128},{128,64},{192,0},{1,193},{65,129},{129,65},{193,1... | collective-permute-start | bytes 811016 | tf_op jit(solution)/shard_map/ppermute | solution.py:344
  51.3 9.9 %collective-permute-start.12 = (bf16[528,256]{1,0:T(8,128)(2,1)S(1)}, bf16[528,256]{1,0:T(8,128)(2,1)S(1)}, u32[]{:S(2)}, u32[]{:S(2)}) collective-permute-start(bf16[528,256]{1,0:T(8,128)(2,1)S(1)} %get-tuple-element.58), channel_id=1, source_target_pairs={{0,64},{64,0},{128,192},{192,128},{1,65},{65,1},{129,193},{193,129... | collective-permute-start | bytes 811016 | tf_op jit(solution)/shard_map/ppermute | solution.py:343
